TPU v7x, 128 devices: a whole 4x4x4 slice. The times are simulated.
128 devices in a mesh: tm: 8 (over y_lo, z), rows: 16 (over x, y_hi, core).
Axes of the slice: x: 4, y: 4 (y_hi: 2, y_lo: 2; y = y_hi * 2 + y_lo), z: 4, core: 2. Of those that a mesh axis runs over, the one named last changes fastest.
Arguments:
- features: bfloat16 [8, 64, 104, 384], P('tm', 'rows'), may hold values from -45 to 45
- conv_cache: bfloat16 [2, 64, 104, 384], P(None, 'rows'), may hold values from -6 to 6
- head_cache: bfloat16 [2, 64, 104, 384], P(None, 'rows'), may hold values from -6 to 6
- conv_weight: bfloat16 [3, 3, 3, 384, 384], replicated, may hold values from -0.0625 to 0.0625
- head_weight: bfloat16 [3, 3, 3, 384, 16], replicated, may hold values from -0.0625 to 0.0625
- patch_weight: bfloat16 [2, 2, 16, 5120], replicated, may hold values from -0.75 to 0.75
- qkv_weight: bfloat16 [5120, 3, 5120], P(None, None, 'rows'), may hold values from -0.078125 to 0.078125
Outputs:
- qkv: bfloat16 [13312, 3, 5120], P('tm', None, 'rows')
All inputs are finite; a program needn't handle non-finite values.
Results may differ from a plain program's by a relative error of at most 0.02.
Values may be sent and summed in bfloat16 or wider, within the bound.
No kernel may reach another device: no remote copies, remote signals or barrier semaphores. Data moves between devices by JAX's collectives and lax.ppermute only.
A program may use at most 128 MiB of HBM per device.

v0:
```python
import jax
import jax.numpy as jnp
from jax import lax
from jax.sharding import PartitionSpec as P


def passed_along(block, axis, distance):
    devices = range(lax.axis_size(axis))
    route = [(i - distance, i) for i in devices if i - distance in devices]
    return lax.ppermute(block, axis, route)


def padded_2(block, sides, width):
    for axis, dim in sides:
        count = lax.axis_size(axis)
        forward = [(i, i + 1) for i in range(count - 1)]
        backward = [(target, source) for source, target in forward]
        low = lax.ppermute(
            lax.slice_in_dim(block, block.shape[dim] - width, None, axis=dim), axis, forward
        )
        high = lax.ppermute(lax.slice_in_dim(block, 0, width, axis=dim), axis, backward)
        block = jnp.concatenate([low, block, high], axis=dim)
    return block


def rms_silu(tensor_in):
    values = tensor_in.astype(jnp.float32)
    scaled = values * lax.rsqrt(jnp.mean(values * values, axis=-1, keepdims=True) + 1e-06)
    return jax.nn.silu(scaled).astype(jnp.bfloat16)


def shifted_history(current, cache_frames):
    position = lax.axis_index("tm")
    earlier = passed_along(current, "tm", 1)
    earlier = jnp.where(position == 0, cache_frames[1:2], earlier)
    earliest = passed_along(earlier, "tm", 1)
    earliest = jnp.where(position == 0, cache_frames[0:1], earliest)
    return (earliest, earlier)


def neighbourhood(current, cache_frames):
    earliest, earlier = shifted_history(current, cache_frames)
    stacked = jnp.concatenate([earliest, earlier, current], axis=0)
    window_stack = padded_2(stacked, (("rows", 1),), 1)
    return window_stack


def causal_conv(window_stack, kernel):
    padded = jnp.pad(window_stack, ((0, 0), (0, 0), (1, 1), (0, 0)))
    row_count = window_stack.shape[1] - 2
    col_count = window_stack.shape[2]
    tap_list = []
    for tap_time in range(3):
        for tap_row in range(3):
            for tap_col in range(3):
                tap_list.append(
                    padded[
                        tap_time, tap_row : tap_row + row_count, tap_col : tap_col + col_count, :
                    ]
                )
    columns = jnp.concatenate(tap_list, axis=-1)
    flat_kernel = kernel.reshape(-1, kernel.shape[-1])
    return jnp.dot(columns, flat_kernel, preferred_element_type=jnp.float32)


def embed_norm(patch_rows, flat_patch):
    embedded = jnp.dot(patch_rows, flat_patch, preferred_element_type=jnp.float32)
    centred = embedded - jnp.mean(embedded, axis=-1, keepdims=True)
    variance = jnp.mean(centred * centred, axis=-1, keepdims=True)
    return (centred * lax.rsqrt(variance + 1e-06)).astype(jnp.bfloat16)


def local(features, conv_cache, head_cache, conv_weight, head_weight, patch_weight, qkv_weight):
    normed_in = rms_silu(features)
    update = causal_conv(neighbourhood(normed_in, conv_cache), conv_weight)
    residual = (features[0].astype(jnp.float32) + update).astype(jnp.bfloat16)
    normed_out = rms_silu(residual)[None]
    latents = causal_conv(neighbourhood(normed_out, head_cache), head_weight).astype(jnp.bfloat16)
    row_count, col_count, latent_dim = latents.shape
    patches = latents.reshape(row_count // 2, 2, col_count // 2, 2, latent_dim)
    patches = patches.transpose(0, 2, 1, 3, 4).reshape(-1, 4 * latent_dim)
    flat_patch = patch_weight.reshape(4 * latent_dim, -1)
    local_cols = qkv_weight.shape[2]
    flat_qkv = qkv_weight.reshape(qkv_weight.shape[0], 3 * local_cols)
    normed_tok = embed_norm(patches, flat_patch)
    token_rows = lax.all_gather(normed_tok, "rows", axis=0, tiled=True)
    result = jnp.dot(token_rows, flat_qkv, preferred_element_type=jnp.float32).astype(jnp.bfloat16)
    return result.reshape(token_rows.shape[0], 3, local_cols)


def solution(mesh):
    return jax.shard_map(
        local,
        mesh=mesh,
        in_specs=(
            P("tm", "rows", None, None),
            P(None, "rows", None, None),
            P(None, "rows", None, None),
            P(),
            P(),
            P(),
            P(None, None, "rows"),
        ),
        out_specs=P("tm", None, "rows"),
        check_vma=False,
    )
```

profile of v0, /device:TPU:1, one launch (start us, length us, event | category | flops | bytes accessed | tf_op | source)
XLA Modules:
  0.0 252.0 jit_solution(14270368701462654024)
XLA Ops:
  6.5 1.2 fusion.23
  7.7 1.2 fusion.22
  9.0 4.4 %collective-permute-start = (bf16[1,4,104,384]{3,2,1,0:T(8,128)(2,1)S(1)}, bf16[1,4,104,384]{3,2,1,0:T(8,128)(2,1)S(1)}, u32[]{:S(2)}, u32[]{:S(2)}) collective-permute-start(bf16[1,4,104,384]{3,2,1,0:T(8,128)(2,1)S(1)} %fusion.22), channel_id=1, source_target_pairs={{0,16},{16,32},{32,48},{48,64},{64,80},{80,96},{96,112},{1,17},{17... | collective-permute-start | bytes 958472 | tf_op jit(solution)/shard_map/ppermute | solution.py:10
  13.4 6.2 %collective-permute-done = bf16[1,4,104,384]{3,2,1,0:T(8,128)(2,1)S(1)} collective-permute-done((bf16[1,4,104,384]{3,2,1,0:T(8,128)(2,1)S(1)}, bf16[1,4,104,384]{3,2,1,0:T(8,128)(2,1)S(1)}, u32[]{:S(2)}, u32[]{:S(2)}) %collective-permute-start) | collective-permute-done | bytes 319520 | tf_op jit(solution)/shard_map/ppermute | solution.py:10
  19.5 1.0 slice_select_fusion
  20.5 4.1 %collective-permute-start.1 = (bf16[1,4,104,384]{3,2,1,0:T(8,128)(2,1)S(1)}, bf16[1,4,104,384]{3,2,1,0:T(8,128)(2,1)S(1)}, u32[]{:S(2)}, u32[]{:S(2)}) collective-permute-start(bf16[1,4,104,384]{3,2,1,0:T(8,128)(2,1)S(1)} %slice_select_fusion), channel_id=1, source_target_pairs={{0,16},{16,32},{32,48},{48,64},{64,80},{80,96},{96,112},{1,17},{17... | collective-permute-start | bytes 958472 | tf_op jit(solution)/shard_map/ppermute | solution.py:10
  24.7 5.2 %collective-permute-done.1 = bf16[1,4,104,384]{3,2,1,0:T(8,128)(2,1)S(1)} collective-permute-done((bf16[1,4,104,384]{3,2,1,0:T(8,128)(2,1)S(1)}, bf16[1,4,104,384]{3,2,1,0:T(8,128)(2,1)S(1)}, u32[]{:S(2)}, u32[]{:S(2)}) %collective-permute-start.1) | collective-permute-done | bytes 319520 | tf_op jit(solution)/shard_map/ppermute | solution.py:10
  29.9 1.0 slice_select_fusion.1
  30.9 0.1 pad_maximum_fusion.17
  31.0 7.2 %collective-permute-start.2 = (bf16[3,1,104,384]{3,2,1,0:T(8,128)(2,1)S(1)}, bf16[3,1,104,384]{3,2,1,0:T(8,128)(2,1)S(1)}, u32[]{:S(2)}, u32[]{:S(2)}) collective-permute-start(bf16[3,1,104,384]{3,2,1,0:T(8,128)(2,1)S(1)} %get-tuple-element.7), channel_id=1, source_target_pairs={{0,1},{1,2},{2,3},{3,4},{4,5},{5,6},{6,7},{7,8},{8,9},{9,10},{10,1... | collective-permute-start | bytes 718856 | tf_op jit(solution)/shard_map/ppermute | solution.py:18
  38.2 1.9 collective-permute-start.3
  40.1 1.1 collective-permute-done.2
  41.3 5.9 %collective-permute-done.3 = bf16[3,1,104,384]{3,2,1,0:T(8,128)(2,1)S(1)} collective-permute-done((bf16[3,1,104,384]{3,2,1,0:T(8,128)(2,1)S(1)}, bf16[3,1,104,384]{3,2,1,0:T(8,128)(2,1)S(1)}, u32[]{:S(2)}, u32[]{:S(2)}) %collective-permute-start.3) | collective-permute-done | bytes 239648 | tf_op jit(solution)/shard_map/ppermute | solution.py:21
  47.2 1.2 fusion.10
  48.5 0.1 fusion.73
  48.8 0.1 fusion.71
  49.0 0.1 fusion.68
  49.2 0.1 fusion.65
  49.5 0.1 fusion.63
  49.7 0.1 fusion.60
  49.9 0.1 fusion.58
  49.9 0.1 fusion.56
  50.1 0.3 bitcast_dynamic-update-slice_fusion.2
  50.4 0.1 fusion.54
  50.6 0.1 fusion.50
  50.8 0.4 slice-done
  51.1 1.3 slice-done.1
  52.5 5.0 %multiply_reduce_fusion.1 = (f32[4,104]{1,0:T(4,128)S(1)}, f32[4,104,384]{2,1,0:T(8,128)S(1)}) fusion(bf16[4,104,10368]{2,1,0:T(8,128)(2,1)S(1)} %fusion.50, bf16[10368,384,1]{1,0,2:T(8,128)(2,1)S(1)} %bitcast.234, bf16[1,4,104,384]{3,2,1,0:T(8,128)(2,1)S(1)} %copy-done.2), kind=kOutput, calls=%fused_computation.37 | convolution fusion | flops 3313409536 | bytes 17548928 | tf_op jit(solution)/shard_map/dot_general | solution.py:63
  57.4 0.3 fusion.85
  57.7 4.1 %collective-permute-start.4 = (bf16[1,4,104,384]{3,2,1,0:T(8,128)(2,1)S(1)}, bf16[1,4,104,384]{3,2,1,0:T(8,128)(2,1)S(1)}, u32[]{:S(2)}, u32[]{:S(2)}) collective-permute-start(bf16[1,4,104,384]{3,2,1,0:T(8,128)(2,1)S(1)} %fusion.85), channel_id=1, source_target_pairs={{0,16},{16,32},{32,48},{48,64},{64,80},{80,96},{96,112},{1,17},{17... | collective-permute-start | bytes 958472 | tf_op jit(solution)/shard_map/ppermute | solution.py:10
  61.8 3.9 %collective-permute-done.4 = bf16[1,4,104,384]{3,2,1,0:T(8,128)(2,1)S(1)} collective-permute-done((bf16[1,4,104,384]{3,2,1,0:T(8,128)(2,1)S(1)}, bf16[1,4,104,384]{3,2,1,0:T(8,128)(2,1)S(1)}, u32[]{:S(2)}, u32[]{:S(2)}) %collective-permute-start.4) | collective-permute-done | bytes 319520 | tf_op jit(solution)/shard_map/ppermute | solution.py:10
  65.7 0.1 slice_select_fusion.2
  65.8 3.8 %collective-permute-start.5 = (bf16[1,4,104,384]{3,2,1,0:T(8,128)(2,1)S(1)}, bf16[1,4,104,384]{3,2,1,0:T(8,128)(2,1)S(1)}, u32[]{:S(2)}, u32[]{:S(2)}) collective-permute-start(bf16[1,4,104,384]{3,2,1,0:T(8,128)(2,1)S(1)} %slice_select_fusion.2), channel_id=1, source_target_pairs={{0,16},{16,32},{32,48},{48,64},{64,80},{80,96},{96,112},{1,17},{17... | collective-permute-start | bytes 958472 | tf_op jit(solution)/shard_map/ppermute | solution.py:10
  69.6 3.9 %collective-permute-done.5 = bf16[1,4,104,384]{3,2,1,0:T(8,128)(2,1)S(1)} collective-permute-done((bf16[1,4,104,384]{3,2,1,0:T(8,128)(2,1)S(1)}, bf16[1,4,104,384]{3,2,1,0:T(8,128)(2,1)S(1)}, u32[]{:S(2)}, u32[]{:S(2)}) %collective-permute-start.5) | collective-permute-done | bytes 319520 | tf_op jit(solution)/shard_map/ppermute | solution.py:10
  73.6 0.9 pad_maximum_fusion.14
  74.4 8.7 %collective-permute-start.6 = (bf16[3,1,104,384]{3,2,1,0:T(8,128)(2,1)}, bf16[3,1,104,384]{3,2,1,0:T(8,128)(2,1)S(1)}, u32[]{:S(2)}, u32[]{:S(2)}) collective-permute-start(bf16[3,1,104,384]{3,2,1,0:T(8,128)(2,1)} %get-tuple-element.5), channel_id=1, source_target_pairs={{0,1},{1,2},{2,3},{3,4},{4,5},{5,6},{6,7},{7,8},{8,9},{9,10},{10,1... | collective-permute-start | bytes 718856 | tf_op jit(solution)/shard_map/ppermute | solution.py:18
  83.2 2.1 collective-permute-start.7
  85.3 0.2 copy.8
  85.5 0.3 reshape.66
  85.8 0.8 collective-permute-done.6
  86.5 5.8 %collective-permute-done.7 = bf16[3,1,104,384]{3,2,1,0:T(8,128)(2,1)S(1)} collective-permute-done((bf16[3,1,104,384]{3,2,1,0:T(8,128)(2,1)}, bf16[3,1,104,384]{3,2,1,0:T(8,128)(2,1)S(1)}, u32[]{:S(2)}, u32[]{:S(2)}) %collective-permute-start.7) | collective-permute-done | bytes 239648 | tf_op jit(solution)/shard_map/ppermute | solution.py:21
  92.3 1.2 select_maximum_fusion
  93.6 0.1 fusion.48
  93.7 0.1 fusion.47
  93.9 0.1 fusion.45
  94.1 0.1 fusion.43
  94.2 0.1 fusion.42
  94.4 0.1 fusion.39
  94.6 0.1 fusion.37
  94.8 0.1 fusion.34
  95.0 0.1 fusion.32
  95.1 0.1 fusion.30
  95.3 0.3 constant_dynamic-update-slice_fusion
  95.5 0.1 fusion.28
  95.8 0.1 fusion.24
  95.9 2.7 %convolution_convert_fusion.1 = bf16[4,104,16]{1,2,0:T(8,128)(2,1)S(1)} fusion(bf16[4,104,10368]{2,1,0:T(8,128)(2,1)S(1)} %fusion.24, bf16[10368,16,1]{0,1,2:T(8,128)(2,1)S(1)} %reshape.66), kind=kOutput, calls=%fused_computation.25 | convolution fusion | flops 138025472 | bytes 8971264 | tf_op jit(solution)/shard_map/dot_general | solution.py:63
  98.5 0.1 copy.9
  98.7 0.1 copy.10
  98.8 0.1 reshape.60
  98.9 0.5 fusion.76
  99.5 0.4 multiply_reduce_fusion
  99.9 1.3 multiply_convert_fusion
  101.2 120.3 %all-gather.2.cloned.1.call-done = bf16[1664,5120]{1,0:T(8,128)(2,1)} async-done(((bf16[104,5120]{1,0:T(8,128)(2,1)}), bf16[1664,5120]{1,0:T(8,128)(2,1)}) %all-gather.2.cloned.1.call-update) | async-done | bytes 17039376 | tf_op jit(solution)/shard_map/all_gather | solution.py:86
  221.5 23.6 %convolution_convert_fusion = bf16[1664,960]{0,1:T(8,128)(2,1)} fusion(bf16[1664,5120]{1,0:T(8,128)(2,1)} %all-gather.2.cloned.1.call-done, bf16[5120,960]{0,1:T(8,128)(2,1)} %bitcast.231), kind=kOutput, calls=%fused_computation.2 | convolution fusion | flops 16359383040 | bytes 30064640 | tf_op jit(solution)/shard_map/dot_general | solution.py:87
  (50 shorter events, 1.7 us)
Async XLA Ops:
  6.5 92.4 %copy-start = (bf16[2,2,16,5120]{3,2,1,0:T(8,128)(2,1)S(1)}, bf16[2,2,16,5120]{3,2,1,0:T(8,128)(2,1)}, u32[]{:S(2)}) copy-start(bf16[2,2,16,5120]{3,2,1,0:T(8,128)(2,1)} %param.12) | copy-start | bytes 1966084
  6.5 215.0 %all-gather.2.cloned.1.call-start = ((), (), s32[]{:S(2)}) async-start(), calls=%async_computation | async-start | bytes 18104320 | tf_op jit(solution)/shard_map/all_gather | solution.py:86
  9.0 10.6 %collective-permute-start = (bf16[1,4,104,384]{3,2,1,0:T(8,128)(2,1)S(1)}, bf16[1,4,104,384]{3,2,1,0:T(8,128)(2,1)S(1)}, u32[]{:S(2)}, u32[]{:S(2)}) collective-permute-start(bf16[1,4,104,384]{3,2,1,0:T(8,128)(2,1)S(1)} %fusion.22), channel_id=1, source_target_pairs={{0,16},{16,32},{32,48},{48,64},{64,80},{80,96},{96,112},{1,17},{17... | collective-permute-start | bytes 958472 | tf_op jit(solution)/shard_map/ppermute | solution.py:10
  20.5 9.4 %collective-permute-start.1 = (bf16[1,4,104,384]{3,2,1,0:T(8,128)(2,1)S(1)}, bf16[1,4,104,384]{3,2,1,0:T(8,128)(2,1)S(1)}, u32[]{:S(2)}, u32[]{:S(2)}) collective-permute-start(bf16[1,4,104,384]{3,2,1,0:T(8,128)(2,1)S(1)} %slice_select_fusion), channel_id=1, source_target_pairs={{0,16},{16,32},{32,48},{48,64},{64,80},{80,96},{96,112},{1,17},{17... | collective-permute-start | bytes 958472 | tf_op jit(solution)/shard_map/ppermute | solution.py:10
  31.0 10.2 %collective-permute-start.2 = (bf16[3,1,104,384]{3,2,1,0:T(8,128)(2,1)S(1)}, bf16[3,1,104,384]{3,2,1,0:T(8,128)(2,1)S(1)}, u32[]{:S(2)}, u32[]{:S(2)}) collective-permute-start(bf16[3,1,104,384]{3,2,1,0:T(8,128)(2,1)S(1)} %get-tuple-element.7), channel_id=1, source_target_pairs={{0,1},{1,2},{2,3},{3,4},{4,5},{5,6},{6,7},{7,8},{8,9},{9,10},{10,1... | collective-permute-start | bytes 718856 | tf_op jit(solution)/shard_map/ppermute | solution.py:18
  38.2 9.0 %collective-permute-start.3 = (bf16[3,1,104,384]{3,2,1,0:T(8,128)(2,1)S(1)}, bf16[3,1,104,384]{3,2,1,0:T(8,128)(2,1)S(1)}, u32[]{:S(2)}, u32[]{:S(2)}) collective-permute-start(bf16[3,1,104,384]{3,2,1,0:T(8,128)(2,1)S(1)} %get-tuple-element.8), channel_id=1, source_target_pairs={{1,0},{2,1},{3,2},{4,3},{5,4},{6,5},{7,6},{8,7},{9,8},{10,9},{11,1... | collective-permute-start | bytes 718856 | tf_op jit(solution)/shard_map/ppermute | solution.py:21
  48.5 1.7 copy-start.2
  48.9 2.2 slice-start
  49.6 2.8 %slice-start.1 = ((s8[7962624]{0:T(1024)(128)(4,1)}), s8[3768320]{0:T(1024)(128)(4,1)S(1)}, s32[]{:S(2)}) async-start(s8[7962624]{0:T(1024)(128)(4,1)} %bitcast.232), calls=%async_computation.2 | async-start | bytes 7536640
  52.5 13.3 %copy-start.3 = (bf16[2,4,104,384]{3,2,1,0:T(8,128)(2,1)S(1)}, bf16[2,4,104,384]{3,2,1,0:T(8,128)(2,1)}, u32[]{:S(2)}) copy-start(bf16[2,4,104,384]{3,2,1,0:T(8,128)(2,1)} %param.9) | copy-start | bytes 1916932
  52.5 32.8 %copy-start.4 = (bf16[3,3,3,384,16]{3,4,2,1,0:T(8,128)(2,1)S(1)}, bf16[3,3,3,384,16]{3,4,2,1,0:T(8,128)(2,1)}, u32[]{:S(2)}) copy-start(bf16[3,3,3,384,16]{3,4,2,1,0:T(8,128)(2,1)} %param.11) | copy-start | bytes 995332
  57.7 8.0 %collective-permute-start.4 = (bf16[1,4,104,384]{3,2,1,0:T(8,128)(2,1)S(1)}, bf16[1,4,104,384]{3,2,1,0:T(8,128)(2,1)S(1)}, u32[]{:S(2)}, u32[]{:S(2)}) collective-permute-start(bf16[1,4,104,384]{3,2,1,0:T(8,128)(2,1)S(1)} %fusion.85), channel_id=1, source_target_pairs={{0,16},{16,32},{32,48},{48,64},{64,80},{80,96},{96,112},{1,17},{17... | collective-permute-start | bytes 958472 | tf_op jit(solution)/shard_map/ppermute | solution.py:10
  65.8 7.7 %collective-permute-start.5 = (bf16[1,4,104,384]{3,2,1,0:T(8,128)(2,1)S(1)}, bf16[1,4,104,384]{3,2,1,0:T(8,128)(2,1)S(1)}, u32[]{:S(2)}, u32[]{:S(2)}) collective-permute-start(bf16[1,4,104,384]{3,2,1,0:T(8,128)(2,1)S(1)} %slice_select_fusion.2), channel_id=1, source_target_pairs={{0,16},{16,32},{32,48},{48,64},{64,80},{80,96},{96,112},{1,17},{17... | collective-permute-start | bytes 958472 | tf_op jit(solution)/shard_map/ppermute | solution.py:10
  74.4 12.1 %collective-permute-start.6 = (bf16[3,1,104,384]{3,2,1,0:T(8,128)(2,1)}, bf16[3,1,104,384]{3,2,1,0:T(8,128)(2,1)S(1)}, u32[]{:S(2)}, u32[]{:S(2)}) collective-permute-start(bf16[3,1,104,384]{3,2,1,0:T(8,128)(2,1)} %get-tuple-element.5), channel_id=1, source_target_pairs={{0,1},{1,2},{2,3},{3,4},{4,5},{5,6},{6,7},{7,8},{8,9},{9,10},{10,1... | collective-permute-start | bytes 718856 | tf_op jit(solution)/shard_map/ppermute | solution.py:18
  83.2 9.2 %collective-permute-start.7 = (bf16[3,1,104,384]{3,2,1,0:T(8,128)(2,1)}, bf16[3,1,104,384]{3,2,1,0:T(8,128)(2,1)S(1)}, u32[]{:S(2)}, u32[]{:S(2)}) collective-permute-start(bf16[3,1,104,384]{3,2,1,0:T(8,128)(2,1)} %get-tuple-element.6), channel_id=1, source_target_pairs={{1,0},{2,1},{3,2},{4,3},{5,4},{6,5},{7,6},{8,7},{9,8},{10,9},{11,1... | collective-permute-start | bytes 718856 | tf_op jit(solution)/shard_map/ppermute | solution.py:21
  221.5 23.6 %copy-start.1 = (bf16[2,2,16,5120]{3,2,1,0:T(8,128)(2,1)S(1)}, bf16[2,2,16,5120]{3,2,1,0:T(8,128)(2,1)}, u32[]{:S(2)}) copy-start(bf16[2,2,16,5120]{3,2,1,0:T(8,128)(2,1)} %param.12) | copy-start | bytes 1966084
Sparse Core Ops, SparseCore 0:
  101.3 120.1 all-gather.1
where the time goes:
time: 252 us
  waiting for transfers between devices  153 us (61%)
  starting transfers between devices  36.4 us (14%)
  matrix products  31.8 us (13%)
  between operations  13.9 us (6%)
  other arithmetic  11.1 us (4%)
  local copies, waits for them, and re-layouts  5.66 us (2%)
    all_gather x1, waiting for transfers between devices, local(): token_rows = lax.all_gather(normed_tok, 'rows', axis=0, tiled=True)  120 us
    dot_general x1, matrix products, local(): jnp.dot(token_rows, flat_qkv, preferred_element_type=jnp.float32)  23.6 us
    ppermute x4, waiting for transfers between devices, passed_along(): return lax.ppermute(block, axis, route)  19.2 us
    ppermute x4, starting transfers between devices, passed_along(): return lax.ppermute(block, axis, route)  16.5 us
    ppermute x2, starting transfers between devices, padded_2(): lax.ppermute(lax.slice_in_dim(block, block.shape[dim] - width, None, axis...  15.9 us
    ppermute x2, waiting for transfers between devices, padded_2(): lax.ppermute(lax.slice_in_dim(block, 0, width, axis=dim), axis, backward)  11.7 us
    dot_general x2, matrix products, causal_conv(): return jnp.dot(columns, flat_kernel, preferred_element_type=jnp.float32)  7.62 us
  transfers between devices with their start and end apart: 9, of which 9 were waited for; matrix products, arithmetic and copies ran while one was open for 0% of the time, Pallas kernels for 0%

commit v1 on v0

--- a/solution.py
+++ b/solution.py
@@ -63,11 +63,29 @@
     return jnp.dot(columns, flat_kernel, preferred_element_type=jnp.float32)
 
 
-def embed_norm(patch_rows, flat_patch):
-    embedded = jnp.dot(patch_rows, flat_patch, preferred_element_type=jnp.float32)
-    centred = embedded - jnp.mean(embedded, axis=-1, keepdims=True)
-    variance = jnp.mean(centred * centred, axis=-1, keepdims=True)
-    return (centred * lax.rsqrt(variance + 1e-06)).astype(jnp.bfloat16)
+def rounded(values):
+    return lax.reduce_precision(values, 8, 7)
+
+
+def three_parts(values):
+    first = rounded(values)
+    second = rounded(values - first)
+    third = values - first - second
+    return [part.astype(jnp.bfloat16) for part in (first, second, third)]
+
+
+def folded_weights(flat_patch, flat_qkv):
+    weights = flat_patch.astype(jnp.float32)
+    depth, width = weights.shape
+    centred = weights - jnp.mean(weights, axis=1, keepdims=True)
+    parts = jnp.concatenate(three_parts(centred), axis=0)
+    left = jnp.concatenate([flat_qkv, parts], axis=0)
+    product = lax.dot_general(left, parts, (((1,), (1,)), ((), ())), preferred_element_type=jnp.float32)
+    product = product[:, :depth] + product[:, depth : 2 * depth] + product[:, 2 * depth :]
+    split = flat_qkv.shape[0]
+    gram = product[split:]
+    gram = (gram[:depth] + gram[depth : 2 * depth] + gram[2 * depth :]) / width
+    return jnp.concatenate([product[:split], gram], axis=0)
 
 
 def local(features, conv_cache, head_cache, conv_weight, head_weight, patch_weight, qkv_weight):
@@ -77,15 +95,25 @@
     normed_out = rms_silu(residual)[None]
     latents = causal_conv(neighbourhood(normed_out, head_cache), head_weight).astype(jnp.bfloat16)
     row_count, col_count, latent_dim = latents.shape
+    depth = 4 * latent_dim
+    local_cols = qkv_weight.shape[2]
     patches = latents.reshape(row_count // 2, 2, col_count // 2, 2, latent_dim)
-    patches = patches.transpose(0, 2, 1, 3, 4).reshape(-1, 4 * latent_dim)
-    flat_patch = patch_weight.reshape(4 * latent_dim, -1)
-    local_cols = qkv_weight.shape[2]
-    flat_qkv = qkv_weight.reshape(qkv_weight.shape[0], 3 * local_cols)
-    normed_tok = embed_norm(patches, flat_patch)
-    token_rows = lax.all_gather(normed_tok, "rows", axis=0, tiled=True)
-    result = jnp.dot(token_rows, flat_qkv, preferred_element_type=jnp.float32).astype(jnp.bfloat16)
-    return result.reshape(token_rows.shape[0], 3, local_cols)
+    patches = patches.transpose(1, 3, 4, 0, 2).reshape(depth, -1)
+    tokens = patches.shape[1]
+    blocks = lax.axis_size("rows")
+    gathered = lax.all_to_all(
+        jnp.broadcast_to(patches[None], (blocks, depth, tokens)), "rows", 0, 0, tiled=True
+    )
+    patch_cols = gathered.transpose(1, 0, 2).reshape(depth, blocks * tokens)
+    flat_qkv = qkv_weight.transpose(1, 2, 0).reshape(3 * local_cols, -1)
+    folded = folded_weights(patch_weight.reshape(depth, -1), flat_qkv)
+    left = jnp.concatenate(three_parts(folded), axis=1)
+    right = jnp.concatenate([patch_cols] * 3, axis=0)
+    product = jnp.dot(left, right, preferred_element_type=jnp.float32)
+    variance = jnp.sum(product[3 * local_cols :] * patch_cols.astype(jnp.float32), axis=0)
+    scale = lax.rsqrt(jnp.maximum(variance, 0.0) + 1e-06)
+    result = (product[: 3 * local_cols] * scale[None]).astype(jnp.bfloat16)
+    return result.reshape(3, local_cols, blocks * tokens).transpose(2, 0, 1)
 
 
 def solution(mesh):

time: 252 us -> 123 us (0.49)
  the two profiles are of different devices: /device:TPU:1 before, /device:TPU:97 now
where the time goes in v1:
time: 123 us; the launch traced here: 122 us
  starting transfers between devices  41.3 us (34%)
  waiting for transfers between devices  37.5 us (30%)
  matrix products  21 us (17%)
  other arithmetic  14.9 us (12%)
  local copies, waits for them, and re-layouts  6.95 us (6%)
    ppermute x4, starting transfers between devices, passed_along(): return lax.ppermute(block, axis, route)  17.8 us
    ppermute x4, waiting for transfers between devices, passed_along(): return lax.ppermute(block, axis, route)  16.2 us
    ppermute x2, starting transfers between devices, padded_2(): lax.ppermute(lax.slice_in_dim(block, block.shape[dim] - width, None, axis...  12.6 us
    dot_general x1, matrix products, folded_weights(): lax.dot_general(left, parts, (((1,), (1,)), ((), ())), preferred_element_...  12.2 us
    ppermute x2, waiting for transfers between devices, padded_2(): lax.ppermute(lax.slice_in_dim(block, 0, width, axis=dim), axis, backward)  11.6 us
    all_to_all x1, waiting for transfers between devices, local(): lax.all_to_all(jnp.broadcast_to(patches[None], (blocks, depth, tokens)),...  8.7 us
    dot_general x2, matrix products, causal_conv(): return jnp.dot(columns, flat_kernel, preferred_element_type=jnp.float32)  7.62 us
    all_to_all x1, starting transfers between devices, local(): lax.all_to_all(jnp.broadcast_to(patches[None], (blocks, depth, tokens)),...  7.05 us
  transfers between devices with their start and end apart: 9, of which 7 were waited for; matrix products, arithmetic and copies ran while one was open for 13% of the time, Pallas kernels for 0%

profile of v1, /device:TPU:97, one launch (start us, length us, event | category | flops | bytes accessed | tf_op | source)
XLA Modules:
  0.0 122.2 jit_solution(856739173473777846)
XLA Ops:
  0.0 1.1 fusion.38
  1.1 1.2 fusion.37
  2.4 1.9 %collective-permute-start = (bf16[1,4,104,384]{3,2,1,0:T(8,128)(2,1)S(1)}, bf16[1,4,104,384]{3,2,1,0:T(8,128)(2,1)S(1)}, u32[]{:S(2)}, u32[]{:S(2)}) collective-permute-start(bf16[1,4,104,384]{3,2,1,0:T(8,128)(2,1)S(1)} %fusion.37), channel_id=1, source_target_pairs={{0,16},{16,32},{32,48},{48,64},{64,80},{80,96},{96,112},{1,17},{17... | collective-permute-start | bytes 958472 | tf_op jit(solution)/shard_map/ppermute | solution.py:10
  4.3 8.4 %collective-permute-done = bf16[1,4,104,384]{3,2,1,0:T(8,128)(2,1)S(1)} collective-permute-done((bf16[1,4,104,384]{3,2,1,0:T(8,128)(2,1)S(1)}, bf16[1,4,104,384]{3,2,1,0:T(8,128)(2,1)S(1)}, u32[]{:S(2)}, u32[]{:S(2)}) %collective-permute-start) | collective-permute-done | bytes 319520 | tf_op jit(solution)/shard_map/ppermute | solution.py:10
  12.6 1.0 slice_select_fusion
  13.7 4.1 %collective-permute-start.1 = (bf16[1,4,104,384]{3,2,1,0:T(8,128)(2,1)S(1)}, bf16[1,4,104,384]{3,2,1,0:T(8,128)(2,1)S(1)}, u32[]{:S(2)}, u32[]{:S(2)}) collective-permute-start(bf16[1,4,104,384]{3,2,1,0:T(8,128)(2,1)S(1)} %slice_select_fusion), channel_id=1, source_target_pairs={{0,16},{16,32},{32,48},{48,64},{64,80},{80,96},{96,112},{1,17},{17... | collective-permute-start | bytes 958472 | tf_op jit(solution)/shard_map/ppermute | solution.py:10
  17.8 5.3 %collective-permute-done.1 = bf16[1,4,104,384]{3,2,1,0:T(8,128)(2,1)S(1)} collective-permute-done((bf16[1,4,104,384]{3,2,1,0:T(8,128)(2,1)S(1)}, bf16[1,4,104,384]{3,2,1,0:T(8,128)(2,1)S(1)}, u32[]{:S(2)}, u32[]{:S(2)}) %collective-permute-start.1) | collective-permute-done | bytes 319520 | tf_op jit(solution)/shard_map/ppermute | solution.py:10
  23.2 1.0 slice_select_fusion.1
  24.2 0.1 pad_maximum_fusion.18
  24.3 7.3 %collective-permute-start.2 = (bf16[3,1,104,384]{3,2,1,0:T(8,128)(2,1)S(1)}, bf16[3,1,104,384]{3,2,1,0:T(8,128)(2,1)S(1)}, u32[]{:S(2)}, u32[]{:S(2)}) collective-permute-start(bf16[3,1,104,384]{3,2,1,0:T(8,128)(2,1)S(1)} %get-tuple-element.7), channel_id=1, source_target_pairs={{0,1},{1,2},{2,3},{3,4},{4,5},{5,6},{6,7},{7,8},{8,9},{9,10},{10,1... | collective-permute-start | bytes 718856 | tf_op jit(solution)/shard_map/ppermute | solution.py:18
  31.6 1.9 %collective-permute-start.3 = (bf16[3,1,104,384]{3,2,1,0:T(8,128)(2,1)S(1)}, bf16[3,1,104,384]{3,2,1,0:T(8,128)(2,1)S(1)}, u32[]{:S(2)}, u32[]{:S(2)}) collective-permute-start(bf16[3,1,104,384]{3,2,1,0:T(8,128)(2,1)S(1)} %get-tuple-element.8), channel_id=1, source_target_pairs={{1,0},{2,1},{3,2},{4,3},{5,4},{6,5},{7,6},{8,7},{9,8},{10,9},{11,1... | collective-permute-start | bytes 718856 | tf_op jit(solution)/shard_map/ppermute | solution.py:21
  33.5 1.2 %convert_reduce_fusion = f32[2,2,16]{2,1,0:T(2,128)S(1)} fusion(bf16[2,2,16,5120]{3,2,1,0:T(8,128)(2,1)} %param.12), kind=kLoop, calls=%fused_computation.40 | loop fusion | flops 655296 | bytes 655616 | tf_op jit(solution)/shard_map/reduce_sum | solution.py:80
  34.8 0.1 div.34
  34.9 5.7 %collective-permute-done.3 = bf16[3,1,104,384]{3,2,1,0:T(8,128)(2,1)S(1)} collective-permute-done((bf16[3,1,104,384]{3,2,1,0:T(8,128)(2,1)S(1)}, bf16[3,1,104,384]{3,2,1,0:T(8,128)(2,1)S(1)}, u32[]{:S(2)}, u32[]{:S(2)}) %collective-permute-start.3) | collective-permute-done | bytes 239648 | tf_op jit(solution)/shard_map/ppermute | solution.py:21
  40.5 1.2 %fusion.24 = bf16[3,6,106,384]{3,2,1,0:T(8,128)(2,1)S(1)} fusion(bf16[3,1,104,384]{3,2,1,0:T(8,128)(2,1)S(1)} %collective-permute-done.3, bf16[3,1,104,384]{3,2,1,0:T(8,128)(2,1)S(1)} %collective-permute-done.2, bf16[1,4,104,384]{3,2,1,0:T(8,128)(2,1)S(1)} %fusion.37, bf16[1,4,104,384]{3,2,1,0:T(8,128)(2,1)S(1)} %slice_select_fusion, ...), kind=kLoop, calls=%fused_computation.33 | loop fusion | flops 13188096 | bytes 2903040 | tf_op jit(solution)/shard_map/concatenate | solution.py:22
  41.9 0.1 fusion.100
  42.1 0.1 fusion.98
  42.4 0.1 fusion.95
  42.6 0.1 fusion.92
  42.9 0.1 fusion.90
  43.1 0.1 fusion.87
  43.3 0.1 fusion.83
  43.5 0.3 bitcast_dynamic-update-slice_fusion.2
  43.8 0.1 fusion.81
  44.0 0.1 fusion.77
  44.1 0.4 slice-done
  44.5 1.3 %slice-done.1 = s8[3768320]{0:T(1024)(128)(4,1)S(1)} async-done(((s8[7962624]{0:T(1024)(128)(4,1)}), s8[3768320]{0:T(1024)(128)(4,1)S(1)}, s32[]{:S(2)}) %slice-start.1) | async-done | bytes 3768344
  45.8 5.0 %multiply_reduce_fusion = (f32[4,104]{1,0:T(4,128)S(1)}, f32[4,104,384]{2,1,0:T(8,128)S(1)}) fusion(bf16[4,104,10368]{2,1,0:T(8,128)(2,1)S(1)} %fusion.77, bf16[10368,384,1]{1,0,2:T(8,128)(2,1)S(1)} %bitcast.242, bf16[1,4,104,384]{3,2,1,0:T(8,128)(2,1)S(1)} %copy-done), kind=kOutput, calls=%fused_computation.62 | convolution fusion | flops 3313409536 | bytes 17548928 | tf_op jit(solution)/shard_map/dot_general | solution.py:63
  50.8 0.3 fusion.111
  51.1 5.6 %collective-permute-start.4 = (bf16[1,4,104,384]{3,2,1,0:T(8,128)(2,1)S(1)}, bf16[1,4,104,384]{3,2,1,0:T(8,128)(2,1)S(1)}, u32[]{:S(2)}, u32[]{:S(2)}) collective-permute-start(bf16[1,4,104,384]{3,2,1,0:T(8,128)(2,1)S(1)} %fusion.111), channel_id=1, source_target_pairs={{0,16},{16,32},{32,48},{48,64},{64,80},{80,96},{96,112},{1,17},{17... | collective-permute-start | bytes 958472 | tf_op jit(solution)/shard_map/ppermute | solution.py:10
  56.7 1.5 %reduce-precision_convert_fusion.1 = (bf16[64,5120]{1,0:T(8,128)(2,1)S(1)}, bf16[64,5120]{1,0:T(8,128)(2,1)}, bf16[64,5120]{1,0:T(8,128)(2,1)}) fusion(bf16[2,2,16,5120]{3,2,1,0:T(8,128)(2,1)S(1)} %copy-done.1, f32[64]{0:T(128)S(1)} %div.34), kind=kLoop, calls=%fused_computation.21 | loop fusion | flops 2949120 | bytes 2621696 | tf_op jit(solution)/shard_map/convert_element_type | solution.py:74
  58.1 2.4 %collective-permute-done.4 = bf16[1,4,104,384]{3,2,1,0:T(8,128)(2,1)S(1)} collective-permute-done((bf16[1,4,104,384]{3,2,1,0:T(8,128)(2,1)S(1)}, bf16[1,4,104,384]{3,2,1,0:T(8,128)(2,1)S(1)}, u32[]{:S(2)}, u32[]{:S(2)}) %collective-permute-start.4) | collective-permute-done | bytes 319520 | tf_op jit(solution)/shard_map/ppermute | solution.py:10
  60.7 6.1 %collective-permute-start.5 = (bf16[1,4,104,384]{3,2,1,0:T(8,128)(2,1)S(1)}, bf16[1,4,104,384]{3,2,1,0:T(8,128)(2,1)}, u32[]{:S(2)}, u32[]{:S(2)}) collective-permute-start(bf16[1,4,104,384]{3,2,1,0:T(8,128)(2,1)S(1)} %slice_select_fusion.2), channel_id=1, source_target_pairs={{0,16},{16,32},{32,48},{48,64},{64,80},{80,96},{96,112},{1,17},{17... | collective-permute-start | bytes 958472 | tf_op jit(solution)/shard_map/ppermute | solution.py:10
  66.8 12.2 %fusion = f32[1152,192]{0,1:T(8,128)S(1)} fusion(bf16[64,5120]{1,0:T(8,128)(2,1)} %get-tuple-element.10, bf16[64,5120]{1,0:T(8,128)(2,1)} %get-tuple-element.11, bf16[64,5120]{1,0:T(8,128)(2,1)S(1)} %get-tuple-element.9, bf16[960,5120]{1,0:T(8,128)(2,1)} %bitcast.239), kind=kOutput, calls=%fused_computation | convolution fusion | flops 2318008320 | bytes 12681216 | tf_op jit(solution)/shard_map/dot_general | solution.py:83
  79.0 0.2 copy.11
  79.2 0.3 reshape.70
  79.5 1.1 slice_select_fusion.3
  80.7 5.3 %collective-permute-start.6 = (bf16[3,1,104,384]{3,2,1,0:T(8,128)(2,1)S(1)}, bf16[3,1,104,384]{3,2,1,0:T(8,128)(2,1)S(1)}, u32[]{:S(2)}, u32[]{:S(2)}) collective-permute-start(bf16[3,1,104,384]{3,2,1,0:T(8,128)(2,1)S(1)} %get-tuple-element.5), channel_id=1, source_target_pairs={{0,1},{1,2},{2,3},{3,4},{4,5},{5,6},{6,7},{7,8},{8,9},{9,10},{10,1... | collective-permute-start | bytes 718856 | tf_op jit(solution)/shard_map/ppermute | solution.py:18
  86.0 1.9 %collective-permute-start.7 = (bf16[3,1,104,384]{3,2,1,0:T(8,128)(2,1)S(1)}, bf16[3,1,104,384]{3,2,1,0:T(8,128)(2,1)S(1)}, u32[]{:S(2)}, u32[]{:S(2)}) collective-permute-start(bf16[3,1,104,384]{3,2,1,0:T(8,128)(2,1)S(1)} %get-tuple-element.6), channel_id=1, source_target_pairs={{1,0},{2,1},{3,2},{4,3},{5,4},{6,5},{7,6},{8,7},{9,8},{10,9},{11,1... | collective-permute-start | bytes 718856 | tf_op jit(solution)/shard_map/ppermute | solution.py:21
  88.0 1.1 collective-permute-done.6
  89.1 5.9 %collective-permute-done.7 = bf16[3,1,104,384]{3,2,1,0:T(8,128)(2,1)S(1)} collective-permute-done((bf16[3,1,104,384]{3,2,1,0:T(8,128)(2,1)S(1)}, bf16[3,1,104,384]{3,2,1,0:T(8,128)(2,1)S(1)}, u32[]{:S(2)}, u32[]{:S(2)}) %collective-permute-start.7) | collective-permute-done | bytes 239648 | tf_op jit(solution)/shard_map/ppermute | solution.py:21
  95.0 1.2 %select_maximum_fusion = bf16[3,6,106,384]{3,2,1,0:T(8,128)(2,1)S(1)} fusion(bf16[3,1,104,384]{3,2,1,0:T(8,128)(2,1)S(1)} %collective-permute-done.7, bf16[3,1,104,384]{3,2,1,0:T(8,128)(2,1)S(1)} %collective-permute-done.6, bf16[1,4,104,384]{3,2,1,0:T(8,128)(2,1)S(1)} %fusion.111, bf16[1,4,104,384]{3,2,1,0:T(8,128)(2,1)S(1)} %slice_select_fusion.2, ...), kind=kLoop, calls=%fused_computation.22 | loop fusion | flops 13188096 | bytes 2903040 | tf_op jit(solution)/shard_map/concatenate | solution.py:22
  96.3 0.1 fusion.74
  96.5 0.1 fusion.72
  96.8 0.1 fusion.69
  97.0 0.1 fusion.66
  97.2 0.1 fusion.64
  97.5 0.1 fusion.61
  97.7 0.1 fusion.57
  97.9 0.3 constant_dynamic-update-slice_fusion
  98.2 0.1 fusion.55
  98.4 0.1 fusion.51
  98.5 2.7 %convolution_convert_fusion = bf16[4,104,16]{1,2,0:T(8,128)(2,1)S(1)} fusion(bf16[4,104,10368]{2,1,0:T(8,128)(2,1)S(1)} %fusion.51, bf16[10368,16,1]{0,1,2:T(8,128)(2,1)S(1)} %reshape.70), kind=kOutput, calls=%fused_computation.44 | convolution fusion | flops 138025472 | bytes 8971264 | tf_op jit(solution)/shard_map/dot_general | solution.py:63
  101.2 0.1 copy.12
  101.3 0.1 copy.13
  101.5 0.1 broadcast_in_dim.7
  101.5 0.8 broadcast_in_dim.16
  102.3 7.0 %all-to-all-start = ((bf16[16,64,104]{2,1,0:T(8,128)(2,1)}), bf16[16,64,104]{2,1,0:T(8,128)(2,1)S(1)}, u32[]{:S(2)}, u32[]{:S(2)}) async-start(bf16[16,64,104]{2,1,0:T(8,128)(2,1)} %broadcast_in_dim.16), calls=%async_computation | async-start | bytes 524288 | tf_op jit(solution)/shard_map/all_to_all | solution.py:104
  109.5 0.1 reduce-precision_convert_fusion.3
  109.6 8.7 %all-to-all-done = bf16[16,64,104]{2,1,0:T(8,128)(2,1)S(1)} async-done(((bf16[16,64,104]{2,1,0:T(8,128)(2,1)}), bf16[16,64,104]{2,1,0:T(8,128)(2,1)S(1)}, u32[]{:S(2)}, u32[]{:S(2)}) %all-to-all-start) | async-done | bytes 213024 | tf_op jit(solution)/shard_map/all_to_all | solution.py:104
  118.3 0.2 copy.14
  118.4 0.3 reshape.65
  118.7 1.2 fusion.39
  120.0 2.2 %fusion.8 = bf16[960,1664]{1,0:T(8,128)(2,1)} fusion(f32[1024,1664]{1,0:T(8,128)S(1)} %fusion.39, f32[1664]{0:T(1024)S(1)} %add_rsqrt_fusion), kind=kLoop, calls=%fused_computation.9 | loop fusion | flops 3194880 | bytes 9591296 | tf_op jit(solution)/shard_map/convert_element_type | solution.py:115
  (57 shorter events, 2.2 us)
Async XLA Ops:
  2.4 10.3 %collective-permute-start = (bf16[1,4,104,384]{3,2,1,0:T(8,128)(2,1)S(1)}, bf16[1,4,104,384]{3,2,1,0:T(8,128)(2,1)S(1)}, u32[]{:S(2)}, u32[]{:S(2)}) collective-permute-start(bf16[1,4,104,384]{3,2,1,0:T(8,128)(2,1)S(1)} %fusion.37), channel_id=1, source_target_pairs={{0,16},{16,32},{32,48},{48,64},{64,80},{80,96},{96,112},{1,17},{17... | collective-permute-start | bytes 958472 | tf_op jit(solution)/shard_map/ppermute | solution.py:10
  13.7 9.5 %collective-permute-start.1 = (bf16[1,4,104,384]{3,2,1,0:T(8,128)(2,1)S(1)}, bf16[1,4,104,384]{3,2,1,0:T(8,128)(2,1)S(1)}, u32[]{:S(2)}, u32[]{:S(2)}) collective-permute-start(bf16[1,4,104,384]{3,2,1,0:T(8,128)(2,1)S(1)} %slice_select_fusion), channel_id=1, source_target_pairs={{0,16},{16,32},{32,48},{48,64},{64,80},{80,96},{96,112},{1,17},{17... | collective-permute-start | bytes 958472 | tf_op jit(solution)/shard_map/ppermute | solution.py:10
  24.3 10.6 %collective-permute-start.2 = (bf16[3,1,104,384]{3,2,1,0:T(8,128)(2,1)S(1)}, bf16[3,1,104,384]{3,2,1,0:T(8,128)(2,1)S(1)}, u32[]{:S(2)}, u32[]{:S(2)}) collective-permute-start(bf16[3,1,104,384]{3,2,1,0:T(8,128)(2,1)S(1)} %get-tuple-element.7), channel_id=1, source_target_pairs={{0,1},{1,2},{2,3},{3,4},{4,5},{5,6},{6,7},{7,8},{8,9},{9,10},{10,1... | collective-permute-start | bytes 718856 | tf_op jit(solution)/shard_map/ppermute | solution.py:18
  31.6 9.0 %collective-permute-start.3 = (bf16[3,1,104,384]{3,2,1,0:T(8,128)(2,1)S(1)}, bf16[3,1,104,384]{3,2,1,0:T(8,128)(2,1)S(1)}, u32[]{:S(2)}, u32[]{:S(2)}) collective-permute-start(bf16[3,1,104,384]{3,2,1,0:T(8,128)(2,1)S(1)} %get-tuple-element.8), channel_id=1, source_target_pairs={{1,0},{2,1},{3,2},{4,3},{5,4},{6,5},{7,6},{8,7},{9,8},{10,9},{11,1... | collective-permute-start | bytes 718856 | tf_op jit(solution)/shard_map/ppermute | solution.py:21
  41.8 1.7 %copy-start = (bf16[1,4,104,384]{3,2,1,0:T(8,128)(2,1)S(1)}, bf16[1,4,104,384]{3,2,1,0:T(8,128)(2,1)}, u32[]{:S(2)}) copy-start(bf16[1,4,104,384]{3,2,1,0:T(8,128)(2,1)} %param.7) | copy-start | bytes 958468
  42.3 2.2 %slice-start = ((s8[7962624]{0:T(1024)(128)(4,1)}), s8[4194304]{0:T(1024)(128)(4,1)S(1)}, s32[]{:S(2)}) async-start(s8[7962624]{0:T(1024)(128)(4,1)} %bitcast.240), calls=%async_computation.1 | async-start | bytes 8388608
  43.0 2.8 %slice-start.1 = ((s8[7962624]{0:T(1024)(128)(4,1)}), s8[3768320]{0:T(1024)(128)(4,1)S(1)}, s32[]{:S(2)}) async-start(s8[7962624]{0:T(1024)(128)(4,1)} %bitcast.240), calls=%async_computation.2 | async-start | bytes 7536640
  45.8 10.9 %copy-start.1 = (bf16[2,2,16,5120]{3,2,1,0:T(8,128)(2,1)S(1)}, bf16[2,2,16,5120]{3,2,1,0:T(8,128)(2,1)}, u32[]{:S(2)}) copy-start(bf16[2,2,16,5120]{3,2,1,0:T(8,128)(2,1)} %param.12) | copy-start | bytes 1966084
  45.8 14.8 %copy-start.2 = (bf16[2,4,104,384]{3,2,1,0:T(8,128)(2,1)S(1)}, bf16[2,4,104,384]{3,2,1,0:T(8,128)(2,1)}, u32[]{:S(2)}) copy-start(bf16[2,4,104,384]{3,2,1,0:T(8,128)(2,1)} %param.9) | copy-start | bytes 1916932
  51.1 9.5 %collective-permute-start.4 = (bf16[1,4,104,384]{3,2,1,0:T(8,128)(2,1)S(1)}, bf16[1,4,104,384]{3,2,1,0:T(8,128)(2,1)S(1)}, u32[]{:S(2)}, u32[]{:S(2)}) collective-permute-start(bf16[1,4,104,384]{3,2,1,0:T(8,128)(2,1)S(1)} %fusion.111), channel_id=1, source_target_pairs={{0,16},{16,32},{32,48},{48,64},{64,80},{80,96},{96,112},{1,17},{17... | collective-permute-start | bytes 958472 | tf_op jit(solution)/shard_map/ppermute | solution.py:10
  60.7 18.8 %collective-permute-start.5 = (bf16[1,4,104,384]{3,2,1,0:T(8,128)(2,1)S(1)}, bf16[1,4,104,384]{3,2,1,0:T(8,128)(2,1)}, u32[]{:S(2)}, u32[]{:S(2)}) collective-permute-start(bf16[1,4,104,384]{3,2,1,0:T(8,128)(2,1)S(1)} %slice_select_fusion.2), channel_id=1, source_target_pairs={{0,16},{16,32},{32,48},{48,64},{64,80},{80,96},{96,112},{1,17},{17... | collective-permute-start | bytes 958472 | tf_op jit(solution)/shard_map/ppermute | solution.py:10
  66.8 12.2 %copy-start.3 = (bf16[3,3,3,384,16]{3,4,2,1,0:T(8,128)(2,1)S(1)}, bf16[3,3,3,384,16]{3,4,2,1,0:T(8,128)(2,1)}, u32[]{:S(2)}) copy-start(bf16[3,3,3,384,16]{3,4,2,1,0:T(8,128)(2,1)} %param.11) | copy-start | bytes 995332
  80.7 8.4 %collective-permute-start.6 = (bf16[3,1,104,384]{3,2,1,0:T(8,128)(2,1)S(1)}, bf16[3,1,104,384]{3,2,1,0:T(8,128)(2,1)S(1)}, u32[]{:S(2)}, u32[]{:S(2)}) collective-permute-start(bf16[3,1,104,384]{3,2,1,0:T(8,128)(2,1)S(1)} %get-tuple-element.5), channel_id=1, source_target_pairs={{0,1},{1,2},{2,3},{3,4},{4,5},{5,6},{6,7},{7,8},{8,9},{9,10},{10,1... | collective-permute-start | bytes 718856 | tf_op jit(solution)/shard_map/ppermute | solution.py:18
  86.0 9.0 %collective-permute-start.7 = (bf16[3,1,104,384]{3,2,1,0:T(8,128)(2,1)S(1)}, bf16[3,1,104,384]{3,2,1,0:T(8,128)(2,1)S(1)}, u32[]{:S(2)}, u32[]{:S(2)}) collective-permute-start(bf16[3,1,104,384]{3,2,1,0:T(8,128)(2,1)S(1)} %get-tuple-element.6), channel_id=1, source_target_pairs={{1,0},{2,1},{3,2},{4,3},{5,4},{6,5},{7,6},{8,7},{9,8},{10,9},{11,1... | collective-permute-start | bytes 718856 | tf_op jit(solution)/shard_map/ppermute | solution.py:21
  102.3 16.0 %all-to-all-start = ((bf16[16,64,104]{2,1,0:T(8,128)(2,1)}), bf16[16,64,104]{2,1,0:T(8,128)(2,1)S(1)}, u32[]{:S(2)}, u32[]{:S(2)}) async-start(bf16[16,64,104]{2,1,0:T(8,128)(2,1)} %broadcast_in_dim.16), calls=%async_computation | async-start | bytes 524288 | tf_op jit(solution)/shard_map/all_to_all | solution.py:104

commit v2 on v0

v2 whole, which is shorter than its diff:
```python
import functools

import jax
import jax.numpy as jnp
from jax import lax
from jax.experimental import pallas as pl
from jax.experimental.pallas import tpu as pltpu
from jax.sharding import PartitionSpec as P

F32 = jnp.float32
BF16 = jnp.bfloat16
EPS = 1e-06
STEP = 14
WIN = 16

MEMORY = 56 << 20


def iota(shape, axis):
    return lax.broadcasted_iota(jnp.int32, shape, axis)


def rms_silu(values):
    scaled = values * lax.rsqrt(jnp.mean(values * values, axis=-1, keepdims=True) + EPS)
    return scaled / (1.0 + jnp.exp(-scaled))


def three_parts(values):
    first = values.astype(BF16)
    rest = values - first.astype(F32)
    second = rest.astype(BF16)
    third = (rest - second.astype(F32)).astype(BF16)
    return first, second, third


def rows_times_rows(left, right):
    return lax.dot_general(left, right, (((1,), (1,)), ((), ())), preferred_element_type=F32)


def feature_windows_kernel(groups, features, send):
    rows, cols, _ = features.shape
    shape = (groups * WIN, cols)
    place = iota(shape, 0)
    source = STEP * (place // WIN) + place % WIN - 1
    pick = (iota(shape, 1) == source).astype(BF16)
    for row in range(rows):
        picked = jnp.dot(pick, features[row], preferred_element_type=F32).astype(BF16)
        for group in range(groups):
            send[group, row] = picked[group * WIN : (group + 1) * WIN]


def cache_windows_kernel(position, conv_cache, head_cache, conv_win, head_win):
    frames, rows, cols, _ = conv_cache.shape
    shape = (WIN, cols)
    place = iota(shape, 0)
    first = STEP * position[0]
    pick_conv = (iota(shape, 1) == first + place - 1).astype(BF16)
    pick_head = ((iota(shape, 1) == first + place) & (place < STEP)).astype(BF16)
    for frame in range(frames):
        for row in range(rows):
            conv_win[frame, row] = jnp.dot(
                pick_conv, conv_cache[frame, row], preferred_element_type=F32
            ).astype(BF16)
            head_win[frame, row] = jnp.dot(
                pick_head, head_cache[frame, row], preferred_element_type=F32
            ).astype(BF16)


def section_kernel(
    cols, position, main, low, high, conv_win, head_win, weight, head, out, normed, sums, left, head_rows, hidden
):
    frames, rows, win, width = main.shape
    count = frames * rows * win
    tap = pl.program_id(0)

    @pl.when(tap == 0)
    def _():
        normed[0:2, 1 : rows + 1] = conv_win[...]
        normed[0:2, 0] = low[0:2]
        normed[0:2, rows + 1] = high[0:2]
        normed[2:, 1 : rows + 1] = rms_silu(main[...].astype(F32)).astype(BF16)
        normed[2:, 0] = rms_silu(low[2:].astype(F32)).astype(BF16)
        normed[2:, rows + 1] = rms_silu(high[2:].astype(F32)).astype(BF16)

    for b in range(3):
        left[:, b * width : (b + 1) * width] = normed[pl.ds(tap, frames), b : b + rows].reshape(
            count, width
        )
    for c in range(3):
        product = jnp.dot(
            left[...], weight[0, :, c].reshape(3 * width, width), preferred_element_type=F32
        )

        @pl.when(tap == 0)
        def _():
            sums[c] = product

        @pl.when(tap > 0)
        def _():
            sums[c] += product

    @pl.when(tap == 2)
    def _():
        update = sums[0] + pltpu.roll(sums[1], count - 1, 0) + pltpu.roll(sums[2], count - 2, 0)
        own = pltpu.roll(main[...].astype(F32).reshape(count, width), count - 1, 0)
        residual = (own + update).astype(BF16).astype(F32)
        place = iota((count, 1), 0) % win
        inside = (place < STEP) & (STEP * position[0] + place < cols)
        normed_out = jnp.where(inside, rms_silu(residual), 0.0).astype(BF16)
        hidden[0 : 2 * rows * win] = head_win[...].reshape(2 * rows * win, width)
        hidden[2 * rows * win :] = normed_out
        depth = head.shape[3]
        head_rows[...] = jnp.zeros_like(head_rows)
        for a in range(3):
            for b in range(3):
                for c in range(3):
                    start = (3 * a + c) * 128 + (2 - b) * depth
                    head_rows[start : start + depth] = head[a, b, c]
        taps = rows_times_rows(hidden[...], head_rows[...])
        shifted = []
        for c in range(3):
            total = jnp.zeros((count, 128), F32)
            for a in range(3):
                total += taps[
                    a * rows * win : a * rows * win + count, (3 * a + c) * 128 : (3 * a + c + 1) * 128
                ]
            shifted.append(total if c == 2 else pltpu.roll(total, 2 - c, 0))
        total = (shifted[0] + shifted[1] + shifted[2]).reshape(frames, rows, win, 128)
        for frame in range(frames):
            piece = total[frame, 0]
            for row in range(1, rows):
                piece += pltpu.roll(total[frame, row], depth * row, 1)
            piece = piece.astype(BF16)
            for target in range(out.shape[1]):
                out[frame, target] = piece


def folded_kernel(patch, qkv, folded, gram, parts):
    depth = patch.shape[2]
    width = patch.shape[3]
    positions = 4 * depth

    def stacked(values):
        pieces = list(three_parts(values))
        pieces.append(jnp.zeros_like(pieces[0]))
        return jnp.concatenate(pieces, axis=1)

    @pl.when(pl.program_id(0) == 0)
    def _():
        for b in range(2):
            for a in range(2):
                weights = patch[a, b].astype(F32)
                centred = weights - jnp.mean(weights, axis=1, keepdims=True)
                for index, part in enumerate(three_parts(centred)):
                    start = index * positions + (2 * b + a) * depth
                    parts[start : start + depth] = part
        product = rows_times_rows(parts[...], parts[...])
        total = jnp.zeros((positions, positions), F32)
        for i in range(3):
            for k in range(3):
                total += product[
                    i * positions : (i + 1) * positions, k * positions : (k + 1) * positions
                ]
        gram[...] = stacked(total / width)

    product = rows_times_rows(qkv[...], parts[...])
    total = (
        product[:, :positions] + product[:, positions : 2 * positions] + product[:, 2 * positions :]
    )
    folded[...] = stacked(total)


def project_kernel(depth, pieces, folded, gram, out, sums, patches, scale):
    groups, blocks, win, lanes = pieces.shape
    positions = 4 * depth
    tokens = patches.shape[0]
    half = tokens // (2 * blocks)
    pad = (half + 7) // 8 * 8

    @pl.when(pl.program_id(0) == 0)
    def _():
        shape = (2 * pad, groups * win)
        row = iota(shape, 0)
        place = iota(shape, 1)
        odd = (row >= pad).astype(jnp.int32)
        patch_col = row - pad * odd
        column = STEP * (place // win) + place % win - 1
        pick = ((column == 2 * patch_col + odd) & (patch_col < half)).astype(BF16)
        for block in range(blocks):
            source = pieces[:, block].reshape(groups * win, lanes)
            sums[block] = jnp.dot(pick, source, preferred_element_type=F32)
        slot = iota((1, lanes), 1) // depth
        for block in range(blocks):
            total = sums[block]
            if block > 0:
                total += jnp.where(slot == 1, pltpu.roll(sums[block - 1], 4 * depth, 1), 0.0)
            if block < blocks - 1:
                total += jnp.where(slot == 4, pltpu.roll(sums[block + 1], 4 * depth, 1), 0.0)
            for i in range(2):
                start = (1 + 2 * i) * depth
                even = pltpu.roll(total, lanes - start, 1)[0:half]
                uneven = pltpu.roll(total, (lanes + 2 * depth - start) % lanes, 1)[pad : pad + half]
                patch = jnp.where(slot < 2, even, jnp.where(slot < 4, uneven, 0.0))
                patch = patch + pltpu.roll(patch, positions, 1)
                first = (2 * block + i) * half
                patches[first : first + half] = patch
        rounded = patches[...].astype(BF16)
        both = jnp.concatenate([rounded, rounded], axis=1)
        same = iota((positions, 2 * lanes), 0) == iota((positions, 2 * lanes), 1)
        probe = jnp.concatenate([gram[...], same.astype(BF16)], axis=0)
        product = rows_times_rows(probe, both)
        variance = jnp.sum(product[:positions] * product[positions:], axis=0, keepdims=True)
        scale[...] = lax.rsqrt(jnp.maximum(variance, 0.0) + EPS)

    rounded = patches[...].astype(BF16)
    both = jnp.concatenate([rounded, rounded], axis=1)
    out[...] = (rows_times_rows(folded[...], both) * scale[...]).astype(BF16)


def params(**kwargs):
    return pltpu.CompilerParams(vmem_limit_bytes=MEMORY, **kwargs)


def whole(shape):
    return pl.BlockSpec(shape, lambda *_: (0,) * len(shape))


def local(features, conv_cache, head_cache, conv_weight, head_weight, patch_weight, qkv_weight):
    groups = lax.axis_size("tm")
    blocks = lax.axis_size("rows")
    _, rows, cols, width = features.shape
    frames = groups
    depth = head_weight.shape[-1]
    local_cols = qkv_weight.shape[2]
    model = qkv_weight.shape[0]
    tokens = blocks * rows * cols // 4
    position = lax.axis_index("tm").astype(jnp.int32).reshape(1)
    scalar = pl.BlockSpec(memory_space=pltpu.SMEM)

    send = pl.pallas_call(
        functools.partial(feature_windows_kernel, groups),
        out_shape=jax.ShapeDtypeStruct((groups, rows, WIN, width), BF16),
        compiler_params=params(),
        name="feature_windows",
    )(features[0])
    main = lax.all_to_all(send, "tm", 0, 0, tiled=True)

    conv_win, head_win = pl.pallas_call(
        cache_windows_kernel,
        in_specs=[scalar, whole(conv_cache.shape), whole(head_cache.shape)],
        out_specs=[whole((2, rows, WIN, width))] * 2,
        grid=(1,),
        out_shape=[jax.ShapeDtypeStruct((2, rows, WIN, width), BF16)] * 2,
        compiler_params=params(),
        name="cache_windows",
    )(position, conv_cache, head_cache)

    flat_qkv = qkv_weight.transpose(1, 2, 0).reshape(3 * local_cols, model)
    positions = 4 * depth
    steps = 4
    share = 3 * local_cols // steps
    folded, gram = pl.pallas_call(
        folded_kernel,
        grid=(steps,),
        in_specs=[whole(patch_weight.shape), pl.BlockSpec((share, model), lambda i: (i, 0))],
        out_specs=[
            pl.BlockSpec((share, 4 * positions), lambda i: (i, 0)),
            whole((positions, 4 * positions)),
        ],
        out_shape=[
            jax.ShapeDtypeStruct((3 * local_cols, 4 * positions), BF16),
            jax.ShapeDtypeStruct((positions, 4 * positions), BF16),
        ],
        scratch_shapes=[pltpu.VMEM((3 * positions, model), BF16)],
        compiler_params=params(),
        name="folded_weights",
    )(patch_weight, flat_qkv)

    down = [(i, i + 1) for i in range(blocks - 1)]
    up = [(i + 1, i) for i in range(blocks - 1)]
    low = lax.ppermute(jnp.concatenate([conv_win[:, rows - 1], main[:, rows - 1]]), "rows", down)
    high = lax.ppermute(jnp.concatenate([conv_win[:, 0], main[:, 0]]), "rows", up)

    head = head_weight.transpose(0, 1, 2, 4, 3)
    count = frames * rows * WIN
    partial = pl.pallas_call(
        functools.partial(section_kernel, cols),
        grid=(3,),
        in_specs=[
            scalar,
            whole(main.shape),
            whole(low.shape),
            whole(high.shape),
            whole(conv_win.shape),
            whole(head_win.shape),
            pl.BlockSpec((1, 3, 3, width, width), lambda i: (i, 0, 0, 0, 0)),
            whole(head.shape),
        ],
        out_specs=whole((frames, blocks, WIN, 128)),
        out_shape=jax.ShapeDtypeStruct((frames, blocks, WIN, 128), BF16),
        scratch_shapes=[
            pltpu.VMEM((frames + 2, rows + 2, WIN, width), BF16),
            pltpu.VMEM((3, count, width), F32),
            pltpu.VMEM((count, 3 * width), BF16),
            pltpu.VMEM((9 * 128, width), BF16),
            pltpu.VMEM((count + 2 * rows * WIN, width), BF16),
        ],
        compiler_params=params(),
        name="section",
    )(position, main, low, high, conv_win, head_win, conv_weight, head)

    pieces = lax.all_to_all(
        partial.reshape(frames * blocks, WIN, 128), ("tm", "rows"), 0, 0, tiled=True
    ).reshape(groups, blocks, WIN, 128)

    half = cols // 2
    pad = (half + 7) // 8 * 8
    result = pl.pallas_call(
        functools.partial(project_kernel, depth),
        grid=(steps,),
        in_specs=[
            whole(pieces.shape),
            pl.BlockSpec((share, 4 * positions), lambda i: (i, 0)),
            whole((positions, 4 * positions)),
        ],
        out_specs=pl.BlockSpec((share, tokens), lambda i: (i, 0)),
        out_shape=jax.ShapeDtypeStruct((3 * local_cols, tokens), BF16),
        scratch_shapes=[
            pltpu.VMEM((blocks, 2 * pad, 128), F32),
            pltpu.VMEM((tokens, 128), F32),
            pltpu.VMEM((1, tokens), F32),
        ],
        compiler_params=params(),
        name="project",
    )(pieces, folded, gram)
    return result.reshape(3, local_cols, tokens).transpose(2, 0, 1)


def solution(mesh):
    return jax.shard_map(
        local,
        mesh=mesh,
        in_specs=(
            P("tm", "rows", None, None),
            P(None, "rows", None, None),
            P(None, "rows", None, None),
            P(),
            P(),
            P(),
            P(None, None, "rows"),
        ),
        out_specs=P("tm", None, "rows"),
        check_vma=False,
    )
```

time: 252 us -> 73 us (0.29)
  waiting for transfers between devices: 153 us -> 14.7 us
  Pallas kernels: 0 us -> 33.2 us
  matrix products: 31.8 us -> 0 us
  starting transfers between devices: 36.4 us -> 22.2 us
  between operations: 13.9 us -> 0.07 us
  other arithmetic: 11.1 us -> 0.04 us
  local copies, waits for them, and re-layouts: 5.66 us -> 2.22 us
    all_gather x1 -> x0, waiting for transfers between devices: 120 us -> none  [local(): token_rows = lax.all_gather(normed_tok, 'rows', axis=0, tiled=True)]
    pallas_call x0 -> x5, Pallas kernels: none -> 33.2 us  [the longest x1 13 us: local(): pl.pallas_call(functools.partial(section_kernel, cols), grid=(3,), in_spe...]
    dot_general x4 -> x0, matrix products: 31.8 us -> none  [the longest x1 23.6 us: local(): jnp.dot(token_rows, flat_qkv, preferred_element_type=jnp.float32)]
    ppermute x8 -> x2, starting transfers between devices: 36.4 us -> 8.95 us  [the longest x1 7.03 us: local(): lax.ppermute(jnp.concatenate([conv_win[:, rows - 1], main[:, rows - 1]]),...]
    ppermute x8 -> x2, waiting for transfers between devices: 32.8 us -> 5.76 us  [the longest x1 5.75 us: local(): lax.ppermute(jnp.concatenate([conv_win[:, 0], main[:, 0]]), 'rows', up)]
    all_to_all x0 -> x2, starting transfers between devices: none -> 13.3 us  [the longest x1 6.88 us: local(): main = lax.all_to_all(send, 'tm', 0, 0, tiled=True)]
    all_to_all x0 -> x2, waiting for transfers between devices: none -> 8.9 us  [the longest x1 5.15 us: local(): lax.all_to_all(partial.reshape(frames * blocks, WIN, 128), ('tm', 'rows')...]
    unnamed x53 -> x8, local copies, waits for them, and re-layouts: 4.77 us -> 1.44 us
  transfers between devices with their start and end apart: 9 -> 4, of which waited for: 9 -> 3; matrix products, arithmetic and copies ran while one was open for 0% -> 1% of each run, Pallas kernels for 0% -> 15%
where the time goes in v2:
time: 73 us; the launch traced here: 72.4 us
  Pallas kernels  33.2 us (45%)
  starting transfers between devices  22.2 us (30%)
  waiting for transfers between devices  14.7 us (20%)
  local copies, waits for them, and re-layouts  2.22 us (3%)
    pallas_call x1, Pallas kernels, local(): pl.pallas_call(functools.partial(section_kernel, cols), grid=(3,), in_spe...  13 us
    pallas_call x1, Pallas kernels, local(): pl.pallas_call(folded_kernel, grid=(steps,), in_specs=[whole(patch_weight...  8.45 us
    pallas_call x1, Pallas kernels, local(): pl.pallas_call(functools.partial(project_kernel, depth), grid=(steps,), i...  7.45 us
    ppermute x1, starting transfers between devices, local(): lax.ppermute(jnp.concatenate([conv_win[:, rows - 1], main[:, rows - 1]]),...  7.03 us
    all_to_all x1, starting transfers between devices, local(): main = lax.all_to_all(send, 'tm', 0, 0, tiled=True)  6.88 us
    all_to_all x1, starting transfers between devices, local(): lax.all_to_all(partial.reshape(frames * blocks, WIN, 128), ('tm', 'rows')...  6.42 us
    ppermute x1, waiting for transfers between devices, local(): lax.ppermute(jnp.concatenate([conv_win[:, 0], main[:, 0]]), 'rows', up)  5.75 us
    all_to_all x1, waiting for transfers between devices, local(): lax.all_to_all(partial.reshape(frames * blocks, WIN, 128), ('tm', 'rows')...  5.15 us
  transfers between devices with their start and end apart: 4, of which 3 were waited for; matrix products, arithmetic and copies ran while one was open for 1% of the time, Pallas kernels for 15%

profile of v2, /device:TPU:1, one launch (start us, length us, event | category | flops | bytes accessed | tf_op | source)
XLA Modules:
  0.0 72.4 jit_solution(5224334506782639487)
XLA Ops:
  0.0 2.0 %feature_windows.1 = bf16[8,4,16,384]{3,2,1,0:T(8,128)(2,1)} custom-call(bf16[4,104,384]{2,1,0:T(8,128)(2,1)} %bitcast.27), custom_call_target="tpu_custom_call" | custom-call | tf_op jit(solution)/shard_map/feature_windows/pallas_call | solution.py:240
  2.0 6.9 %all-to-all-start = ((bf16[8,4,16,384]{3,2,1,0:T(8,128)(2,1)}), bf16[8,4,16,384]{3,2,1,0:T(8,128)(2,1)S(1)}, u32[]{:S(2)}, u32[]{:S(2)}) async-start(bf16[8,4,16,384]{3,2,1,0:T(8,128)(2,1)} %feature_windows.1), calls=%async_computation | async-start | bytes 786432 | tf_op jit(solution)/shard_map/all_to_all | solution.py:246
  8.8 2.3 %cache_windows.1 = (bf16[2,4,16,384]{3,2,1,0:T(8,128)(2,1)}, bf16[2,4,16,384]{3,2,1,0:T(8,128)(2,1)}) custom-call(s32[1]{0:T(128)} %bitcast.position, bf16[2,4,104,384]{3,2,1,0:T(8,128)(2,1)} %conv_cache.1, bf16[2,4,104,384]{3,2,1,0:T(8,128)(2,1)} %head_cache.1), custom_call_target="tpu_custom_call" | custom-call | tf_op jit(solution)/shard_map/cache_windows/pallas_call | solution.py:248
  11.1 0.8 %slice_bitcast_fusion.2 = (bf16[2,16,384]{2,1,0:T(8,128)(2,1)S(1)}, bf16[2,16,384]{2,1,0:T(8,128)(2,1)S(1)}) fusion(bf16[2,4,16,384]{3,2,1,0:T(8,128)(2,1)} %get-tuple-element.9.conv_win), kind=kLoop, calls=%fused_computation.4 | loop fusion | bytes 98304 | tf_op jit(solution)/shard_map/squeeze | solution.py:282
  11.9 3.8 %all-to-all-done.main = bf16[8,4,16,384]{3,2,1,0:T(8,128)(2,1)S(1)} async-done(((bf16[8,4,16,384]{3,2,1,0:T(8,128)(2,1)}), bf16[8,4,16,384]{3,2,1,0:T(8,128)(2,1)S(1)}, u32[]{:S(2)}, u32[]{:S(2)}) %all-to-all-start) | async-done | bytes 393248 | tf_op jit(solution)/shard_map/all_to_all | solution.py:246
  15.6 0.0 copy-start
  15.7 7.0 %collective-permute-start = (bf16[10,16,384]{2,1,0:T(8,128)(2,1)S(1)}, bf16[10,16,384]{2,1,0:T(8,128)(2,1)S(1)}, u32[]{:S(2)}, u32[]{:S(2)}) collective-permute-start(bf16[10,16,384]{2,1,0:T(8,128)(2,1)S(1)} %pad_maximum_fusion), channel_id=1, source_target_pairs={{0,1},{1,2},{2,3},{3,4},{4,5},{5,6},{6,7},{7,8},{8,9},{9,10},{10,1... | collective-permute-start | bytes 368648 | tf_op jit(solution)/shard_map/ppermute | solution.py:281
  22.8 1.9 %collective-permute-start.1 = (bf16[10,16,384]{2,1,0:T(8,128)(2,1)S(1)}, bf16[10,16,384]{2,1,0:T(8,128)(2,1)S(1)}, u32[]{:S(2)}, u32[]{:S(2)}) collective-permute-start(bf16[10,16,384]{2,1,0:T(8,128)(2,1)S(1)} %pad_maximum_fusion.1), channel_id=1, source_target_pairs={{1,0},{2,1},{3,2},{4,3},{5,4},{6,5},{7,6},{8,7},{9,8},{10,9},{11,1... | collective-permute-start | bytes 368648 | tf_op jit(solution)/shard_map/ppermute | solution.py:282
  24.7 0.0 collective-permute-done.low
  24.7 0.0 copy-start.2
  24.7 5.8 %collective-permute-done.1.high = bf16[10,16,384]{2,1,0:T(8,128)(2,1)S(1)} collective-permute-done((bf16[10,16,384]{2,1,0:T(8,128)(2,1)S(1)}, bf16[10,16,384]{2,1,0:T(8,128)(2,1)S(1)}, u32[]{:S(2)}, u32[]{:S(2)}) %collective-permute-start.1) | collective-permute-done | bytes 122912 | tf_op jit(solution)/shard_map/ppermute | solution.py:282
  30.5 0.0 copy-start.3
  30.5 0.0 copy-done
  30.5 0.0 copy-done.2
  30.5 0.6 copy-done.3
  31.1 13.0 %section.1 = bf16[8,16,16,128]{3,2,1,0:T(8,128)(2,1)} custom-call(s32[1]{0:T(128)} %bitcast.position, bf16[8,4,16,384]{3,2,1,0:T(8,128)(2,1)} %copy-done, bf16[10,16,384]{2,1,0:T(8,128)(2,1)} %copy-done.2, bf16[10,16,384]{2,1,0:T(8,128)(2,1)} %copy-done.3, bf16[2,4,16,384]{3,2,1,0:T(8,128)(2,1)} %get-tuple-element.9.conv_win, ...), custom_call_target="tpu_custom_call" | custom-call | tf_op jit(solution)/shard_map/section/pallas_call | solution.py:286
  44.1 6.4 %all-to-all-start.1 = ((bf16[128,16,128]{2,1,0:T(8,128)(2,1)}), bf16[128,16,128]{2,1,0:T(8,128)(2,1)S(1)}, u32[]{:S(2)}, u32[]{:S(2)}) async-start(bf16[128,16,128]{2,1,0:T(8,128)(2,1)} %bitcast.24), calls=%async_computation.1 | async-start | bytes 1048576 | tf_op jit(solution)/shard_map/all_to_all | solution.py:312
  50.6 8.4 %folded_weights.1 = (bf16[960,256]{1,0:T(8,128)(2,1)}, bf16[64,256]{1,0:T(8,128)(2,1)}) custom-call(bf16[2,2,16,5120]{3,2,1,0:T(8,128)(2,1)} %patch.1, bf16[960,5120]{1,0:T(8,128)(2,1)} %bitcast.23), custom_call_target="tpu_custom_call" | custom-call | tf_op jit(solution)/shard_map/folded_weights/pallas_call | solution.py:262
  59.0 5.1 %all-to-all-done.1 = bf16[128,16,128]{2,1,0:T(8,128)(2,1)S(1)} async-done(((bf16[128,16,128]{2,1,0:T(8,128)(2,1)}), bf16[128,16,128]{2,1,0:T(8,128)(2,1)S(1)}, u32[]{:S(2)}, u32[]{:S(2)}) %all-to-all-start.1) | async-done | bytes 524320 | tf_op jit(solution)/shard_map/all_to_all | solution.py:312
  64.2 0.0 copy-start.1
  64.2 0.8 %copy-done.1 = bf16[128,16,128]{2,1,0:T(8,128)(2,1)} copy-done((bf16[128,16,128]{2,1,0:T(8,128)(2,1)}, bf16[128,16,128]{2,1,0:T(8,128)(2,1)S(1)}, u32[]{:S(2)}) %copy-start.1) | copy-done | bytes 524312
  65.0 7.4 %project.1 = bf16[960,1664]{1,0:T(8,128)(2,1)} custom-call(bf16[8,16,16,128]{3,2,1,0:T(8,128)(2,1)} %bitcast.25, bf16[960,256]{1,0:T(8,128)(2,1)} %get-tuple-element.11.folded, bf16[64,256]{1,0:T(8,128)(2,1)} %get-tuple-element.12.gram), custom_call_target="tpu_custom_call" | custom-call | tf_op jit(solution)/shard_map/project/pallas_call | solution.py:318
  (3 shorter events, 0.1 us)
Async XLA Ops:
  2.0 13.7 %all-to-all-start = ((bf16[8,4,16,384]{3,2,1,0:T(8,128)(2,1)}), bf16[8,4,16,384]{3,2,1,0:T(8,128)(2,1)S(1)}, u32[]{:S(2)}, u32[]{:S(2)}) async-start(bf16[8,4,16,384]{3,2,1,0:T(8,128)(2,1)} %feature_windows.1), calls=%async_computation | async-start | bytes 786432 | tf_op jit(solution)/shard_map/all_to_all | solution.py:246
  15.6 14.8 %copy-start = (bf16[8,4,16,384]{3,2,1,0:T(8,128)(2,1)}, bf16[8,4,16,384]{3,2,1,0:T(8,128)(2,1)S(1)}, u32[]{:S(2)}) copy-start(bf16[8,4,16,384]{3,2,1,0:T(8,128)(2,1)S(1)} %all-to-all-done.main) | copy-start | bytes 1179652
  15.7 9.0 %collective-permute-start = (bf16[10,16,384]{2,1,0:T(8,128)(2,1)S(1)}, bf16[10,16,384]{2,1,0:T(8,128)(2,1)S(1)}, u32[]{:S(2)}, u32[]{:S(2)}) collective-permute-start(bf16[10,16,384]{2,1,0:T(8,128)(2,1)S(1)} %pad_maximum_fusion), channel_id=1, source_target_pairs={{0,1},{1,2},{2,3},{3,4},{4,5},{5,6},{6,7},{7,8},{8,9},{9,10},{10,1... | collective-permute-start | bytes 368648 | tf_op jit(solution)/shard_map/ppermute | solution.py:281
  22.8 7.7 %collective-permute-start.1 = (bf16[10,16,384]{2,1,0:T(8,128)(2,1)S(1)}, bf16[10,16,384]{2,1,0:T(8,128)(2,1)S(1)}, u32[]{:S(2)}, u32[]{:S(2)}) collective-permute-start(bf16[10,16,384]{2,1,0:T(8,128)(2,1)S(1)} %pad_maximum_fusion.1), channel_id=1, source_target_pairs={{1,0},{2,1},{3,2},{4,3},{5,4},{6,5},{7,6},{8,7},{9,8},{10,9},{11,1... | collective-permute-start | bytes 368648 | tf_op jit(solution)/shard_map/ppermute | solution.py:282
  24.7 5.8 %copy-start.2 = (bf16[10,16,384]{2,1,0:T(8,128)(2,1)}, bf16[10,16,384]{2,1,0:T(8,128)(2,1)S(1)}, u32[]{:S(2)}) copy-start(bf16[10,16,384]{2,1,0:T(8,128)(2,1)S(1)} %collective-permute-done.low) | copy-start | bytes 368644
  30.5 0.6 copy-start.3
  44.1 20.0 %all-to-all-start.1 = ((bf16[128,16,128]{2,1,0:T(8,128)(2,1)}), bf16[128,16,128]{2,1,0:T(8,128)(2,1)S(1)}, u32[]{:S(2)}, u32[]{:S(2)}) async-start(bf16[128,16,128]{2,1,0:T(8,128)(2,1)} %bitcast.24), calls=%async_computation.1 | async-start | bytes 1048576 | tf_op jit(solution)/shard_map/all_to_all | solution.py:312
  64.2 0.8 %copy-start.1 = (bf16[128,16,128]{2,1,0:T(8,128)(2,1)}, bf16[128,16,128]{2,1,0:T(8,128)(2,1)S(1)}, u32[]{:S(2)}) copy-start(bf16[128,16,128]{2,1,0:T(8,128)(2,1)S(1)} %all-to-all-done.1) | copy-start | bytes 1572868

commit v3 on v0

v3 whole, which is shorter than its diff:
```python
import functools

import jax
import jax.numpy as jnp
from jax import lax
from jax.experimental import pallas as pl
from jax.experimental.pallas import tpu as pltpu
from jax.sharding import PartitionSpec as P

F32 = jnp.float32
BF16 = jnp.bfloat16
EPS = 1e-06
STEP = 14
WIN = 16


def iota(shape, axis):
    return lax.broadcasted_iota(jnp.int32, shape, axis)


def rms_silu(values):
    scaled = values * lax.rsqrt(jnp.mean(values * values, axis=-1, keepdims=True) + EPS)
    return scaled / (1.0 + jnp.exp(-scaled))


def three_parts(values):
    first = values.astype(BF16)
    rest = values - first.astype(F32)
    second = rest.astype(BF16)
    third = (rest - second.astype(F32)).astype(BF16)
    return first, second, third


def rows_times_rows(left, right):
    return lax.dot_general(left, right, (((1,), (1,)), ((), ())), preferred_element_type=F32)


def feature_windows_kernel(groups, features, send, rows_in, sems):
    rows, cols, _ = features.shape
    copies = [
        pltpu.make_async_copy(features.at[row], rows_in.at[row], sems.at[row]) for row in range(rows)
    ]
    for copy in copies:
        copy.start()
    shape = (groups * WIN, cols)
    place = iota(shape, 0)
    source = STEP * (place // WIN) + place % WIN - 1
    pick = (iota(shape, 1) == source).astype(BF16)
    for row in range(rows):
        copies[row].wait()
        picked = jnp.dot(pick, rows_in[row], preferred_element_type=F32).astype(BF16)
        for group in range(groups):
            send[group, row] = picked[group * WIN : (group + 1) * WIN]


def cache_windows_kernel(position, conv_cache, head_cache, conv_win, head_win, conv_in, head_in, sems):
    frames, rows, cols, _ = conv_cache.shape
    copies = [
        pltpu.make_async_copy(conv_cache, conv_in, sems.at[0]),
        pltpu.make_async_copy(head_cache, head_in, sems.at[1]),
    ]
    for copy in copies:
        copy.start()
    shape = (WIN, cols)
    place = iota(shape, 0)
    first = STEP * position[0]
    pick_conv = (iota(shape, 1) == first + place - 1).astype(BF16)
    pick_head = ((iota(shape, 1) == first + place) & (place < STEP)).astype(BF16)
    for copy, pick, source, out in (
        (copies[0], pick_conv, conv_in, conv_win),
        (copies[1], pick_head, head_in, head_win),
    ):
        copy.wait()
        for frame in range(frames):
            for row in range(rows):
                out[frame, row] = jnp.dot(
                    pick, source[frame, row], preferred_element_type=F32
                ).astype(BF16)


def weights_kernel(after, weight, head, weight_out, head_rows, head_in, sems):
    depth = head.shape[3]
    copies = [pltpu.make_async_copy(head, head_in, sems.at[3])]
    copies += [pltpu.make_async_copy(weight.at[a], weight_out.at[a], sems.at[a]) for a in range(3)]
    for copy in copies:
        copy.start()
    head_rows[...] = jnp.zeros_like(head_rows)
    copies[0].wait()
    for a in range(3):
        for b in range(3):
            for c in range(3):
                start = (3 * a + c) * 128 + (2 - b) * depth
                head_rows[start : start + depth] = head_in[a, b, c]
    for copy in copies[1:]:
        copy.wait()


def section_kernel(
    cols, depth, position, main, low, high, conv_win, head_win, weight, head_rows, out, normed, hidden
):
    frames, rows, win, width = main.shape
    count = frames * rows * win
    normed[0:2, 1 : rows + 1] = conv_win[...]
    normed[0:2, 0] = low[0:2]
    normed[0:2, rows + 1] = high[0:2]
    normed[2:, 1 : rows + 1] = rms_silu(main[...].astype(F32)).astype(BF16)
    normed[2:, 0] = rms_silu(low[2:].astype(F32)).astype(BF16)
    normed[2:, rows + 1] = rms_silu(high[2:].astype(F32)).astype(BF16)
    before = 2 * rows * win
    hidden[0:before] = head_win[...].reshape(before, width)

    together = 4
    chunk = together * rows * win
    place = iota((chunk, 1), 0) % win
    inside = (place < STEP) & (STEP * position[0] + place < cols)
    for first in range(0, frames, together):
        left = jnp.concatenate(
            [
                normed[first + a : first + a + together, b : b + rows].reshape(chunk, width)
                for a in range(3)
                for b in range(3)
            ],
            axis=1,
        )
        right = jnp.concatenate(
            [weight[:, :, c].reshape(9 * width, width) for c in range(3)], axis=1
        )
        sums = jnp.dot(left, right, preferred_element_type=F32)
        update = (
            sums[:, :width]
            + pltpu.roll(sums[:, width : 2 * width], chunk - 1, 0)
            + pltpu.roll(sums[:, 2 * width :], chunk - 2, 0)
        )
        own = main[first : first + together].astype(F32).reshape(chunk, width)
        residual = (pltpu.roll(own, chunk - 1, 0) + update).astype(BF16).astype(F32)
        start = before + first * rows * win
        hidden[start : start + chunk] = jnp.where(inside, rms_silu(residual), 0.0).astype(BF16)

    taps = rows_times_rows(hidden[...], head_rows[...])
    shifted = []
    for c in range(3):
        total = jnp.zeros((count, 128), F32)
        for a in range(3):
            total += taps[
                a * rows * win : a * rows * win + count, (3 * a + c) * 128 : (3 * a + c + 1) * 128
            ]
        shifted.append(total if c == 2 else pltpu.roll(total, 2 - c, 0))
    total = (shifted[0] + shifted[1] + shifted[2]).reshape(frames, rows, win, 128)
    for frame in range(frames):
        piece = total[frame, 0]
        for row in range(1, rows):
            piece += pltpu.roll(total[frame, row], depth * row, 1)
        piece = piece.astype(BF16)
        for target in range(out.shape[1]):
            out[frame, target] = piece


def folded_kernel(patch, qkv, folded, gram, parts, qkv_in, sems):
    depth = patch.shape[2]
    width = patch.shape[3]
    positions = 4 * depth
    chunks = sems.shape[0]
    share = qkv.shape[0] // chunks
    copies = []
    for index in range(chunks):
        part = pl.ds(index * share, share)
        copies.append(pltpu.make_async_copy(qkv.at[part], qkv_in.at[part], sems.at[index]))
        copies[-1].start()

    def stacked(values):
        pieces = list(three_parts(values))
        pieces.append(jnp.zeros_like(pieces[0]))
        return jnp.concatenate(pieces, axis=1)

    for b in range(2):
        for a in range(2):
            weights = patch[a, b].astype(F32)
            centred = weights - jnp.mean(weights, axis=1, keepdims=True)
            for index, part in enumerate(three_parts(centred)):
                start = index * positions + (2 * b + a) * depth
                parts[start : start + depth] = part
    product = rows_times_rows(parts[...], parts[...])
    total = jnp.zeros((positions, positions), F32)
    for i in range(3):
        for k in range(3):
            total += product[
                i * positions : (i + 1) * positions, k * positions : (k + 1) * positions
            ]
    gram[...] = stacked(total / width)

    for index in range(chunks):
        copies[index].wait()
        part = pl.ds(index * share, share)
        product = rows_times_rows(qkv_in[part], parts[...])
        folded[part] = stacked(
            product[:, :positions]
            + product[:, positions : 2 * positions]
            + product[:, 2 * positions :]
        )


def project_kernel(depth, pieces, folded, gram, out, sums, patches, columns, staged, sems):
    groups, blocks, win, lanes = pieces.shape
    positions = 4 * depth
    tokens = patches.shape[0]
    half = tokens // (2 * blocks)
    pad = (half + 7) // 8 * 8

    shape = (2 * pad, groups * win)
    row = iota(shape, 0)
    place = iota(shape, 1)
    odd = (row >= pad).astype(jnp.int32)
    patch_col = row - pad * odd
    column = STEP * (place // win) + place % win - 1
    pick = ((column == 2 * patch_col + odd) & (patch_col < half)).astype(BF16)
    for block in range(blocks):
        source = pieces[:, block].reshape(groups * win, lanes)
        sums[block] = jnp.dot(pick, source, preferred_element_type=F32)
    slot = iota((1, lanes), 1) // depth
    turned = [None] * blocks
    for block in range(blocks):
        for near in (block, block + 1):
            if near < blocks and turned[near] is None:
                turned[near] = pltpu.roll(sums[near], 4 * depth, 1)
        total = sums[block]
        if block > 0:
            total += jnp.where(slot == 1, turned[block - 1], 0.0)
        if block < blocks - 1:
            total += jnp.where(slot == 4, turned[block + 1], 0.0)
        for i in range(2):
            start = (1 + 2 * i) * depth
            even = pltpu.roll(total[0:pad], lanes - start, 1)
            uneven = pltpu.roll(total[pad:], (lanes + 2 * depth - start) % lanes, 1)
            patch = jnp.where(slot < 2, even, jnp.where(slot < 4, uneven, 0.0))
            first = (2 * block + i) * half
            patches[first : first + half] = patch[0:half]
    turned = jnp.transpose(patches[...])[0:positions]
    rounded = turned.astype(BF16)
    for index in range(4):
        columns[index * positions : (index + 1) * positions] = rounded
    product = jnp.dot(gram[...], columns[...], preferred_element_type=F32)
    variance = jnp.sum(product * rounded.astype(F32), axis=0, keepdims=True)
    scale = lax.rsqrt(jnp.maximum(variance, 0.0) + EPS)
    chunks = sems.shape[0]
    share = folded.shape[0] // chunks
    copies = []
    for index in range(chunks):
        part = pl.ds(index * share, share)
        product = jnp.dot(folded[part], columns[...], preferred_element_type=F32)
        staged[part] = (product * scale).astype(BF16)
        copies.append(pltpu.make_async_copy(staged.at[part], out.at[part], sems.at[index]))
        copies[-1].start()
    for copy in copies:
        copy.wait()


ON_CHIP = pl.BlockSpec(memory_space=pltpu.VMEM)
IN_HBM = pl.BlockSpec(memory_space=pltpu.HBM)
SCALAR = pl.BlockSpec(memory_space=pltpu.SMEM)


def params(mebibytes):
    return pltpu.CompilerParams(vmem_limit_bytes=mebibytes << 20)


def in_hbm(array):
    return pltpu.with_memory_space_constraint(array, pltpu.HBM)


def feature_windows(features, groups):
    rows, cols, width = features.shape
    return pl.pallas_call(
        functools.partial(feature_windows_kernel, groups),
        in_specs=[IN_HBM],
        out_specs=ON_CHIP,
        out_shape=pltpu.VMEM((groups, rows, WIN, width), BF16),
        scratch_shapes=[pltpu.VMEM(features.shape, BF16), pltpu.SemaphoreType.DMA((rows,))],
        compiler_params=params(8),
        name="feature_windows",
    )(in_hbm(features))


def cache_windows(position, conv_cache, head_cache):
    frames, rows, cols, width = conv_cache.shape
    window = pltpu.VMEM((frames, rows, WIN, width), BF16)
    return pl.pallas_call(
        cache_windows_kernel,
        in_specs=[SCALAR, IN_HBM, IN_HBM],
        out_specs=[ON_CHIP] * 2,
        out_shape=[window, window],
        scratch_shapes=[
            pltpu.VMEM(conv_cache.shape, BF16),
            pltpu.VMEM(head_cache.shape, BF16),
            pltpu.SemaphoreType.DMA((2,)),
        ],
        compiler_params=params(8),
        name="cache_windows",
    )(position, in_hbm(conv_cache), in_hbm(head_cache))


def weights_on_chip(after, weight, head):
    return pl.pallas_call(
        weights_kernel,
        in_specs=[ON_CHIP, IN_HBM, IN_HBM],
        out_specs=[ON_CHIP] * 2,
        out_shape=[pltpu.VMEM(weight.shape, BF16), pltpu.VMEM((9 * 128, weight.shape[3]), BF16)],
        scratch_shapes=[pltpu.VMEM(head.shape, BF16), pltpu.SemaphoreType.DMA((4,))],
        compiler_params=params(8),
        name="weights_on_chip",
    )(after, in_hbm(weight), in_hbm(head))


def section(position, main, low, high, conv_win, head_win, weight, head_rows, cols, depth, blocks):
    frames, rows, win, width = main.shape
    return pl.pallas_call(
        functools.partial(section_kernel, cols, depth),
        in_specs=[SCALAR] + [ON_CHIP] * 7,
        out_specs=ON_CHIP,
        out_shape=pltpu.VMEM((frames, blocks, win, 128), BF16),
        scratch_shapes=[
            pltpu.VMEM((frames + 2, rows + 2, win, width), BF16),
            pltpu.VMEM(((frames + 2) * rows * win, width), BF16),
        ],
        compiler_params=params(20),
        name="section",
    )(position, main, low, high, conv_win, head_win, weight, head_rows)


def folded_weights(patch, qkv):
    positions = 4 * patch.shape[2]
    chunks = 4
    return pl.pallas_call(
        folded_kernel,
        in_specs=[ON_CHIP, IN_HBM],
        out_specs=[ON_CHIP] * 2,
        out_shape=[
            pltpu.VMEM((qkv.shape[0], 4 * positions), BF16),
            pltpu.VMEM((positions, 4 * positions), BF16),
        ],
        scratch_shapes=[
            pltpu.VMEM((3 * positions, patch.shape[3]), BF16),
            pltpu.VMEM(qkv.shape, BF16),
            pltpu.SemaphoreType.DMA((chunks,)),
        ],
        compiler_params=params(24),
        name="folded_weights",
    )(patch, in_hbm(qkv))


def project(pieces, folded, gram, cols, depth):
    groups, blocks, win, lanes = pieces.shape
    half = cols // 2
    pad = (half + 7) // 8 * 8
    tokens = 2 * blocks * half
    outputs = folded.shape[0]
    chunks = 4
    return pl.pallas_call(
        functools.partial(project_kernel, depth),
        in_specs=[ON_CHIP] * 3,
        out_specs=IN_HBM,
        out_shape=pltpu.HBM((outputs, tokens), BF16),
        scratch_shapes=[
            pltpu.VMEM((blocks, 2 * pad, lanes), F32),
            pltpu.VMEM((tokens, lanes), F32),
            pltpu.VMEM((16 * depth, tokens), BF16),
            pltpu.VMEM((outputs, tokens), BF16),
            pltpu.SemaphoreType.DMA((chunks,)),
        ],
        compiler_params=params(20),
        name="project",
    )(pieces, folded, gram)


def local(features, conv_cache, head_cache, conv_weight, head_weight, patch_weight, qkv_weight):
    groups = lax.axis_size("tm")
    blocks = lax.axis_size("rows")
    _, rows, cols, width = features.shape
    depth = head_weight.shape[-1]
    local_cols = qkv_weight.shape[2]
    position = lax.axis_index("tm").astype(jnp.int32).reshape(1)
    head = head_weight.transpose(0, 1, 2, 4, 3)
    flat_qkv = qkv_weight.transpose(1, 2, 0).reshape(3 * local_cols, qkv_weight.shape[0])

    main = lax.all_to_all(feature_windows(features[0], groups), "tm", 0, 0, tiled=True)
    conv_win, head_win = cache_windows(position, conv_cache, head_cache)
    down = [(i, i + 1) for i in range(blocks - 1)]
    up = [(i + 1, i) for i in range(blocks - 1)]
    low = lax.ppermute(jnp.concatenate([conv_win[:, rows - 1], main[:, rows - 1]]), "rows", down)
    high = lax.ppermute(jnp.concatenate([conv_win[:, 0], main[:, 0]]), "rows", up)
    weight, head_rows = weights_on_chip(main, conv_weight, head)
    partial = section(
        position, main, low, high, conv_win, head_win, weight, head_rows, cols, depth, blocks
    )
    pieces = lax.all_to_all(
        partial.reshape(groups * blocks, WIN, 128), ("tm", "rows"), 0, 0, tiled=True
    ).reshape(groups, blocks, WIN, 128)
    folded, gram = folded_weights(patch_weight, flat_qkv)
    result = project(pieces, folded, gram, cols, depth)
    return result.reshape(3, local_cols, result.shape[1]).transpose(2, 0, 1)


def solution(mesh):
    return jax.shard_map(
        local,
        mesh=mesh,
        in_specs=(
            P("tm", "rows", None, None),
            P(None, "rows", None, None),
            P(None, "rows", None, None),
            P(),
            P(),
            P(),
            P(None, None, "rows"),
        ),
        out_specs=P("tm", None, "rows"),
        check_vma=False,
    )
```

time: 252 us -> 61.8 us (0.25)
  waiting for transfers between devices: 153 us -> 13.5 us
  matrix products: 31.8 us -> 0 us
  Pallas kernels: 0 us -> 25.4 us
  starting transfers between devices: 36.4 us -> 22.3 us
  between operations: 13.9 us -> 0.27 us
  other arithmetic: 11.1 us -> 0.04 us
  local copies, waits for them, and re-layouts: 5.66 us -> 0.03 us
    all_gather x1 -> x0, waiting for transfers between devices: 120 us -> none  [local(): token_rows = lax.all_gather(normed_tok, 'rows', axis=0, tiled=True)]
    dot_general x4 -> x0, matrix products: 31.8 us -> none  [the longest x1 23.6 us: local(): jnp.dot(token_rows, flat_qkv, preferred_element_type=jnp.float32)]
    ppermute x8 -> x2, waiting for transfers between devices: 32.8 us -> 2.2 us  [the longest x1 2.2 us: local(): lax.ppermute(jnp.concatenate([conv_win[:, 0], main[:, 0]]), 'rows', up)]
    ppermute x8 -> x2, starting transfers between devices: 36.4 us -> 8.95 us  [the longest x1 7.03 us: local(): lax.ppermute(jnp.concatenate([conv_win[:, rows - 1], main[:, rows - 1]]),...]
    pallas_call x0 -> x6, Pallas kernels: none -> 25.4 us  [the longest x1 7.52 us: folded_weights(): pl.pallas_call(folded_kernel, in_specs=[ON_CHIP, IN_HBM], out_specs=[ON_C...]
    all_to_all x0 -> x2, starting transfers between devices: none -> 13.3 us  [the longest x1 6.89 us: local(): lax.all_to_all(feature_windows(features[0], groups), 'tm', 0, 0, tiled=True)]
    all_to_all x0 -> x2, waiting for transfers between devices: none -> 11.3 us  [the longest x1 6.05 us: local(): lax.all_to_all(partial.reshape(groups * blocks, WIN, 128), ('tm', 'rows')...]
    unnamed x53 -> x2, local copies, waits for them, and re-layouts: 4.77 us -> 0.01 us
  transfers between devices with their start and end apart: 9 -> 4, of which waited for: 9 -> 3; matrix products, arithmetic and copies ran while one was open for 0% -> 0% of each run, Pallas kernels for 0% -> 21%
where the time goes in v3:
time: 61.8 us; the launch traced here: 61.5 us
  Pallas kernels  25.4 us (41%)
  starting transfers between devices  22.3 us (36%)
  waiting for transfers between devices  13.5 us (22%)
    pallas_call x1, Pallas kernels, folded_weights(): pl.pallas_call(folded_kernel, in_specs=[ON_CHIP, IN_HBM], out_specs=[ON_C...  7.52 us
    pallas_call x1, Pallas kernels, section(): pl.pallas_call(functools.partial(section_kernel, cols, depth), in_specs=[...  7.18 us
    ppermute x1, starting transfers between devices, local(): lax.ppermute(jnp.concatenate([conv_win[:, rows - 1], main[:, rows - 1]]),...  7.03 us
    all_to_all x1, starting transfers between devices, local(): lax.all_to_all(feature_windows(features[0], groups), 'tm', 0, 0, tiled=True)  6.89 us
    all_to_all x1, starting transfers between devices, local(): lax.all_to_all(partial.reshape(groups * blocks, WIN, 128), ('tm', 'rows')...  6.43 us
    all_to_all x1, waiting for transfers between devices, local(): lax.all_to_all(partial.reshape(groups * blocks, WIN, 128), ('tm', 'rows')...  6.05 us
    all_to_all x1, waiting for transfers between devices, local(): lax.all_to_all(feature_windows(features[0], groups), 'tm', 0, 0, tiled=True)  5.21 us
    pallas_call x1, Pallas kernels, weights_on_chip(): pl.pallas_call(weights_kernel, in_specs=[ON_CHIP, IN_HBM, IN_HBM], out_sp...  3.54 us
  transfers between devices with their start and end apart: 4, of which 3 were waited for; matrix products, arithmetic and copies ran while one was open for 0% of the time, Pallas kernels for 21%

profile of v3, /device:TPU:1, one launch (start us, length us, event | category | flops | bytes accessed | tf_op | source)
XLA Modules:
  0.0 61.5 jit_solution(8688975460860882863)
XLA Ops:
  0.0 2.4 %feature_windows.1 = bf16[8,4,16,384]{3,2,1,0:T(8,128)(2,1)} custom-call(bf16[4,104,384]{2,1,0:T(8,128)(2,1)} %bitcast.26), custom_call_target="tpu_custom_call" | custom-call | tf_op jit(solution)/shard_map/feature_windows/pallas_call | solution.py:272
  2.4 6.9 %all-to-all-start = ((bf16[8,4,16,384]{3,2,1,0:T(8,128)(2,1)}), bf16[8,4,16,384]{3,2,1,0:T(8,128)(2,1)S(1)}, u32[]{:S(2)}, u32[]{:S(2)}) async-start(bf16[8,4,16,384]{3,2,1,0:T(8,128)(2,1)} %feature_windows.1), calls=%async_computation | async-start | bytes 786432 | tf_op jit(solution)/shard_map/all_to_all | solution.py:384
  9.2 1.6 %cache_windows.1 = (bf16[2,4,16,384]{3,2,1,0:T(8,128)(2,1)S(1)}, bf16[2,4,16,384]{3,2,1,0:T(8,128)(2,1)S(1)}) custom-call(s32[1]{0:T(128)} %bitcast.position, bf16[2,4,104,384]{3,2,1,0:T(8,128)(2,1)} %conv_cache.1, bf16[2,4,104,384]{3,2,1,0:T(8,128)(2,1)} %head_cache.1), custom_call_target="tpu_custom_call" | custom-call | tf_op jit(solution)/shard_map/cache_windows/pallas_call | solution.py:286
  10.8 5.2 %all-to-all-done.after.main = bf16[8,4,16,384]{3,2,1,0:T(8,128)(2,1)S(1)} async-done(((bf16[8,4,16,384]{3,2,1,0:T(8,128)(2,1)}), bf16[8,4,16,384]{3,2,1,0:T(8,128)(2,1)S(1)}, u32[]{:S(2)}, u32[]{:S(2)}) %all-to-all-start) | async-done | bytes 393248 | tf_op jit(solution)/shard_map/all_to_all | solution.py:384
  16.1 7.0 %collective-permute-start = (bf16[10,16,384]{2,1,0:T(8,128)(2,1)S(1)}, bf16[10,16,384]{2,1,0:T(8,128)(2,1)S(1)}, u32[]{:S(2)}, u32[]{:S(2)}) collective-permute-start(bf16[10,16,384]{2,1,0:T(8,128)(2,1)S(1)} %pad_maximum_fusion), channel_id=1, source_target_pairs={{0,1},{1,2},{2,3},{3,4},{4,5},{5,6},{6,7},{7,8},{8,9},{9,10},{10,1... | collective-permute-start | bytes 368648 | tf_op jit(solution)/shard_map/ppermute | solution.py:388
  23.2 1.9 %collective-permute-start.1 = (bf16[10,16,384]{2,1,0:T(8,128)(2,1)S(1)}, bf16[10,16,384]{2,1,0:T(8,128)(2,1)S(1)}, u32[]{:S(2)}, u32[]{:S(2)}) collective-permute-start(bf16[10,16,384]{2,1,0:T(8,128)(2,1)S(1)} %pad_maximum_fusion.1), channel_id=1, source_target_pairs={{1,0},{2,1},{3,2},{4,3},{5,4},{6,5},{7,6},{8,7},{9,8},{10,9},{11,1... | collective-permute-start | bytes 368648 | tf_op jit(solution)/shard_map/ppermute | solution.py:389
  25.1 0.0 copy-start
  25.1 3.5 %weights_on_chip.1 = (bf16[3,3,3,384,384]{4,3,2,1,0:T(8,128)(2,1)S(1)}, bf16[1152,384]{1,0:T(8,128)(2,1)S(1)}) custom-call(bf16[8,4,16,384]{3,2,1,0:T(8,128)(2,1)S(1)} %all-to-all-done.after.main, bf16[3,3,3,384,384]{4,3,2,1,0:T(8,128)(2,1)} %weight.1, bf16[3,3,3,16,384]{4,3,2,1,0:T(8,128)(2,1)} %bitcast.25), custom_call_target="tpu_custom_call" | custom-call | tf_op jit(solution)/shard_map/weights_on_chip/pallas_call | solution.py:302
  28.7 0.0 collective-permute-done.low
  28.7 2.2 %collective-permute-done.1.high = bf16[10,16,384]{2,1,0:T(8,128)(2,1)S(1)} collective-permute-done((bf16[10,16,384]{2,1,0:T(8,128)(2,1)S(1)}, bf16[10,16,384]{2,1,0:T(8,128)(2,1)S(1)}, u32[]{:S(2)}, u32[]{:S(2)}) %collective-permute-start.1) | collective-permute-done | bytes 122912 | tf_op jit(solution)/shard_map/ppermute | solution.py:389
  30.9 7.2 %section.1 = bf16[8,16,16,128]{3,2,1,0:T(8,128)(2,1)} custom-call(s32[1]{0:T(128)} %bitcast.position, bf16[8,4,16,384]{3,2,1,0:T(8,128)(2,1)S(1)} %all-to-all-done.after.main, bf16[10,16,384]{2,1,0:T(8,128)(2,1)S(1)} %collective-permute-done.low, bf16[10,16,384]{2,1,0:T(8,128)(2,1)S(1)} %collective-permute-done.1.high, ...), custom_call_target="tpu_custom_call" | custom-call | tf_op jit(solution)/shard_map/section/pallas_call | solution.py:315
  38.1 6.4 %all-to-all-start.1 = ((bf16[128,16,128]{2,1,0:T(8,128)(2,1)}), bf16[128,16,128]{2,1,0:T(8,128)(2,1)S(1)}, u32[]{:S(2)}, u32[]{:S(2)}) async-start(bf16[128,16,128]{2,1,0:T(8,128)(2,1)} %bitcast.7), calls=%async_computation.1 | async-start | bytes 1048576 | tf_op jit(solution)/shard_map/all_to_all | solution.py:394
  44.5 0.0 copy-done
  44.5 7.5 %folded_weights.1 = (bf16[960,256]{1,0:T(8,128)(2,1)S(1)}, bf16[64,256]{1,0:T(8,128)(2,1)S(1)}) custom-call(bf16[2,2,16,5120]{3,2,1,0:T(8,128)(2,1)S(1)} %copy-done, bf16[960,5120]{1,0:T(8,128)(2,1)} %bitcast.24), custom_call_target="tpu_custom_call" | custom-call | tf_op jit(solution)/shard_map/folded_weights/pallas_call | solution.py:332
  52.0 6.0 %all-to-all-done.1 = bf16[128,16,128]{2,1,0:T(8,128)(2,1)S(1)} async-done(((bf16[128,16,128]{2,1,0:T(8,128)(2,1)}), bf16[128,16,128]{2,1,0:T(8,128)(2,1)S(1)}, u32[]{:S(2)}, u32[]{:S(2)}) %all-to-all-start.1) | async-done | bytes 524320 | tf_op jit(solution)/shard_map/all_to_all | solution.py:394
  58.1 3.2 %project.1 = bf16[960,1664]{1,0:T(8,128)(2,1)} custom-call(bf16[8,16,16,128]{3,2,1,0:T(8,128)(2,1)S(1)} %bitcast.23, bf16[960,256]{1,0:T(8,128)(2,1)S(1)} %get-tuple-element.15.folded, bf16[64,256]{1,0:T(8,128)(2,1)S(1)} %get-tuple-element.16.gram), custom_call_target="tpu_custom_call" | custom-call | tf_op jit(solution)/shard_map/project/pallas_call | solution.py:357
  (4 shorter events, 0.1 us)
Async XLA Ops:
  2.4 13.7 %all-to-all-start = ((bf16[8,4,16,384]{3,2,1,0:T(8,128)(2,1)}), bf16[8,4,16,384]{3,2,1,0:T(8,128)(2,1)S(1)}, u32[]{:S(2)}, u32[]{:S(2)}) async-start(bf16[8,4,16,384]{3,2,1,0:T(8,128)(2,1)} %feature_windows.1), calls=%async_computation | async-start | bytes 786432 | tf_op jit(solution)/shard_map/all_to_all | solution.py:384
  16.1 12.6 %collective-permute-start = (bf16[10,16,384]{2,1,0:T(8,128)(2,1)S(1)}, bf16[10,16,384]{2,1,0:T(8,128)(2,1)S(1)}, u32[]{:S(2)}, u32[]{:S(2)}) collective-permute-start(bf16[10,16,384]{2,1,0:T(8,128)(2,1)S(1)} %pad_maximum_fusion), channel_id=1, source_target_pairs={{0,1},{1,2},{2,3},{3,4},{4,5},{5,6},{6,7},{7,8},{8,9},{9,10},{10,1... | collective-permute-start | bytes 368648 | tf_op jit(solution)/shard_map/ppermute | solution.py:388
  23.2 7.7 %collective-permute-start.1 = (bf16[10,16,384]{2,1,0:T(8,128)(2,1)S(1)}, bf16[10,16,384]{2,1,0:T(8,128)(2,1)S(1)}, u32[]{:S(2)}, u32[]{:S(2)}) collective-permute-start(bf16[10,16,384]{2,1,0:T(8,128)(2,1)S(1)} %pad_maximum_fusion.1), channel_id=1, source_target_pairs={{1,0},{2,1},{3,2},{4,3},{5,4},{6,5},{7,6},{8,7},{9,8},{10,9},{11,1... | collective-permute-start | bytes 368648 | tf_op jit(solution)/shard_map/ppermute | solution.py:389
  25.1 19.4 %copy-start = (bf16[2,2,16,5120]{3,2,1,0:T(8,128)(2,1)S(1)}, bf16[2,2,16,5120]{3,2,1,0:T(8,128)(2,1)}, u32[]{:S(2)}) copy-start(bf16[2,2,16,5120]{3,2,1,0:T(8,128)(2,1)} %patch.1) | copy-start | bytes 1966084
  38.1 20.0 %all-to-all-start.1 = ((bf16[128,16,128]{2,1,0:T(8,128)(2,1)}), bf16[128,16,128]{2,1,0:T(8,128)(2,1)S(1)}, u32[]{:S(2)}, u32[]{:S(2)}) async-start(bf16[128,16,128]{2,1,0:T(8,128)(2,1)} %bitcast.7), calls=%async_computation.1 | async-start | bytes 1048576 | tf_op jit(solution)/shard_map/all_to_all | solution.py:394

commit v4 on v3

--- a/solution.py
+++ b/solution.py
@@ -35,22 +35,36 @@
     return lax.dot_general(left, right, (((1,), (1,)), ((), ())), preferred_element_type=F32)
 
 
-def feature_windows_kernel(groups, features, send, rows_in, sems):
-    rows, cols, _ = features.shape
+def feature_windows_kernel(groups, features, send, rows_in, windows, sems_in, sems_out):
+    rows, cols, width = features.shape
     copies = [
-        pltpu.make_async_copy(features.at[row], rows_in.at[row], sems.at[row]) for row in range(rows)
+        pltpu.make_async_copy(features.at[row], rows_in.at[row], sems_in.at[row])
+        for row in range(rows)
     ]
     for copy in copies:
         copy.start()
-    shape = (groups * WIN, cols)
-    place = iota(shape, 0)
-    source = STEP * (place // WIN) + place % WIN - 1
-    pick = (iota(shape, 1) == source).astype(BF16)
+    after = STEP * (groups - 1) + WIN - 1 - cols
+    results = []
     for row in range(rows):
         copies[row].wait()
-        picked = jnp.dot(pick, rows_in[row], preferred_element_type=F32).astype(BF16)
+        values = jnp.concatenate(
+            [
+                jnp.zeros((8, width), F32),
+                rows_in[row].astype(F32),
+                jnp.zeros(((after + 7) // 8 * 8, width), F32),
+            ],
+            axis=0,
+        )
         for group in range(groups):
-            send[group, row] = picked[group * WIN : (group + 1) * WIN]
+            first = 8 + STEP * group - 1
+            windows[group, row] = values[first : first + WIN].astype(BF16)
+        part = pl.ds(row, 1)
+        results.append(
+            pltpu.make_async_copy(windows.at[:, part], send.at[:, part], sems_out.at[row])
+        )
+        results[-1].start()
+    for copy in results:
+        copy.wait()
 
 
 def cache_windows_kernel(position, conv_cache, head_cache, conv_win, head_win, conv_in, head_in, sems):
@@ -78,13 +92,14 @@
                 ).astype(BF16)
 
 
-def weights_kernel(after, weight, head, weight_out, head_rows, head_in, sems):
+def weights_kernel(main, weight, head, weight_out, head_rows, normed, head_in, sems):
     depth = head.shape[3]
     copies = [pltpu.make_async_copy(head, head_in, sems.at[3])]
     copies += [pltpu.make_async_copy(weight.at[a], weight_out.at[a], sems.at[a]) for a in range(3)]
     for copy in copies:
         copy.start()
     head_rows[...] = jnp.zeros_like(head_rows)
+    normed[...] = rms_silu(main[...].astype(F32)).astype(BF16)
     copies[0].wait()
     for a in range(3):
         for b in range(3):
@@ -96,23 +111,25 @@
 
 
 def section_kernel(
-    cols, depth, position, main, low, high, conv_win, head_win, weight, head_rows, out, normed, hidden
+    cols, depth, place_in_mesh, main, near, far, conv_win, head_win, weight, head_rows, ready, out, normed, hidden
 ):
     frames, rows, win, width = main.shape
     count = frames * rows * win
     normed[0:2, 1 : rows + 1] = conv_win[...]
-    normed[0:2, 0] = low[0:2]
-    normed[0:2, rows + 1] = high[0:2]
-    normed[2:, 1 : rows + 1] = rms_silu(main[...].astype(F32)).astype(BF16)
-    normed[2:, 0] = rms_silu(low[2:].astype(F32)).astype(BF16)
-    normed[2:, rows + 1] = rms_silu(high[2:].astype(F32)).astype(BF16)
+    normed[2:, 1 : rows + 1] = ready[...]
+    odd = place_in_mesh[1] % 2 == 1
+    for edge, when_odd, when_even in ((0, near, far), (rows + 1, far, near)):
+        cached = jnp.where(odd, when_odd[0:2], when_even[0:2])
+        values = jnp.where(odd, when_odd[2:].astype(F32), when_even[2:].astype(F32))
+        normed[0:2, edge] = cached
+        normed[2:, edge] = rms_silu(values).astype(BF16)
     before = 2 * rows * win
     hidden[0:before] = head_win[...].reshape(before, width)
 
     together = 4
     chunk = together * rows * win
     place = iota((chunk, 1), 0) % win
-    inside = (place < STEP) & (STEP * position[0] + place < cols)
+    inside = (place < STEP) & (STEP * place_in_mesh[0] + place < cols)
     for first in range(0, frames, together):
         left = jnp.concatenate(
             [
@@ -272,9 +289,14 @@
     return pl.pallas_call(
         functools.partial(feature_windows_kernel, groups),
         in_specs=[IN_HBM],
-        out_specs=ON_CHIP,
-        out_shape=pltpu.VMEM((groups, rows, WIN, width), BF16),
-        scratch_shapes=[pltpu.VMEM(features.shape, BF16), pltpu.SemaphoreType.DMA((rows,))],
+        out_specs=IN_HBM,
+        out_shape=pltpu.HBM((groups, rows, WIN, width), BF16),
+        scratch_shapes=[
+            pltpu.VMEM(features.shape, BF16),
+            pltpu.VMEM((groups, rows, WIN, width), BF16),
+            pltpu.SemaphoreType.DMA((rows,)),
+            pltpu.SemaphoreType.DMA((rows,)),
+        ],
         compiler_params=params(8),
         name="feature_windows",
     )(in_hbm(features))
@@ -298,23 +320,27 @@
     )(position, in_hbm(conv_cache), in_hbm(head_cache))
 
 
-def weights_on_chip(after, weight, head):
+def weights_on_chip(main, weight, head):
     return pl.pallas_call(
         weights_kernel,
         in_specs=[ON_CHIP, IN_HBM, IN_HBM],
-        out_specs=[ON_CHIP] * 2,
-        out_shape=[pltpu.VMEM(weight.shape, BF16), pltpu.VMEM((9 * 128, weight.shape[3]), BF16)],
+        out_specs=[ON_CHIP] * 3,
+        out_shape=[
+            pltpu.VMEM(weight.shape, BF16),
+            pltpu.VMEM((9 * 128, weight.shape[3]), BF16),
+            pltpu.VMEM(main.shape, BF16),
+        ],
         scratch_shapes=[pltpu.VMEM(head.shape, BF16), pltpu.SemaphoreType.DMA((4,))],
         compiler_params=params(8),
         name="weights_on_chip",
-    )(after, in_hbm(weight), in_hbm(head))
-
-
-def section(position, main, low, high, conv_win, head_win, weight, head_rows, cols, depth, blocks):
+    )(main, in_hbm(weight), in_hbm(head))
+
+
+def section(place_in_mesh, main, near, far, conv_win, head_win, weight, head_rows, ready, cols, depth, blocks):
     frames, rows, win, width = main.shape
     return pl.pallas_call(
         functools.partial(section_kernel, cols, depth),
-        in_specs=[SCALAR] + [ON_CHIP] * 7,
+        in_specs=[SCALAR] + [ON_CHIP] * 8,
         out_specs=ON_CHIP,
         out_shape=pltpu.VMEM((frames, blocks, win, 128), BF16),
         scratch_shapes=[
@@ -323,7 +349,7 @@
         ],
         compiler_params=params(20),
         name="section",
-    )(position, main, low, high, conv_win, head_win, weight, head_rows)
+    )(place_in_mesh, main, near, far, conv_win, head_win, weight, head_rows, ready)
 
 
 def folded_weights(patch, qkv):
@@ -371,25 +397,35 @@
     )(pieces, folded, gram)
 
 
+def swaps(count, first):
+    pairs = [(i, i + 1) for i in range(first, count - 1, 2)]
+    return pairs + [(target, source) for source, target in pairs]
+
+
 def local(features, conv_cache, head_cache, conv_weight, head_weight, patch_weight, qkv_weight):
     groups = lax.axis_size("tm")
     blocks = lax.axis_size("rows")
     _, rows, cols, width = features.shape
     depth = head_weight.shape[-1]
     local_cols = qkv_weight.shape[2]
-    position = lax.axis_index("tm").astype(jnp.int32).reshape(1)
+    block = lax.axis_index("rows")
+    place_in_mesh = jnp.stack([lax.axis_index("tm"), block]).astype(jnp.int32)
     head = head_weight.transpose(0, 1, 2, 4, 3)
     flat_qkv = qkv_weight.transpose(1, 2, 0).reshape(3 * local_cols, qkv_weight.shape[0])
 
     main = lax.all_to_all(feature_windows(features[0], groups), "tm", 0, 0, tiled=True)
-    conv_win, head_win = cache_windows(position, conv_cache, head_cache)
-    down = [(i, i + 1) for i in range(blocks - 1)]
-    up = [(i + 1, i) for i in range(blocks - 1)]
-    low = lax.ppermute(jnp.concatenate([conv_win[:, rows - 1], main[:, rows - 1]]), "rows", down)
-    high = lax.ppermute(jnp.concatenate([conv_win[:, 0], main[:, 0]]), "rows", up)
-    weight, head_rows = weights_on_chip(main, conv_weight, head)
+    conv_win, head_win = cache_windows(place_in_mesh, conv_cache, head_cache)
+    def edge(row):
+        return jnp.concatenate(
+            [lax.dynamic_index_in_dim(part, row, 1, False) for part in (conv_win, main)]
+        )
+
+    odd = block % 2
+    far = lax.ppermute(edge((rows - 1) * odd), "rows", swaps(blocks, 1))
+    near = lax.ppermute(edge((rows - 1) * (1 - odd)), "rows", swaps(blocks, 0))
+    weight, head_rows, ready = weights_on_chip(main, conv_weight, head)
     partial = section(
-        position, main, low, high, conv_win, head_win, weight, head_rows, cols, depth, blocks
+        place_in_mesh, main, near, far, conv_win, head_win, weight, head_rows, ready, cols, depth, blocks
     )
     pieces = lax.all_to_all(
         partial.reshape(groups * blocks, WIN, 128), ("tm", "rows"), 0, 0, tiled=True

time: 61.8 us -> 58.4 us (0.945)
  waiting for transfers between devices: 13.5 us -> 10.6 us
  starting transfers between devices: 22.3 us -> 21.4 us
    ppermute x2, waiting for transfers between devices: 2.2 us -> 0.01 us  [the longest x1 0.01 us: local(): near = lax.ppermute(edge((rows - 1) * (1 - odd)), 'rows', swaps(blocks, 0))]
    ppermute x2, starting transfers between devices: 8.95 us -> 7.11 us  [the longest x1 7.03 us: local(): far = lax.ppermute(edge((rows - 1) * odd), 'rows', swaps(blocks, 1))]
    all_to_all x1, starting transfers between devices: 6.43 us -> 7.43 us  [local(): lax.all_to_all(partial.reshape(groups * blocks, WIN, 128), ('tm', 'rows')...]
    all_to_all x1, waiting for transfers between devices: 5.21 us -> 4.59 us  [local(): lax.all_to_all(feature_windows(features[0], groups), 'tm', 0, 0, tiled=True)]
  transfers between devices with their start and end apart: 4 -> 4, of which waited for: 3 -> 2; matrix products, arithmetic and copies ran while one was open for 0% -> 0% of each run, Pallas kernels for 21% -> 23%
where the time goes in v4:
time: 58.4 us; the launch traced here: 58.1 us
  Pallas kernels  25.6 us (44%)
  starting transfers between devices  21.4 us (37%)
  waiting for transfers between devices  10.6 us (18%)
    pallas_call x1, Pallas kernels, folded_weights(): pl.pallas_call(folded_kernel, in_specs=[ON_CHIP, IN_HBM], out_specs=[ON_C...  7.53 us
    pallas_call x1, Pallas kernels, section(): pl.pallas_call(functools.partial(section_kernel, cols, depth), in_specs=[...  7.5 us
    all_to_all x1, starting transfers between devices, local(): lax.all_to_all(partial.reshape(groups * blocks, WIN, 128), ('tm', 'rows')...  7.43 us
    ppermute x1, starting transfers between devices, local(): far = lax.ppermute(edge((rows - 1) * odd), 'rows', swaps(blocks, 1))  7.03 us
    all_to_all x1, starting transfers between devices, local(): lax.all_to_all(feature_windows(features[0], groups), 'tm', 0, 0, tiled=True)  6.89 us
    all_to_all x1, waiting for transfers between devices, local(): lax.all_to_all(partial.reshape(groups * blocks, WIN, 128), ('tm', 'rows')...  6.04 us
    all_to_all x1, waiting for transfers between devices, local(): lax.all_to_all(feature_windows(features[0], groups), 'tm', 0, 0, tiled=True)  4.59 us
    pallas_call x1, Pallas kernels, weights_on_chip(): pl.pallas_call(weights_kernel, in_specs=[ON_CHIP, IN_HBM, IN_HBM], out_sp...  3.49 us
  transfers between devices with their start and end apart: 4, of which 2 were waited for; matrix products, arithmetic and copies ran while one was open for 0% of the time, Pallas kernels for 23%

profile of v4, /device:TPU:1, one launch (start us, length us, event | category | flops | bytes accessed | tf_op | source)
XLA Modules:
  0.0 58.1 jit_solution(7798399078974644258)
XLA Ops:
  0.0 1.7 %feature_windows.1 = bf16[8,4,16,384]{3,2,1,0:T(8,128)(2,1)} custom-call(bf16[4,104,384]{2,1,0:T(8,128)(2,1)} %bitcast.23), custom_call_target="tpu_custom_call" | custom-call | tf_op jit(solution)/shard_map/feature_windows/pallas_call | solution.py:289
  1.8 6.9 %all-to-all-start = ((bf16[8,4,16,384]{3,2,1,0:T(8,128)(2,1)}), bf16[8,4,16,384]{3,2,1,0:T(8,128)(2,1)S(1)}, u32[]{:S(2)}, u32[]{:S(2)}) async-start(bf16[8,4,16,384]{3,2,1,0:T(8,128)(2,1)} %feature_windows.1), calls=%async_computation | async-start | bytes 786432 | tf_op jit(solution)/shard_map/all_to_all | solution.py:416
  8.6 0.1 pad_add_fusion.position.place_in_mesh
  8.7 2.1 %cache_windows.1 = (bf16[2,4,16,384]{3,2,1,0:T(8,128)(2,1)S(1)}, bf16[2,4,16,384]{3,2,1,0:T(8,128)(2,1)S(1)}) custom-call(s32[2]{0:T(128)S(1)} %pad_add_fusion.position.place_in_mesh, bf16[2,4,104,384]{3,2,1,0:T(8,128)(2,1)} %conv_cache.1, bf16[2,4,104,384]{3,2,1,0:T(8,128)(2,1)} %head_cache.1), custom_call_target="tpu_custom_call" | custom-call | tf_op jit(solution)/shard_map/cache_windows/pallas_call | solution.py:308
  10.9 4.6 %all-to-all-done.main = bf16[8,4,16,384]{3,2,1,0:T(8,128)(2,1)S(1)} async-done(((bf16[8,4,16,384]{3,2,1,0:T(8,128)(2,1)}), bf16[8,4,16,384]{3,2,1,0:T(8,128)(2,1)S(1)}, u32[]{:S(2)}, u32[]{:S(2)}) %all-to-all-start) | async-done | bytes 393248 | tf_op jit(solution)/shard_map/all_to_all | solution.py:416
  15.5 7.0 %collective-permute-start.1 = (bf16[10,16,384]{2,1,0:T(8,128)(2,1)S(1)}, bf16[10,16,384]{2,1,0:T(8,128)(2,1)S(1)}, u32[]{:S(2)}, u32[]{:S(2)}) collective-permute-start(bf16[10,16,384]{2,1,0:T(8,128)(2,1)S(1)} %pad_maximum_fusion.1), channel_id=1, source_target_pairs={{1,2},{3,4},{5,6},{7,8},{9,10},{11,12},{13,14},{2,1},{4,3},{6,5},{... | collective-permute-start | bytes 368648 | tf_op jit(solution)/shard_map/ppermute | solution.py:424
  22.6 0.1 collective-permute-start
  22.7 3.5 %weights_on_chip.1 = (bf16[3,3,3,384,384]{4,3,2,1,0:T(8,128)(2,1)S(1)}, bf16[1152,384]{1,0:T(8,128)(2,1)S(1)}, bf16[8,4,16,384]{3,2,1,0:T(8,128)(2,1)S(1)}) custom-call(bf16[8,4,16,384]{3,2,1,0:T(8,128)(2,1)S(1)} %all-to-all-done.main, bf16[3,3,3,384,384]{4,3,2,1,0:T(8,128)(2,1)} %weight.1, bf16[3,3,3,16,384]{4,3,2,1,0:T(8,128)(2,1)} %bitcast.22), custom_call_target="tpu_custom_call" | custom-call | tf_op jit(solution)/shard_map/weights_on_chip/pallas_call | solution.py:324
  26.2 0.0 copy-start
  26.2 0.0 collective-permute-done.1.far
  26.2 0.0 collective-permute-done.near
  26.2 7.5 %section.1 = bf16[8,16,16,128]{3,2,1,0:T(8,128)(2,1)} custom-call(s32[2]{0:T(128)S(1)} %pad_add_fusion.position.place_in_mesh, bf16[8,4,16,384]{3,2,1,0:T(8,128)(2,1)S(1)} %all-to-all-done.main, bf16[10,16,384]{2,1,0:T(8,128)(2,1)S(1)} %collective-permute-done.near, bf16[10,16,384]{2,1,0:T(8,128)(2,1)S(1)} %collective-permute-done.1.far, ...), custom_call_target="tpu_custom_call" | custom-call | tf_op jit(solution)/shard_map/section/pallas_call | solution.py:341
  33.7 7.4 %all-to-all-start.1 = ((bf16[128,16,128]{2,1,0:T(8,128)(2,1)}), bf16[128,16,128]{2,1,0:T(8,128)(2,1)S(1)}, u32[]{:S(2)}, u32[]{:S(2)}) async-start(bf16[128,16,128]{2,1,0:T(8,128)(2,1)} %bitcast.8), calls=%async_computation.1 | async-start | bytes 1048576 | tf_op jit(solution)/shard_map/all_to_all | solution.py:430
  41.1 0.0 copy-done
  41.1 7.5 %folded_weights.1 = (bf16[960,256]{1,0:T(8,128)(2,1)S(1)}, bf16[64,256]{1,0:T(8,128)(2,1)S(1)}) custom-call(bf16[2,2,16,5120]{3,2,1,0:T(8,128)(2,1)S(1)} %copy-done, bf16[960,5120]{1,0:T(8,128)(2,1)} %bitcast.21), custom_call_target="tpu_custom_call" | custom-call | tf_op jit(solution)/shard_map/folded_weights/pallas_call | solution.py:358
  48.7 6.0 %all-to-all-done.1 = bf16[128,16,128]{2,1,0:T(8,128)(2,1)S(1)} async-done(((bf16[128,16,128]{2,1,0:T(8,128)(2,1)}), bf16[128,16,128]{2,1,0:T(8,128)(2,1)S(1)}, u32[]{:S(2)}, u32[]{:S(2)}) %all-to-all-start.1) | async-done | bytes 524320 | tf_op jit(solution)/shard_map/all_to_all | solution.py:430
  54.7 3.2 %project.1 = bf16[960,1664]{1,0:T(8,128)(2,1)} custom-call(bf16[8,16,16,128]{3,2,1,0:T(8,128)(2,1)S(1)} %bitcast.20, bf16[960,256]{1,0:T(8,128)(2,1)S(1)} %get-tuple-element.17.folded, bf16[64,256]{1,0:T(8,128)(2,1)S(1)} %get-tuple-element.18.gram), custom_call_target="tpu_custom_call" | custom-call | tf_op jit(solution)/shard_map/project/pallas_call | solution.py:383
  (4 shorter events, 0.1 us)
Async XLA Ops:
  1.8 13.7 %all-to-all-start = ((bf16[8,4,16,384]{3,2,1,0:T(8,128)(2,1)}), bf16[8,4,16,384]{3,2,1,0:T(8,128)(2,1)S(1)}, u32[]{:S(2)}, u32[]{:S(2)}) async-start(bf16[8,4,16,384]{3,2,1,0:T(8,128)(2,1)} %feature_windows.1), calls=%async_computation | async-start | bytes 786432 | tf_op jit(solution)/shard_map/all_to_all | solution.py:416
  15.5 10.7 %collective-permute-start.1 = (bf16[10,16,384]{2,1,0:T(8,128)(2,1)S(1)}, bf16[10,16,384]{2,1,0:T(8,128)(2,1)S(1)}, u32[]{:S(2)}, u32[]{:S(2)}) collective-permute-start(bf16[10,16,384]{2,1,0:T(8,128)(2,1)S(1)} %pad_maximum_fusion.1), channel_id=1, source_target_pairs={{1,2},{3,4},{5,6},{7,8},{9,10},{11,12},{13,14},{2,1},{4,3},{6,5},{... | collective-permute-start | bytes 368648 | tf_op jit(solution)/shard_map/ppermute | solution.py:424
  22.6 3.6 %collective-permute-start = (bf16[10,16,384]{2,1,0:T(8,128)(2,1)S(1)}, bf16[10,16,384]{2,1,0:T(8,128)(2,1)S(1)}, u32[]{:S(2)}, u32[]{:S(2)}) collective-permute-start(bf16[10,16,384]{2,1,0:T(8,128)(2,1)S(1)} %pad_maximum_fusion), channel_id=1, source_target_pairs={{0,1},{2,3},{4,5},{6,7},{8,9},{10,11},{12,13},{14,15},{1,0},{3,2},... | collective-permute-start | bytes 368648 | tf_op jit(solution)/shard_map/ppermute | solution.py:425
  26.2 15.0 %copy-start = (bf16[2,2,16,5120]{3,2,1,0:T(8,128)(2,1)S(1)}, bf16[2,2,16,5120]{3,2,1,0:T(8,128)(2,1)}, u32[]{:S(2)}) copy-start(bf16[2,2,16,5120]{3,2,1,0:T(8,128)(2,1)} %patch.1) | copy-start | bytes 1966084
  33.7 21.0 %all-to-all-start.1 = ((bf16[128,16,128]{2,1,0:T(8,128)(2,1)}), bf16[128,16,128]{2,1,0:T(8,128)(2,1)S(1)}, u32[]{:S(2)}, u32[]{:S(2)}) async-start(bf16[128,16,128]{2,1,0:T(8,128)(2,1)} %bitcast.8), calls=%async_computation.1 | async-start | bytes 1048576 | tf_op jit(solution)/shard_map/all_to_all | solution.py:430

commit v5 on v4

--- a/solution.py
+++ b/solution.py
@@ -11,6 +11,7 @@
 BF16 = jnp.bfloat16
 EPS = 1e-06
 STEP = 14
+EARLY = 2
 WIN = 16
 
 
@@ -67,11 +68,14 @@
         copy.wait()
 
 
-def cache_windows_kernel(position, conv_cache, head_cache, conv_win, head_win, conv_in, head_in, sems):
+def cache_windows_kernel(
+    position, conv_cache, head_cache, weight, conv_win, head_win, early, conv_in, head_in, sems
+):
     frames, rows, cols, _ = conv_cache.shape
     copies = [
         pltpu.make_async_copy(conv_cache, conv_in, sems.at[0]),
         pltpu.make_async_copy(head_cache, head_in, sems.at[1]),
+        pltpu.make_async_copy(weight.at[pl.ds(0, early.shape[0])], early, sems.at[2]),
     ]
     for copy in copies:
         copy.start()
@@ -90,86 +94,126 @@
                 out[frame, row] = jnp.dot(
                     pick, source[frame, row], preferred_element_type=F32
                 ).astype(BF16)
-
-
-def weights_kernel(main, weight, head, weight_out, head_rows, normed, head_in, sems):
+    copies[2].wait()
+
+
+def after_block(sums, features, place_in_mesh, cols):
+    count, width = features.shape
+    update = (
+        sums[:, :width]
+        + pltpu.roll(sums[:, width : 2 * width], count - 1, 0)
+        + pltpu.roll(sums[:, 2 * width :], count - 2, 0)
+    )
+    residual = (pltpu.roll(features, count - 1, 0) + update).astype(BF16).astype(F32)
+    place = iota((count, 1), 0) % WIN
+    inside = (place < STEP) & (STEP * place_in_mesh[0] + place < cols)
+    return jnp.where(inside, rms_silu(residual), 0.0).astype(BF16)
+
+
+def column_taps(weights):
+    return jnp.concatenate(
+        [jnp.concatenate([weight[c] for c in range(weight.shape[0])], axis=1) for weight in weights],
+        axis=0,
+    )
+
+
+def inner_kernel(
+    cols, place_in_mesh, main, conv_win, early, weight, head, late, head_rows, normed, inner, head_in, sems
+):
+    frames, rows, win, width = main.shape
     depth = head.shape[3]
-    copies = [pltpu.make_async_copy(head, head_in, sems.at[3])]
-    copies += [pltpu.make_async_copy(weight.at[a], weight_out.at[a], sems.at[a]) for a in range(3)]
+    head_copy = pltpu.make_async_copy(head, head_in, sems.at[late.shape[0]])
+    copies = [
+        pltpu.make_async_copy(weight.at[EARLY + i], late.at[i], sems.at[i])
+        for i in range(late.shape[0])
+    ]
+    head_copy.start()
     for copy in copies:
         copy.start()
+    normed[0:2] = conv_win[...]
+    normed[2:] = rms_silu(main[...].astype(F32)).astype(BF16)
     head_rows[...] = jnp.zeros_like(head_rows)
-    normed[...] = rms_silu(main[...].astype(F32)).astype(BF16)
-    copies[0].wait()
+    head_copy.wait()
     for a in range(3):
         for b in range(3):
             for c in range(3):
-                start = (3 * a + c) * 128 + (2 - b) * depth
+                slot = 2 * a + c if c < 2 else 6 + a
+                start = slot * 64 + (2 - b) * depth
                 head_rows[start : start + depth] = head_in[a, b, c]
-    for copy in copies[1:]:
-        copy.wait()
+    count = frames * (rows - 2) * win
+    sums = None
+    for pairs in (range(0, EARLY), range(EARLY, 5), range(5, 8), range(8, 9)):
+        left = jnp.concatenate(
+            [
+                normed[pair // 3 : pair // 3 + frames, pair % 3 : pair % 3 + rows - 2].reshape(
+                    count, width
+                )
+                for pair in pairs
+            ],
+            axis=1,
+        )
+        weights = []
+        for pair in pairs:
+            if pair < EARLY:
+                weights.append(early[pair])
+            else:
+                copies[pair - EARLY].wait()
+                weights.append(late[pair - EARLY])
+        product = jnp.dot(left, column_taps(weights), preferred_element_type=F32)
+        sums = product if sums is None else sums + product
+    own = main[:, 1 : rows - 1].astype(F32).reshape(count, width)
+    inner[...] = after_block(sums, own, place_in_mesh, cols).reshape(inner.shape)
 
 
 def section_kernel(
-    cols, depth, place_in_mesh, main, near, far, conv_win, head_win, weight, head_rows, ready, out, normed, hidden
+    cols, depth, place_in_mesh, main, near, far, head_win, early, late, head_rows, normed, inner, out, edges, hidden, pieces, sems
 ):
     frames, rows, win, width = main.shape
     count = frames * rows * win
-    normed[0:2, 1 : rows + 1] = conv_win[...]
-    normed[2:, 1 : rows + 1] = ready[...]
     odd = place_in_mesh[1] % 2 == 1
-    for edge, when_odd, when_even in ((0, near, far), (rows + 1, far, near)):
-        cached = jnp.where(odd, when_odd[0:2], when_even[0:2])
+    for edge, when_odd, when_even in ((0, near, far), (1, far, near)):
+        edges[edge, 0:2] = jnp.where(odd, when_odd[0:2], when_even[0:2])
         values = jnp.where(odd, when_odd[2:].astype(F32), when_even[2:].astype(F32))
-        normed[0:2, edge] = cached
-        normed[2:, edge] = rms_silu(values).astype(BF16)
-    before = 2 * rows * win
-    hidden[0:before] = head_win[...].reshape(before, width)
-
-    together = 4
-    chunk = together * rows * win
-    place = iota((chunk, 1), 0) % win
-    inside = (place < STEP) & (STEP * place_in_mesh[0] + place < cols)
-    for first in range(0, frames, together):
-        left = jnp.concatenate(
-            [
-                normed[first + a : first + a + together, b : b + rows].reshape(chunk, width)
-                for a in range(3)
-                for b in range(3)
-            ],
-            axis=1,
-        )
-        right = jnp.concatenate(
-            [weight[:, :, c].reshape(9 * width, width) for c in range(3)], axis=1
-        )
-        sums = jnp.dot(left, right, preferred_element_type=F32)
-        update = (
-            sums[:, :width]
-            + pltpu.roll(sums[:, width : 2 * width], chunk - 1, 0)
-            + pltpu.roll(sums[:, 2 * width :], chunk - 2, 0)
-        )
-        own = main[first : first + together].astype(F32).reshape(chunk, width)
-        residual = (pltpu.roll(own, chunk - 1, 0) + update).astype(BF16).astype(F32)
-        start = before + first * rows * win
-        hidden[start : start + chunk] = jnp.where(inside, rms_silu(residual), 0.0).astype(BF16)
-
-    taps = rows_times_rows(hidden[...], head_rows[...])
-    shifted = []
-    for c in range(3):
-        total = jnp.zeros((count, 128), F32)
-        for a in range(3):
-            total += taps[
-                a * rows * win : a * rows * win + count, (3 * a + c) * 128 : (3 * a + c + 1) * 128
-            ]
-        shifted.append(total if c == 2 else pltpu.roll(total, 2 - c, 0))
-    total = (shifted[0] + shifted[1] + shifted[2]).reshape(frames, rows, win, 128)
+        edges[edge, 2:] = rms_silu(values).astype(BF16)
+    hidden[0:2] = head_win[...]
+    hidden[2:, 1 : rows - 1] = inner[...]
+
+    def both(first, second):
+        return jnp.concatenate([first[:, None], second[:, None]], axis=1).reshape(-1, width)
+
+    columns = []
+    for a in range(3):
+        part = slice(a, a + frames)
+        columns.append(both(edges[0, part], normed[part, rows - 2]))
+        columns.append(both(normed[part, 0], normed[part, rows - 1]))
+        columns.append(both(normed[part, 1], edges[1, part]))
+    left = jnp.concatenate(columns, axis=1)
+    weights = [early[i] for i in range(EARLY)] + [late[i] for i in range(late.shape[0])]
+    sums = jnp.dot(left, column_taps(weights), preferred_element_type=F32)
+    own = both(main[:, 0].astype(F32), main[:, rows - 1].astype(F32))
+    outer = after_block(sums, own, place_in_mesh, cols).reshape(frames, 2, win, width)
+    hidden[2:, 0] = outer[:, 0]
+    hidden[2:, rows - 1] = outer[:, 1]
+
+    before = rows * win
+    taps = rows_times_rows(hidden[...].reshape(count + 2 * before, width), head_rows[...])
+    pair = sum(taps[a * before : a * before + count, a * 128 : (a + 1) * 128] for a in range(3))
+    last = taps[0:count, 384:512] + pltpu.roll(taps[before : before + count, 384:512], 64, 1)
+    last += taps[2 * before : 2 * before + count, 512:576 + 64]
+    total = pltpu.roll(pair, 2, 0) + pltpu.roll(pltpu.roll(pair, 64, 1), 1, 0) + last
+    total = jnp.where(iota((1, 128), 1) < 64, total, 0.0).reshape(frames, rows, win, 128)
+    copies = []
     for frame in range(frames):
         piece = total[frame, 0]
         for row in range(1, rows):
             piece += pltpu.roll(total[frame, row], depth * row, 1)
         piece = piece.astype(BF16)
         for target in range(out.shape[1]):
-            out[frame, target] = piece
+            pieces[frame, target] = piece
+        copies.append(pltpu.make_async_copy(pieces.at[frame], out.at[frame], sems.at[frame]))
+        copies[-1].start()
+    for copy in copies:
+        copy.wait()
 
 
 def folded_kernel(patch, qkv, folded, gram, parts, qkv_in, sems):
@@ -302,54 +346,59 @@
     )(in_hbm(features))
 
 
-def cache_windows(position, conv_cache, head_cache):
+def cache_windows(position, conv_cache, head_cache, weight):
     frames, rows, cols, width = conv_cache.shape
     window = pltpu.VMEM((frames, rows, WIN, width), BF16)
     return pl.pallas_call(
         cache_windows_kernel,
-        in_specs=[SCALAR, IN_HBM, IN_HBM],
-        out_specs=[ON_CHIP] * 2,
-        out_shape=[window, window],
+        in_specs=[SCALAR, IN_HBM, IN_HBM, IN_HBM],
+        out_specs=[ON_CHIP] * 3,
+        out_shape=[window, window, pltpu.VMEM((EARLY,) + weight.shape[1:], BF16)],
         scratch_shapes=[
             pltpu.VMEM(conv_cache.shape, BF16),
             pltpu.VMEM(head_cache.shape, BF16),
-            pltpu.SemaphoreType.DMA((2,)),
+            pltpu.SemaphoreType.DMA((3,)),
         ],
         compiler_params=params(8),
         name="cache_windows",
-    )(position, in_hbm(conv_cache), in_hbm(head_cache))
-
-
-def weights_on_chip(main, weight, head):
+    )(position, in_hbm(conv_cache), in_hbm(head_cache), in_hbm(weight))
+
+
+def inner_rows(place_in_mesh, main, conv_win, early, weight, head, cols):
+    frames, rows, win, width = main.shape
+    late = (weight.shape[0] - EARLY,) + weight.shape[1:]
     return pl.pallas_call(
-        weights_kernel,
-        in_specs=[ON_CHIP, IN_HBM, IN_HBM],
-        out_specs=[ON_CHIP] * 3,
+        functools.partial(inner_kernel, cols),
+        in_specs=[SCALAR] + [ON_CHIP] * 3 + [IN_HBM] * 2,
+        out_specs=[ON_CHIP] * 4,
         out_shape=[
-            pltpu.VMEM(weight.shape, BF16),
-            pltpu.VMEM((9 * 128, weight.shape[3]), BF16),
-            pltpu.VMEM(main.shape, BF16),
-        ],
-        scratch_shapes=[pltpu.VMEM(head.shape, BF16), pltpu.SemaphoreType.DMA((4,))],
-        compiler_params=params(8),
-        name="weights_on_chip",
-    )(main, in_hbm(weight), in_hbm(head))
-
-
-def section(place_in_mesh, main, near, far, conv_win, head_win, weight, head_rows, ready, cols, depth, blocks):
+            pltpu.VMEM(late, BF16),
+            pltpu.VMEM((10 * 64, width), BF16),
+            pltpu.VMEM((frames + 2, rows, win, width), BF16),
+            pltpu.VMEM((frames, rows - 2, win, width), BF16),
+        ],
+        scratch_shapes=[pltpu.VMEM(head.shape, BF16), pltpu.SemaphoreType.DMA((late[0] + 1,))],
+        compiler_params=params(20),
+        name="inner_rows",
+    )(place_in_mesh, main, conv_win, early, in_hbm(weight), in_hbm(head))
+
+
+def section(place_in_mesh, main, near, far, head_win, early, prepared, cols, depth, blocks):
     frames, rows, win, width = main.shape
     return pl.pallas_call(
         functools.partial(section_kernel, cols, depth),
-        in_specs=[SCALAR] + [ON_CHIP] * 8,
-        out_specs=ON_CHIP,
-        out_shape=pltpu.VMEM((frames, blocks, win, 128), BF16),
+        in_specs=[SCALAR] + [ON_CHIP] * 9,
+        out_specs=IN_HBM,
+        out_shape=pltpu.HBM((frames, blocks, win, 128), BF16),
         scratch_shapes=[
-            pltpu.VMEM((frames + 2, rows + 2, win, width), BF16),
-            pltpu.VMEM(((frames + 2) * rows * win, width), BF16),
+            pltpu.VMEM((2, frames + 2, win, width), BF16),
+            pltpu.VMEM((frames + 2, rows, win, width), BF16),
+            pltpu.VMEM((frames, blocks, win, 128), BF16),
+            pltpu.SemaphoreType.DMA((frames,)),
         ],
         compiler_params=params(20),
         name="section",
-    )(place_in_mesh, main, near, far, conv_win, head_win, weight, head_rows, ready)
+    )(place_in_mesh, main, near, far, head_win, early, *prepared)
 
 
 def folded_weights(patch, qkv):
@@ -414,7 +463,8 @@
     flat_qkv = qkv_weight.transpose(1, 2, 0).reshape(3 * local_cols, qkv_weight.shape[0])
 
     main = lax.all_to_all(feature_windows(features[0], groups), "tm", 0, 0, tiled=True)
-    conv_win, head_win = cache_windows(place_in_mesh, conv_cache, head_cache)
+    pairs = conv_weight.reshape((9,) + conv_weight.shape[2:])
+    conv_win, head_win, early = cache_windows(place_in_mesh, conv_cache, head_cache, pairs)
     def edge(row):
         return jnp.concatenate(
             [lax.dynamic_index_in_dim(part, row, 1, False) for part in (conv_win, main)]
@@ -423,9 +473,9 @@
     odd = block % 2
     far = lax.ppermute(edge((rows - 1) * odd), "rows", swaps(blocks, 1))
     near = lax.ppermute(edge((rows - 1) * (1 - odd)), "rows", swaps(blocks, 0))
-    weight, head_rows, ready = weights_on_chip(main, conv_weight, head)
+    prepared = inner_rows(place_in_mesh, main, conv_win, early, pairs, head, cols)
     partial = section(
-        place_in_mesh, main, near, far, conv_win, head_win, weight, head_rows, ready, cols, depth, blocks
+        place_in_mesh, main, near, far, head_win, early, prepared, cols, depth, blocks
     )
     pieces = lax.all_to_all(
         partial.reshape(groups * blocks, WIN, 128), ("tm", "rows"), 0, 0, tiled=True

time: 58.4 us -> 56.7 us (0.971)
  starting transfers between devices: 21.4 us -> 19.9 us
    pallas_call x2, Pallas kernels: 5.6 us -> 8.38 us  [the longest x1 5.94 us: inner_rows(): pl.pallas_call(functools.partial(inner_kernel, cols), in_specs=[SCALAR] +...]
    pallas_call x1, Pallas kernels: 7.5 us -> 4.8 us  [section(): pl.pallas_call(functools.partial(section_kernel, cols, depth), in_specs=[...]
    all_to_all x1, starting transfers between devices: 7.43 us -> 5.91 us  [local(): lax.all_to_all(partial.reshape(groups * blocks, WIN, 128), ('tm', 'rows')...]
  transfers between devices with their start and end apart: 4 -> 4, of which waited for: 2 -> 2; matrix products, arithmetic and copies ran while one was open for 0% -> 0% of each run, Pallas kernels for 23% -> 28%
where the time goes in v5:
time: 56.7 us; the launch traced here: 56.3 us
  Pallas kernels  25.7 us (45%)
  starting transfers between devices  19.9 us (35%)
  waiting for transfers between devices  10.3 us (18%)
    pallas_call x1, Pallas kernels, folded_weights(): pl.pallas_call(folded_kernel, in_specs=[ON_CHIP, IN_HBM], out_specs=[ON_C...  7.53 us
    ppermute x1, starting transfers between devices, local(): far = lax.ppermute(edge((rows - 1) * odd), 'rows', swaps(blocks, 1))  7.03 us
    all_to_all x1, starting transfers between devices, local(): lax.all_to_all(feature_windows(features[0], groups), 'tm', 0, 0, tiled=True)  6.89 us
    all_to_all x1, waiting for transfers between devices, local(): lax.all_to_all(partial.reshape(groups * blocks, WIN, 128), ('tm', 'rows')...  6.04 us
    pallas_call x1, Pallas kernels, inner_rows(): pl.pallas_call(functools.partial(inner_kernel, cols), in_specs=[SCALAR] +...  5.94 us
    all_to_all x1, starting transfers between devices, local(): lax.all_to_all(partial.reshape(groups * blocks, WIN, 128), ('tm', 'rows')...  5.91 us
    pallas_call x1, Pallas kernels, section(): pl.pallas_call(functools.partial(section_kernel, cols, depth), in_specs=[...  4.8 us
    all_to_all x1, waiting for transfers between devices, local(): lax.all_to_all(feature_windows(features[0], groups), 'tm', 0, 0, tiled=True)  4.26 us
  transfers between devices with their start and end apart: 4, of which 2 were waited for; matrix products, arithmetic and copies ran while one was open for 0% of the time, Pallas kernels for 28%

profile of v5, /device:TPU:1, one launch (start us, length us, event | category | flops | bytes accessed | tf_op | source)
XLA Modules:
  0.0 56.3 jit_solution(12919189826985225999)
XLA Ops:
  0.0 1.7 %feature_windows.1 = bf16[8,4,16,384]{3,2,1,0:T(8,128)(2,1)} custom-call(bf16[4,104,384]{2,1,0:T(8,128)(2,1)} %bitcast.27), custom_call_target="tpu_custom_call" | custom-call | tf_op jit(solution)/shard_map/feature_windows/pallas_call | solution.py:333
  1.8 6.9 %all-to-all-start = ((bf16[8,4,16,384]{3,2,1,0:T(8,128)(2,1)}), bf16[8,4,16,384]{3,2,1,0:T(8,128)(2,1)S(1)}, u32[]{:S(2)}, u32[]{:S(2)}) async-start(bf16[8,4,16,384]{3,2,1,0:T(8,128)(2,1)} %feature_windows.1), calls=%async_computation | async-start | bytes 786432 | tf_op jit(solution)/shard_map/all_to_all | solution.py:465
  8.6 0.1 pad_add_fusion.position.place_in_mesh
  8.7 2.4 %cache_windows.1 = (bf16[2,4,16,384]{3,2,1,0:T(8,128)(2,1)S(1)}, bf16[2,4,16,384]{3,2,1,0:T(8,128)(2,1)S(1)}, bf16[2,3,384,384]{3,2,1,0:T(8,128)(2,1)S(1)}) custom-call(s32[2]{0:T(128)S(1)} %pad_add_fusion.position.place_in_mesh, bf16[2,4,104,384]{3,2,1,0:T(8,128)(2,1)} %conv_cache.1, bf16[2,4,104,384]{3,2,1,0:T(8,128)(2,1)} %head_cache.1, ...), custom_call_target="tpu_custom_call" | custom-call | tf_op jit(solution)/shard_map/cache_windows/pallas_call | solution.py:352
  11.2 4.3 %all-to-all-done.main = bf16[8,4,16,384]{3,2,1,0:T(8,128)(2,1)S(1)} async-done(((bf16[8,4,16,384]{3,2,1,0:T(8,128)(2,1)}), bf16[8,4,16,384]{3,2,1,0:T(8,128)(2,1)S(1)}, u32[]{:S(2)}, u32[]{:S(2)}) %all-to-all-start) | async-done | bytes 393248 | tf_op jit(solution)/shard_map/all_to_all | solution.py:465
  15.5 7.0 %collective-permute-start.1 = (bf16[10,16,384]{2,1,0:T(8,128)(2,1)S(1)}, bf16[10,16,384]{2,1,0:T(8,128)(2,1)S(1)}, u32[]{:S(2)}, u32[]{:S(2)}) collective-permute-start(bf16[10,16,384]{2,1,0:T(8,128)(2,1)S(1)} %pad_maximum_fusion.1), channel_id=1, source_target_pairs={{1,2},{3,4},{5,6},{7,8},{9,10},{11,12},{13,14},{2,1},{4,3},{6,5},{... | collective-permute-start | bytes 368648 | tf_op jit(solution)/shard_map/ppermute | solution.py:474
  22.6 0.1 collective-permute-start
  22.7 5.9 %inner_rows.1 = (bf16[7,3,384,384]{3,2,1,0:T(8,128)(2,1)S(1)}, bf16[640,384]{1,0:T(8,128)(2,1)S(1)}, bf16[10,4,16,384]{3,2,1,0:T(8,128)(2,1)S(1)}, bf16[8,2,16,384]{3,2,1,0:T(8,128)(2,1)S(1)}) custom-call(s32[2]{0:T(128)S(1)} %pad_add_fusion.position.place_in_mesh, bf16[8,4,16,384]{3,2,1,0:T(8,128)(2,1)S(1)} %all-to-all-done.main, ...), custom_call_target="tpu_custom_call" | custom-call | tf_op jit(solution)/shard_map/inner_rows/pallas_call | solution.py:370
  28.6 0.0 copy-start
  28.6 0.0 collective-permute-done.1.far
  28.6 0.0 collective-permute-done.near
  28.6 4.8 %section.1 = bf16[8,16,16,128]{3,2,1,0:T(8,128)(2,1)} custom-call(s32[2]{0:T(128)S(1)} %pad_add_fusion.position.place_in_mesh, bf16[8,4,16,384]{3,2,1,0:T(8,128)(2,1)S(1)} %all-to-all-done.main, bf16[10,16,384]{2,1,0:T(8,128)(2,1)S(1)} %collective-permute-done.near, bf16[10,16,384]{2,1,0:T(8,128)(2,1)S(1)} %collective-permute-done.1.far, ...), custom_call_target="tpu_custom_call" | custom-call | tf_op jit(solution)/shard_map/section/pallas_call | solution.py:388
  33.4 5.9 %all-to-all-start.1 = ((bf16[128,16,128]{2,1,0:T(8,128)(2,1)}), bf16[128,16,128]{2,1,0:T(8,128)(2,1)S(1)}, u32[]{:S(2)}, u32[]{:S(2)}) async-start(bf16[128,16,128]{2,1,0:T(8,128)(2,1)} %bitcast.25), calls=%async_computation.1 | async-start | bytes 1048576 | tf_op jit(solution)/shard_map/all_to_all | solution.py:480
  39.4 0.0 copy-done
  39.4 7.5 %folded_weights.1 = (bf16[960,256]{1,0:T(8,128)(2,1)S(1)}, bf16[64,256]{1,0:T(8,128)(2,1)S(1)}) custom-call(bf16[2,2,16,5120]{3,2,1,0:T(8,128)(2,1)S(1)} %copy-done, bf16[960,5120]{1,0:T(8,128)(2,1)} %bitcast.24), custom_call_target="tpu_custom_call" | custom-call | tf_op jit(solution)/shard_map/folded_weights/pallas_call | solution.py:407
  46.9 6.0 %all-to-all-done.1 = bf16[128,16,128]{2,1,0:T(8,128)(2,1)S(1)} async-done(((bf16[128,16,128]{2,1,0:T(8,128)(2,1)}), bf16[128,16,128]{2,1,0:T(8,128)(2,1)S(1)}, u32[]{:S(2)}, u32[]{:S(2)}) %all-to-all-start.1) | async-done | bytes 524320 | tf_op jit(solution)/shard_map/all_to_all | solution.py:480
  53.0 3.2 %project.1 = bf16[960,1664]{1,0:T(8,128)(2,1)} custom-call(bf16[8,16,16,128]{3,2,1,0:T(8,128)(2,1)S(1)} %bitcast.21, bf16[960,256]{1,0:T(8,128)(2,1)S(1)} %get-tuple-element.21.folded, bf16[64,256]{1,0:T(8,128)(2,1)S(1)} %get-tuple-element.22.gram), custom_call_target="tpu_custom_call" | custom-call | tf_op jit(solution)/shard_map/project/pallas_call | solution.py:432
  (4 shorter events, 0.1 us)
Async XLA Ops:
  1.8 13.7 %all-to-all-start = ((bf16[8,4,16,384]{3,2,1,0:T(8,128)(2,1)}), bf16[8,4,16,384]{3,2,1,0:T(8,128)(2,1)S(1)}, u32[]{:S(2)}, u32[]{:S(2)}) async-start(bf16[8,4,16,384]{3,2,1,0:T(8,128)(2,1)} %feature_windows.1), calls=%async_computation | async-start | bytes 786432 | tf_op jit(solution)/shard_map/all_to_all | solution.py:465
  15.5 13.1 %collective-permute-start.1 = (bf16[10,16,384]{2,1,0:T(8,128)(2,1)S(1)}, bf16[10,16,384]{2,1,0:T(8,128)(2,1)S(1)}, u32[]{:S(2)}, u32[]{:S(2)}) collective-permute-start(bf16[10,16,384]{2,1,0:T(8,128)(2,1)S(1)} %pad_maximum_fusion.1), channel_id=1, source_target_pairs={{1,2},{3,4},{5,6},{7,8},{9,10},{11,12},{13,14},{2,1},{4,3},{6,5},{... | collective-permute-start | bytes 368648 | tf_op jit(solution)/shard_map/ppermute | solution.py:474
  22.6 6.1 %collective-permute-start = (bf16[10,16,384]{2,1,0:T(8,128)(2,1)S(1)}, bf16[10,16,384]{2,1,0:T(8,128)(2,1)S(1)}, u32[]{:S(2)}, u32[]{:S(2)}) collective-permute-start(bf16[10,16,384]{2,1,0:T(8,128)(2,1)S(1)} %pad_maximum_fusion), channel_id=1, source_target_pairs={{0,1},{2,3},{4,5},{6,7},{8,9},{10,11},{12,13},{14,15},{1,0},{3,2},... | collective-permute-start | bytes 368648 | tf_op jit(solution)/shard_map/ppermute | solution.py:475
  28.6 10.8 %copy-start = (bf16[2,2,16,5120]{3,2,1,0:T(8,128)(2,1)S(1)}, bf16[2,2,16,5120]{3,2,1,0:T(8,128)(2,1)}, u32[]{:S(2)}) copy-start(bf16[2,2,16,5120]{3,2,1,0:T(8,128)(2,1)} %patch.1) | copy-start | bytes 1966084
  33.4 19.5 %all-to-all-start.1 = ((bf16[128,16,128]{2,1,0:T(8,128)(2,1)}), bf16[128,16,128]{2,1,0:T(8,128)(2,1)S(1)}, u32[]{:S(2)}, u32[]{:S(2)}) async-start(bf16[128,16,128]{2,1,0:T(8,128)(2,1)} %bitcast.25), calls=%async_computation.1 | async-start | bytes 1048576 | tf_op jit(solution)/shard_map/all_to_all | solution.py:480

commit v6 on v5

--- a/solution.py
+++ b/solution.py
@@ -11,7 +11,7 @@
 BF16 = jnp.bfloat16
 EPS = 1e-06
 STEP = 14
-EARLY = 2
+EARLY = 1
 WIN = 16
 
 
@@ -112,27 +112,67 @@
 
 def column_taps(weights):
     return jnp.concatenate(
-        [jnp.concatenate([weight[c] for c in range(weight.shape[0])], axis=1) for weight in weights],
+        [
+            jnp.concatenate([weight[b, c] for c in range(weight.shape[1])], axis=1)
+            for weight in weights
+            for b in range(weight.shape[0])
+        ],
         axis=0,
     )
 
 
 def inner_kernel(
-    cols, place_in_mesh, main, conv_win, early, weight, head, late, head_rows, normed, inner, head_in, sems
+    cols,
+    place_in_mesh,
+    main,
+    conv_win,
+    early,
+    weight,
+    head,
+    late,
+    head_rows,
+    normed,
+    inner,
+    head_in,
+    sums,
+    sems,
 ):
     frames, rows, win, width = main.shape
     depth = head.shape[3]
-    head_copy = pltpu.make_async_copy(head, head_in, sems.at[late.shape[0]])
-    copies = [
-        pltpu.make_async_copy(weight.at[EARLY + i], late.at[i], sems.at[i])
-        for i in range(late.shape[0])
-    ]
+    taps = late.shape[0]
+
+    def arriving(i):
+        return pltpu.make_async_copy(weight.at[EARLY + i], late.at[i], sems.at[i])
+
+    for i in range(taps):
+        arriving(i).start()
+    head_copy = pltpu.make_async_copy(head, head_in, sems.at[taps])
     head_copy.start()
-    for copy in copies:
-        copy.start()
     normed[0:2] = conv_win[...]
     normed[2:] = rms_silu(main[...].astype(F32)).astype(BF16)
     head_rows[...] = jnp.zeros_like(head_rows)
+    count = frames * (rows - 2) * win
+
+    def product(a, weights):
+        left = jnp.concatenate(
+            [
+                normed[pl.ds(a, frames), b : b + rows - 2].reshape(count, width)
+                for b in range(3)
+            ],
+            axis=1,
+        )
+        return jnp.dot(left, column_taps([weights]), preferred_element_type=F32)
+
+    sums[...] = product(0, early[0])
+
+    def step(i, carry):
+        arriving(i).wait()
+        sums[...] += product(EARLY + i, late[i])
+        return carry
+
+    lax.fori_loop(0, taps, step, 0)
+    own = main[:, 1 : rows - 1].astype(F32).reshape(count, width)
+    inner[...] = after_block(sums[...], own, place_in_mesh, cols).reshape(inner.shape)
     head_copy.wait()
     for a in range(3):
         for b in range(3):
@@ -140,29 +180,6 @@
                 slot = 2 * a + c if c < 2 else 6 + a
                 start = slot * 64 + (2 - b) * depth
                 head_rows[start : start + depth] = head_in[a, b, c]
-    count = frames * (rows - 2) * win
-    sums = None
-    for pairs in (range(0, EARLY), range(EARLY, 5), range(5, 8), range(8, 9)):
-        left = jnp.concatenate(
-            [
-                normed[pair // 3 : pair // 3 + frames, pair % 3 : pair % 3 + rows - 2].reshape(
-                    count, width
-                )
-                for pair in pairs
-            ],
-            axis=1,
-        )
-        weights = []
-        for pair in pairs:
-            if pair < EARLY:
-                weights.append(early[pair])
-            else:
-                copies[pair - EARLY].wait()
-                weights.append(late[pair - EARLY])
-        product = jnp.dot(left, column_taps(weights), preferred_element_type=F32)
-        sums = product if sums is None else sums + product
-    own = main[:, 1 : rows - 1].astype(F32).reshape(count, width)
-    inner[...] = after_block(sums, own, place_in_mesh, cols).reshape(inner.shape)
 
 
 def section_kernel(
@@ -377,7 +394,11 @@
             pltpu.VMEM((frames + 2, rows, win, width), BF16),
             pltpu.VMEM((frames, rows - 2, win, width), BF16),
         ],
-        scratch_shapes=[pltpu.VMEM(head.shape, BF16), pltpu.SemaphoreType.DMA((late[0] + 1,))],
+        scratch_shapes=[
+            pltpu.VMEM(head.shape, BF16),
+            pltpu.VMEM((frames * (rows - 2) * win, 3 * width), F32),
+            pltpu.SemaphoreType.DMA((late[0] + 1,)),
+        ],
         compiler_params=params(20),
         name="inner_rows",
     )(place_in_mesh, main, conv_win, early, in_hbm(weight), in_hbm(head))
@@ -463,8 +484,7 @@
     flat_qkv = qkv_weight.transpose(1, 2, 0).reshape(3 * local_cols, qkv_weight.shape[0])
 
     main = lax.all_to_all(feature_windows(features[0], groups), "tm", 0, 0, tiled=True)
-    pairs = conv_weight.reshape((9,) + conv_weight.shape[2:])
-    conv_win, head_win, early = cache_windows(place_in_mesh, conv_cache, head_cache, pairs)
+    conv_win, head_win, early = cache_windows(place_in_mesh, conv_cache, head_cache, conv_weight)
     def edge(row):
         return jnp.concatenate(
             [lax.dynamic_index_in_dim(part, row, 1, False) for part in (conv_win, main)]
@@ -473,7 +493,7 @@
     odd = block % 2
     far = lax.ppermute(edge((rows - 1) * odd), "rows", swaps(blocks, 1))
     near = lax.ppermute(edge((rows - 1) * (1 - odd)), "rows", swaps(blocks, 0))
-    prepared = inner_rows(place_in_mesh, main, conv_win, early, pairs, head, cols)
+    prepared = inner_rows(place_in_mesh, main, conv_win, early, conv_weight, head, cols)
     partial = section(
         place_in_mesh, main, near, far, head_win, early, prepared, cols, depth, blocks
     )

time: 56.7 us -> 55.8 us (0.984)
  waiting for transfers between devices: 10.3 us -> 8.96 us
  local copies, waits for them, and re-layouts: 0.04 us -> 1.12 us
  Pallas kernels: 25.7 us -> 24.7 us
    pallas_call x1, Pallas kernels: 5.94 us -> 4.68 us  [inner_rows(): pl.pallas_call(functools.partial(inner_kernel, cols), in_specs=[SCALAR] +...]
    unnamed x2, local copies, waits for them, and re-layouts: 0.01 us -> 1.08 us
    all_to_all x1, waiting for transfers between devices: 6.04 us -> 4.97 us  [local(): lax.all_to_all(partial.reshape(groups * blocks, WIN, 128), ('tm', 'rows')...]
  transfers between devices with their start and end apart: 4 -> 4, of which waited for: 2 -> 2; matrix products, arithmetic and copies ran while one was open for 0% -> 0% of each run, Pallas kernels for 28% -> 27%
where the time goes in v6:
time: 55.8 us; the launch traced here: 55.4 us
  Pallas kernels  24.7 us (44%)
  starting transfers between devices  20.3 us (36%)
  waiting for transfers between devices  8.96 us (16%)
  local copies, waits for them, and re-layouts  1.12 us (2%)
    pallas_call x1, Pallas kernels, folded_weights(): pl.pallas_call(folded_kernel, in_specs=[ON_CHIP, IN_HBM], out_specs=[ON_C...  7.52 us
    ppermute x1, starting transfers between devices, local(): far = lax.ppermute(edge((rows - 1) * odd), 'rows', swaps(blocks, 1))  7.03 us
    all_to_all x1, starting transfers between devices, local(): lax.all_to_all(feature_windows(features[0], groups), 'tm', 0, 0, tiled=True)  6.89 us
    all_to_all x1, starting transfers between devices, local(): lax.all_to_all(partial.reshape(groups * blocks, WIN, 128), ('tm', 'rows')...  6.26 us
    all_to_all x1, waiting for transfers between devices, local(): lax.all_to_all(partial.reshape(groups * blocks, WIN, 128), ('tm', 'rows')...  4.97 us
    pallas_call x1, Pallas kernels, section(): pl.pallas_call(functools.partial(section_kernel, cols, depth), in_specs=[...  4.81 us
    pallas_call x1, Pallas kernels, inner_rows(): pl.pallas_call(functools.partial(inner_kernel, cols), in_specs=[SCALAR] +...  4.68 us
    all_to_all x1, waiting for transfers between devices, local(): lax.all_to_all(feature_windows(features[0], groups), 'tm', 0, 0, tiled=True)  3.98 us
  transfers between devices with their start and end apart: 4, of which 2 were waited for; matrix products, arithmetic and copies ran while one was open for 0% of the time, Pallas kernels for 27%

profile of v6, /device:TPU:1, one launch (start us, length us, event | category | flops | bytes accessed | tf_op | source)
XLA Modules:
  0.0 55.4 jit_solution(13065141657817947094)
XLA Ops:
  0.0 1.7 %feature_windows.1 = bf16[8,4,16,384]{3,2,1,0:T(8,128)(2,1)} custom-call(bf16[4,104,384]{2,1,0:T(8,128)(2,1)} %bitcast.24), custom_call_target="tpu_custom_call" | custom-call | tf_op jit(solution)/shard_map/feature_windows/pallas_call | solution.py:350
  1.8 6.9 %all-to-all-start = ((bf16[8,4,16,384]{3,2,1,0:T(8,128)(2,1)}), bf16[8,4,16,384]{3,2,1,0:T(8,128)(2,1)S(1)}, u32[]{:S(2)}, u32[]{:S(2)}) async-start(bf16[8,4,16,384]{3,2,1,0:T(8,128)(2,1)} %feature_windows.1), calls=%async_computation | async-start | bytes 786432 | tf_op jit(solution)/shard_map/all_to_all | solution.py:486
  8.6 0.1 pad_add_fusion.position.place_in_mesh
  8.7 2.7 %cache_windows.1 = (bf16[2,4,16,384]{3,2,1,0:T(8,128)(2,1)S(1)}, bf16[2,4,16,384]{3,2,1,0:T(8,128)(2,1)S(1)}, bf16[1,3,3,384,384]{4,3,2,1,0:T(8,128)(2,1)S(1)}) custom-call(s32[2]{0:T(128)S(1)} %pad_add_fusion.position.place_in_mesh, bf16[2,4,104,384]{3,2,1,0:T(8,128)(2,1)} %conv_cache.1, bf16[2,4,104,384]{3,2,1,0:T(8,128)(2,1)} %head_cache.1, ...), custom_call_target="tpu_custom_call" | custom-call | tf_op jit(solution)/shard_map/cache_windows/pallas_call | solution.py:369
  11.5 4.0 %all-to-all-done.main = bf16[8,4,16,384]{3,2,1,0:T(8,128)(2,1)S(1)} async-done(((bf16[8,4,16,384]{3,2,1,0:T(8,128)(2,1)}), bf16[8,4,16,384]{3,2,1,0:T(8,128)(2,1)S(1)}, u32[]{:S(2)}, u32[]{:S(2)}) %all-to-all-start) | async-done | bytes 393248 | tf_op jit(solution)/shard_map/all_to_all | solution.py:486
  15.5 7.0 %collective-permute-start.1 = (bf16[10,16,384]{2,1,0:T(8,128)(2,1)S(1)}, bf16[10,16,384]{2,1,0:T(8,128)(2,1)S(1)}, u32[]{:S(2)}, u32[]{:S(2)}) collective-permute-start(bf16[10,16,384]{2,1,0:T(8,128)(2,1)S(1)} %pad_maximum_fusion.1), channel_id=1, source_target_pairs={{1,2},{3,4},{5,6},{7,8},{9,10},{11,12},{13,14},{2,1},{4,3},{6,5},{... | collective-permute-start | bytes 368648 | tf_op jit(solution)/shard_map/ppermute | solution.py:494
  22.6 0.1 collective-permute-start
  22.7 4.7 %inner_rows.1 = (bf16[2,3,3,384,384]{4,3,2,1,0:T(8,128)(2,1)S(1)}, bf16[640,384]{1,0:T(8,128)(2,1)S(1)}, bf16[10,4,16,384]{3,2,1,0:T(8,128)(2,1)S(1)}, bf16[8,2,16,384]{3,2,1,0:T(8,128)(2,1)S(1)}) custom-call(s32[2]{0:T(128)S(1)} %pad_add_fusion.position.place_in_mesh, bf16[8,4,16,384]{3,2,1,0:T(8,128)(2,1)S(1)} %all-to-all-done.main, ...), custom_call_target="tpu_custom_call" | custom-call | tf_op jit(solution)/shard_map/inner_rows/pallas_call | solution.py:387
  27.3 0.0 collective-permute-done.1.far
  27.4 0.0 collective-permute-done.near
  27.4 4.8 %section.1 = bf16[8,16,16,128]{3,2,1,0:T(8,128)(2,1)} custom-call(s32[2]{0:T(128)S(1)} %pad_add_fusion.position.place_in_mesh, bf16[8,4,16,384]{3,2,1,0:T(8,128)(2,1)S(1)} %all-to-all-done.main, bf16[10,16,384]{2,1,0:T(8,128)(2,1)S(1)} %collective-permute-done.near, bf16[10,16,384]{2,1,0:T(8,128)(2,1)S(1)} %collective-permute-done.1.far, ...), custom_call_target="tpu_custom_call" | custom-call | tf_op jit(solution)/shard_map/section/pallas_call | solution.py:409
  32.2 6.3 %all-to-all-start.1 = ((bf16[128,16,128]{2,1,0:T(8,128)(2,1)}), bf16[128,16,128]{2,1,0:T(8,128)(2,1)S(1)}, u32[]{:S(2)}, u32[]{:S(2)}) async-start(bf16[128,16,128]{2,1,0:T(8,128)(2,1)} %bitcast.22), calls=%async_computation.1 | async-start | bytes 1048576 | tf_op jit(solution)/shard_map/all_to_all | solution.py:500
  38.4 0.0 copy-start
  38.5 1.1 %copy-done = bf16[2,2,16,5120]{3,2,1,0:T(8,128)(2,1)S(1)} copy-done((bf16[2,2,16,5120]{3,2,1,0:T(8,128)(2,1)S(1)}, bf16[2,2,16,5120]{3,2,1,0:T(8,128)(2,1)}, u32[]{:S(2)}) %copy-start) | copy-done | bytes 655384
  39.5 7.5 %folded_weights.1 = (bf16[960,256]{1,0:T(8,128)(2,1)S(1)}, bf16[64,256]{1,0:T(8,128)(2,1)S(1)}) custom-call(bf16[2,2,16,5120]{3,2,1,0:T(8,128)(2,1)S(1)} %copy-done, bf16[960,5120]{1,0:T(8,128)(2,1)} %bitcast.21), custom_call_target="tpu_custom_call" | custom-call | tf_op jit(solution)/shard_map/folded_weights/pallas_call | solution.py:428
  47.1 5.0 %all-to-all-done.1 = bf16[128,16,128]{2,1,0:T(8,128)(2,1)S(1)} async-done(((bf16[128,16,128]{2,1,0:T(8,128)(2,1)}), bf16[128,16,128]{2,1,0:T(8,128)(2,1)S(1)}, u32[]{:S(2)}, u32[]{:S(2)}) %all-to-all-start.1) | async-done | bytes 524320 | tf_op jit(solution)/shard_map/all_to_all | solution.py:500
  52.0 3.2 %project.1 = bf16[960,1664]{1,0:T(8,128)(2,1)} custom-call(bf16[8,16,16,128]{3,2,1,0:T(8,128)(2,1)S(1)} %bitcast.20, bf16[960,256]{1,0:T(8,128)(2,1)S(1)} %get-tuple-element.21.folded, bf16[64,256]{1,0:T(8,128)(2,1)S(1)} %get-tuple-element.22.gram), custom_call_target="tpu_custom_call" | custom-call | tf_op jit(solution)/shard_map/project/pallas_call | solution.py:453
  (4 shorter events, 0.1 us)
Async XLA Ops:
  1.8 13.7 %all-to-all-start = ((bf16[8,4,16,384]{3,2,1,0:T(8,128)(2,1)}), bf16[8,4,16,384]{3,2,1,0:T(8,128)(2,1)S(1)}, u32[]{:S(2)}, u32[]{:S(2)}) async-start(bf16[8,4,16,384]{3,2,1,0:T(8,128)(2,1)} %feature_windows.1), calls=%async_computation | async-start | bytes 786432 | tf_op jit(solution)/shard_map/all_to_all | solution.py:486
  15.5 11.8 %collective-permute-start.1 = (bf16[10,16,384]{2,1,0:T(8,128)(2,1)S(1)}, bf16[10,16,384]{2,1,0:T(8,128)(2,1)S(1)}, u32[]{:S(2)}, u32[]{:S(2)}) collective-permute-start(bf16[10,16,384]{2,1,0:T(8,128)(2,1)S(1)} %pad_maximum_fusion.1), channel_id=1, source_target_pairs={{1,2},{3,4},{5,6},{7,8},{9,10},{11,12},{13,14},{2,1},{4,3},{6,5},{... | collective-permute-start | bytes 368648 | tf_op jit(solution)/shard_map/ppermute | solution.py:494
  22.6 4.8 %collective-permute-start = (bf16[10,16,384]{2,1,0:T(8,128)(2,1)S(1)}, bf16[10,16,384]{2,1,0:T(8,128)(2,1)S(1)}, u32[]{:S(2)}, u32[]{:S(2)}) collective-permute-start(bf16[10,16,384]{2,1,0:T(8,128)(2,1)S(1)} %pad_maximum_fusion), channel_id=1, source_target_pairs={{0,1},{2,3},{4,5},{6,7},{8,9},{10,11},{12,13},{14,15},{1,0},{3,2},... | collective-permute-start | bytes 368648 | tf_op jit(solution)/shard_map/ppermute | solution.py:495
  32.2 19.9 %all-to-all-start.1 = ((bf16[128,16,128]{2,1,0:T(8,128)(2,1)}), bf16[128,16,128]{2,1,0:T(8,128)(2,1)S(1)}, u32[]{:S(2)}, u32[]{:S(2)}) async-start(bf16[128,16,128]{2,1,0:T(8,128)(2,1)} %bitcast.22), calls=%async_computation.1 | async-start | bytes 1048576 | tf_op jit(solution)/shard_map/all_to_all | solution.py:500
  38.4 1.1 %copy-start = (bf16[2,2,16,5120]{3,2,1,0:T(8,128)(2,1)S(1)}, bf16[2,2,16,5120]{3,2,1,0:T(8,128)(2,1)}, u32[]{:S(2)}) copy-start(bf16[2,2,16,5120]{3,2,1,0:T(8,128)(2,1)} %patch.1) | copy-start | bytes 1966084

commit v7 on v6

--- a/solution.py
+++ b/solution.py
@@ -11,7 +11,8 @@
 BF16 = jnp.bfloat16
 EPS = 1e-06
 STEP = 14
-EARLY = 1
+EARLY = 3
+GROUP = 2
 WIN = 16
 
 
@@ -112,11 +113,7 @@
 
 def column_taps(weights):
     return jnp.concatenate(
-        [
-            jnp.concatenate([weight[b, c] for c in range(weight.shape[1])], axis=1)
-            for weight in weights
-            for b in range(weight.shape[0])
-        ],
+        [jnp.concatenate([weight[c] for c in range(weight.shape[0])], axis=1) for weight in weights],
         axis=0,
     )
 
@@ -139,47 +136,55 @@
 ):
     frames, rows, win, width = main.shape
     depth = head.shape[3]
-    taps = late.shape[0]
+    groups = late.shape[0] // GROUP
 
     def arriving(i):
-        return pltpu.make_async_copy(weight.at[EARLY + i], late.at[i], sems.at[i])
-
-    for i in range(taps):
+        return pltpu.make_async_copy(
+            weight.at[pl.ds(EARLY + GROUP * i, GROUP)], late.at[pl.ds(GROUP * i, GROUP)], sems.at[i]
+        )
+
+    head_copy = pltpu.make_async_copy(head, head_in, sems.at[groups])
+    for i in range(groups):
         arriving(i).start()
-    head_copy = pltpu.make_async_copy(head, head_in, sems.at[taps])
-    head_copy.start()
+        if i == 0:
+            head_copy.start()
     normed[0:2] = conv_win[...]
     normed[2:] = rms_silu(main[...].astype(F32)).astype(BF16)
     head_rows[...] = jnp.zeros_like(head_rows)
     count = frames * (rows - 2) * win
 
-    def product(a, weights):
+    def product(pairs, weights):
         left = jnp.concatenate(
             [
-                normed[pl.ds(a, frames), b : b + rows - 2].reshape(count, width)
-                for b in range(3)
+                normed[pl.ds(pair // 3, frames), pl.ds(pair % 3, rows - 2)].reshape(count, width)
+                for pair in pairs
             ],
             axis=1,
         )
-        return jnp.dot(left, column_taps([weights]), preferred_element_type=F32)
-
-    sums[...] = product(0, early[0])
+        return jnp.dot(left, column_taps(weights), preferred_element_type=F32)
+
+    sums[...] = product(range(EARLY), [early[i] for i in range(EARLY)])
 
     def step(i, carry):
         arriving(i).wait()
-        sums[...] += product(EARLY + i, late[i])
+        here = [GROUP * i + k for k in range(GROUP)]
+        sums[...] += product([EARLY + k for k in here], [late[k] for k in here])
+
+        @pl.when(i == 0)
+        def _():
+            head_copy.wait()
+            for a in range(3):
+                for b in range(3):
+                    for c in range(3):
+                        slot = 2 * a + c if c < 2 else 6 + a
+                        start = slot * 64 + (2 - b) * depth
+                        head_rows[start : start + depth] = head_in[a, b, c]
+
         return carry
 
-    lax.fori_loop(0, taps, step, 0)
+    lax.fori_loop(0, groups, step, 0)
     own = main[:, 1 : rows - 1].astype(F32).reshape(count, width)
     inner[...] = after_block(sums[...], own, place_in_mesh, cols).reshape(inner.shape)
-    head_copy.wait()
-    for a in range(3):
-        for b in range(3):
-            for c in range(3):
-                slot = 2 * a + c if c < 2 else 6 + a
-                start = slot * 64 + (2 - b) * depth
-                head_rows[start : start + depth] = head_in[a, b, c]
 
 
 def section_kernel(
@@ -239,11 +244,12 @@
     positions = 4 * depth
     chunks = sems.shape[0]
     share = qkv.shape[0] // chunks
-    copies = []
+    def arriving(index):
+        part = pl.ds(pl.multiple_of(index * share, 16), share)
+        return part, pltpu.make_async_copy(qkv.at[part], qkv_in.at[part], sems.at[index])
+
     for index in range(chunks):
-        part = pl.ds(index * share, share)
-        copies.append(pltpu.make_async_copy(qkv.at[part], qkv_in.at[part], sems.at[index]))
-        copies[-1].start()
+        arriving(index)[1].start()
 
     def stacked(values):
         pieces = list(three_parts(values))
@@ -266,15 +272,18 @@
             ]
     gram[...] = stacked(total / width)
 
-    for index in range(chunks):
-        copies[index].wait()
-        part = pl.ds(index * share, share)
+    def step(index, carry):
+        part, copy = arriving(index)
+        copy.wait()
         product = rows_times_rows(qkv_in[part], parts[...])
         folded[part] = stacked(
             product[:, :positions]
             + product[:, positions : 2 * positions]
             + product[:, 2 * positions :]
         )
+        return carry
+
+    lax.fori_loop(0, chunks, step, 0)
 
 
 def project_kernel(depth, pieces, folded, gram, out, sums, patches, columns, staged, sems):
@@ -397,7 +406,7 @@
         scratch_shapes=[
             pltpu.VMEM(head.shape, BF16),
             pltpu.VMEM((frames * (rows - 2) * win, 3 * width), F32),
-            pltpu.SemaphoreType.DMA((late[0] + 1,)),
+            pltpu.SemaphoreType.DMA((late[0] // GROUP + 1,)),
         ],
         compiler_params=params(20),
         name="inner_rows",
@@ -484,7 +493,8 @@
     flat_qkv = qkv_weight.transpose(1, 2, 0).reshape(3 * local_cols, qkv_weight.shape[0])
 
     main = lax.all_to_all(feature_windows(features[0], groups), "tm", 0, 0, tiled=True)
-    conv_win, head_win, early = cache_windows(place_in_mesh, conv_cache, head_cache, conv_weight)
+    pairs = conv_weight.reshape((9,) + conv_weight.shape[2:])
+    conv_win, head_win, early = cache_windows(place_in_mesh, conv_cache, head_cache, pairs)
     def edge(row):
         return jnp.concatenate(
             [lax.dynamic_index_in_dim(part, row, 1, False) for part in (conv_win, main)]
@@ -493,7 +503,7 @@
     odd = block % 2
     far = lax.ppermute(edge((rows - 1) * odd), "rows", swaps(blocks, 1))
     near = lax.ppermute(edge((rows - 1) * (1 - odd)), "rows", swaps(blocks, 0))
-    prepared = inner_rows(place_in_mesh, main, conv_win, early, conv_weight, head, cols)
+    prepared = inner_rows(place_in_mesh, main, conv_win, early, pairs, head, cols)
     partial = section(
         place_in_mesh, main, near, far, head_win, early, prepared, cols, depth, blocks
     )

time: 55.8 us -> 55.6 us (level)
  Pallas kernels: 24.7 us -> 22.6 us
  waiting for transfers between devices: 8.96 us -> 10.9 us
    all_to_all x1, waiting for transfers between devices: 4.97 us -> 6.93 us  [local(): lax.all_to_all(partial.reshape(groups * blocks, WIN, 128), ('tm', 'rows')...]
    pallas_call x1, Pallas kernels: 7.52 us -> 5.56 us  [folded_weights(): pl.pallas_call(folded_kernel, in_specs=[ON_CHIP, IN_HBM], out_specs=[ON_C...]
  transfers between devices with their start and end apart: 4 -> 4, of which waited for: 2 -> 2; matrix products, arithmetic and copies ran while one was open for 0% -> 0% of each run, Pallas kernels for 27% -> 23%
where the time goes in v7:
time: 55.6 us; the launch traced here: 55.3 us
  Pallas kernels  22.6 us (41%)
  starting transfers between devices  20.4 us (37%)
  waiting for transfers between devices  10.9 us (20%)
  local copies, waits for them, and re-layouts  1.12 us (2%)
    ppermute x1, starting transfers between devices, local(): far = lax.ppermute(edge((rows - 1) * odd), 'rows', swaps(blocks, 1))  7.03 us
    all_to_all x1, waiting for transfers between devices, local(): lax.all_to_all(partial.reshape(groups * blocks, WIN, 128), ('tm', 'rows')...  6.93 us
    all_to_all x1, starting transfers between devices, local(): lax.all_to_all(feature_windows(features[0], groups), 'tm', 0, 0, tiled=True)  6.89 us
    all_to_all x1, starting transfers between devices, local(): lax.all_to_all(partial.reshape(groups * blocks, WIN, 128), ('tm', 'rows')...  6.4 us
    pallas_call x1, Pallas kernels, folded_weights(): pl.pallas_call(folded_kernel, in_specs=[ON_CHIP, IN_HBM], out_specs=[ON_C...  5.56 us
    pallas_call x1, Pallas kernels, section(): pl.pallas_call(functools.partial(section_kernel, cols, depth), in_specs=[...  4.81 us
    pallas_call x1, Pallas kernels, inner_rows(): pl.pallas_call(functools.partial(inner_kernel, cols), in_specs=[SCALAR] +...  4.53 us
    all_to_all x1, waiting for transfers between devices, local(): lax.all_to_all(feature_windows(features[0], groups), 'tm', 0, 0, tiled=True)  3.98 us
  transfers between devices with their start and end apart: 4, of which 2 were waited for; matrix products, arithmetic and copies ran while one was open for 0% of the time, Pallas kernels for 23%

profile of v7, /device:TPU:1, one launch (start us, length us, event | category | flops | bytes accessed | tf_op | source)
XLA Modules:
  0.0 55.3 jit_solution(6373777285202602328)
XLA Ops:
  0.0 1.7 %feature_windows.1 = bf16[8,4,16,384]{3,2,1,0:T(8,128)(2,1)} custom-call(bf16[4,104,384]{2,1,0:T(8,128)(2,1)} %bitcast.27), custom_call_target="tpu_custom_call" | custom-call | tf_op jit(solution)/shard_map/feature_windows/pallas_call | solution.py:359
  1.8 6.9 %all-to-all-start = ((bf16[8,4,16,384]{3,2,1,0:T(8,128)(2,1)}), bf16[8,4,16,384]{3,2,1,0:T(8,128)(2,1)S(1)}, u32[]{:S(2)}, u32[]{:S(2)}) async-start(bf16[8,4,16,384]{3,2,1,0:T(8,128)(2,1)} %feature_windows.1), calls=%async_computation | async-start | bytes 786432 | tf_op jit(solution)/shard_map/all_to_all | solution.py:495
  8.6 0.1 pad_add_fusion.position.place_in_mesh
  8.7 2.7 %cache_windows.1 = (bf16[2,4,16,384]{3,2,1,0:T(8,128)(2,1)S(1)}, bf16[2,4,16,384]{3,2,1,0:T(8,128)(2,1)S(1)}, bf16[3,3,384,384]{3,2,1,0:T(8,128)(2,1)S(1)}) custom-call(s32[2]{0:T(128)S(1)} %pad_add_fusion.position.place_in_mesh, bf16[2,4,104,384]{3,2,1,0:T(8,128)(2,1)} %conv_cache.1, bf16[2,4,104,384]{3,2,1,0:T(8,128)(2,1)} %head_cache.1, ...), custom_call_target="tpu_custom_call" | custom-call | tf_op jit(solution)/shard_map/cache_windows/pallas_call | solution.py:378
  11.5 4.0 %all-to-all-done.main = bf16[8,4,16,384]{3,2,1,0:T(8,128)(2,1)S(1)} async-done(((bf16[8,4,16,384]{3,2,1,0:T(8,128)(2,1)}), bf16[8,4,16,384]{3,2,1,0:T(8,128)(2,1)S(1)}, u32[]{:S(2)}, u32[]{:S(2)}) %all-to-all-start) | async-done | bytes 393248 | tf_op jit(solution)/shard_map/all_to_all | solution.py:495
  15.5 7.0 %collective-permute-start.1 = (bf16[10,16,384]{2,1,0:T(8,128)(2,1)S(1)}, bf16[10,16,384]{2,1,0:T(8,128)(2,1)S(1)}, u32[]{:S(2)}, u32[]{:S(2)}) collective-permute-start(bf16[10,16,384]{2,1,0:T(8,128)(2,1)S(1)} %pad_maximum_fusion.1), channel_id=1, source_target_pairs={{1,2},{3,4},{5,6},{7,8},{9,10},{11,12},{13,14},{2,1},{4,3},{6,5},{... | collective-permute-start | bytes 368648 | tf_op jit(solution)/shard_map/ppermute | solution.py:504
  22.6 0.1 collective-permute-start
  22.7 4.5 %inner_rows.1 = (bf16[6,3,384,384]{3,2,1,0:T(8,128)(2,1)S(1)}, bf16[640,384]{1,0:T(8,128)(2,1)S(1)}, bf16[10,4,16,384]{3,2,1,0:T(8,128)(2,1)S(1)}, bf16[8,2,16,384]{3,2,1,0:T(8,128)(2,1)S(1)}) custom-call(s32[2]{0:T(128)S(1)} %pad_add_fusion.position.place_in_mesh, bf16[8,4,16,384]{3,2,1,0:T(8,128)(2,1)S(1)} %all-to-all-done.main, ...), custom_call_target="tpu_custom_call" | custom-call | tf_op jit(solution)/shard_map/inner_rows/pallas_call | solution.py:396
  27.2 0.0 collective-permute-done.1.far
  27.2 0.0 collective-permute-done.near
  27.2 4.8 %section.1 = bf16[8,16,16,128]{3,2,1,0:T(8,128)(2,1)} custom-call(s32[2]{0:T(128)S(1)} %pad_add_fusion.position.place_in_mesh, bf16[8,4,16,384]{3,2,1,0:T(8,128)(2,1)S(1)} %all-to-all-done.main, bf16[10,16,384]{2,1,0:T(8,128)(2,1)S(1)} %collective-permute-done.near, bf16[10,16,384]{2,1,0:T(8,128)(2,1)S(1)} %collective-permute-done.1.far, ...), custom_call_target="tpu_custom_call" | custom-call | tf_op jit(solution)/shard_map/section/pallas_call | solution.py:418
  32.0 6.4 %all-to-all-start.1 = ((bf16[128,16,128]{2,1,0:T(8,128)(2,1)}), bf16[128,16,128]{2,1,0:T(8,128)(2,1)S(1)}, u32[]{:S(2)}, u32[]{:S(2)}) async-start(bf16[128,16,128]{2,1,0:T(8,128)(2,1)} %bitcast.25), calls=%async_computation.1 | async-start | bytes 1048576 | tf_op jit(solution)/shard_map/all_to_all | solution.py:510
  38.4 0.0 copy-start
  38.5 1.1 %copy-done = bf16[2,2,16,5120]{3,2,1,0:T(8,128)(2,1)S(1)} copy-done((bf16[2,2,16,5120]{3,2,1,0:T(8,128)(2,1)S(1)}, bf16[2,2,16,5120]{3,2,1,0:T(8,128)(2,1)}, u32[]{:S(2)}) %copy-start) | copy-done | bytes 655384
  39.5 5.6 %folded_weights.1 = (bf16[960,256]{1,0:T(8,128)(2,1)S(1)}, bf16[64,256]{1,0:T(8,128)(2,1)S(1)}) custom-call(bf16[2,2,16,5120]{3,2,1,0:T(8,128)(2,1)S(1)} %copy-done, bf16[960,5120]{1,0:T(8,128)(2,1)} %bitcast.24), custom_call_target="tpu_custom_call" | custom-call | tf_op jit(solution)/shard_map/folded_weights/pallas_call | solution.py:437
  45.1 6.9 %all-to-all-done.1 = bf16[128,16,128]{2,1,0:T(8,128)(2,1)S(1)} async-done(((bf16[128,16,128]{2,1,0:T(8,128)(2,1)}), bf16[128,16,128]{2,1,0:T(8,128)(2,1)S(1)}, u32[]{:S(2)}, u32[]{:S(2)}) %all-to-all-start.1) | async-done | bytes 524320 | tf_op jit(solution)/shard_map/all_to_all | solution.py:510
  52.0 3.2 %project.1 = bf16[960,1664]{1,0:T(8,128)(2,1)} custom-call(bf16[8,16,16,128]{3,2,1,0:T(8,128)(2,1)S(1)} %bitcast.21, bf16[960,256]{1,0:T(8,128)(2,1)S(1)} %get-tuple-element.21.folded, bf16[64,256]{1,0:T(8,128)(2,1)S(1)} %get-tuple-element.22.gram), custom_call_target="tpu_custom_call" | custom-call | tf_op jit(solution)/shard_map/project/pallas_call | solution.py:462
  (4 shorter events, 0.1 us)
Async XLA Ops:
  1.8 13.7 %all-to-all-start = ((bf16[8,4,16,384]{3,2,1,0:T(8,128)(2,1)}), bf16[8,4,16,384]{3,2,1,0:T(8,128)(2,1)S(1)}, u32[]{:S(2)}, u32[]{:S(2)}) async-start(bf16[8,4,16,384]{3,2,1,0:T(8,128)(2,1)} %feature_windows.1), calls=%async_computation | async-start | bytes 786432 | tf_op jit(solution)/shard_map/all_to_all | solution.py:495
  15.5 11.7 %collective-permute-start.1 = (bf16[10,16,384]{2,1,0:T(8,128)(2,1)S(1)}, bf16[10,16,384]{2,1,0:T(8,128)(2,1)S(1)}, u32[]{:S(2)}, u32[]{:S(2)}) collective-permute-start(bf16[10,16,384]{2,1,0:T(8,128)(2,1)S(1)} %pad_maximum_fusion.1), channel_id=1, source_target_pairs={{1,2},{3,4},{5,6},{7,8},{9,10},{11,12},{13,14},{2,1},{4,3},{6,5},{... | collective-permute-start | bytes 368648 | tf_op jit(solution)/shard_map/ppermute | solution.py:504
  22.6 4.6 %collective-permute-start = (bf16[10,16,384]{2,1,0:T(8,128)(2,1)S(1)}, bf16[10,16,384]{2,1,0:T(8,128)(2,1)S(1)}, u32[]{:S(2)}, u32[]{:S(2)}) collective-permute-start(bf16[10,16,384]{2,1,0:T(8,128)(2,1)S(1)} %pad_maximum_fusion), channel_id=1, source_target_pairs={{0,1},{2,3},{4,5},{6,7},{8,9},{10,11},{12,13},{14,15},{1,0},{3,2},... | collective-permute-start | bytes 368648 | tf_op jit(solution)/shard_map/ppermute | solution.py:505
  32.0 20.0 %all-to-all-start.1 = ((bf16[128,16,128]{2,1,0:T(8,128)(2,1)}), bf16[128,16,128]{2,1,0:T(8,128)(2,1)S(1)}, u32[]{:S(2)}, u32[]{:S(2)}) async-start(bf16[128,16,128]{2,1,0:T(8,128)(2,1)} %bitcast.25), calls=%async_computation.1 | async-start | bytes 1048576 | tf_op jit(solution)/shard_map/all_to_all | solution.py:510
  38.4 1.1 %copy-start = (bf16[2,2,16,5120]{3,2,1,0:T(8,128)(2,1)S(1)}, bf16[2,2,16,5120]{3,2,1,0:T(8,128)(2,1)}, u32[]{:S(2)}) copy-start(bf16[2,2,16,5120]{3,2,1,0:T(8,128)(2,1)} %patch.1) | copy-start | bytes 1966084

commit v8 on v7

--- a/solution.py
+++ b/solution.py
@@ -188,7 +188,7 @@
 
 
 def section_kernel(
-    cols, depth, place_in_mesh, main, near, far, head_win, early, late, head_rows, normed, inner, out, edges, hidden, pieces, sems
+    cols, depth, place_in_mesh, main, near, far, head_win, early, late, head_rows, normed, inner, out, edges, pieces, sems
 ):
     frames, rows, win, width = main.shape
     count = frames * rows * win
@@ -197,8 +197,14 @@
         edges[edge, 0:2] = jnp.where(odd, when_odd[0:2], when_even[0:2])
         values = jnp.where(odd, when_odd[2:].astype(F32), when_even[2:].astype(F32))
         edges[edge, 2:] = rms_silu(values).astype(BF16)
-    hidden[0:2] = head_win[...]
-    hidden[2:, 1 : rows - 1] = inner[...]
+    lanes = head_rows.shape[0]
+
+    def head_taps(values):
+        product = rows_times_rows(values.reshape(-1, width), head_rows[...])
+        return product.reshape(values.shape[:3] + (lanes,))
+
+    cached_taps = head_taps(head_win[...])
+    inner_taps = head_taps(inner[...])
 
     def both(first, second):
         return jnp.concatenate([first[:, None], second[:, None]], axis=1).reshape(-1, width)
@@ -214,11 +220,11 @@
     sums = jnp.dot(left, column_taps(weights), preferred_element_type=F32)
     own = both(main[:, 0].astype(F32), main[:, rows - 1].astype(F32))
     outer = after_block(sums, own, place_in_mesh, cols).reshape(frames, 2, win, width)
-    hidden[2:, 0] = outer[:, 0]
-    hidden[2:, rows - 1] = outer[:, 1]
+    outer_taps = head_taps(outer)
 
     before = rows * win
-    taps = rows_times_rows(hidden[...].reshape(count + 2 * before, width), head_rows[...])
+    taps = jnp.concatenate([outer_taps[:, 0:1], inner_taps, outer_taps[:, 1:2]], axis=1)
+    taps = jnp.concatenate([cached_taps, taps], axis=0).reshape(count + 2 * before, lanes)
     pair = sum(taps[a * before : a * before + count, a * 128 : (a + 1) * 128] for a in range(3))
     last = taps[0:count, 384:512] + pltpu.roll(taps[before : before + count, 384:512], 64, 1)
     last += taps[2 * before : 2 * before + count, 512:576 + 64]
@@ -422,7 +428,6 @@
         out_shape=pltpu.HBM((frames, blocks, win, 128), BF16),
         scratch_shapes=[
             pltpu.VMEM((2, frames + 2, win, width), BF16),
-            pltpu.VMEM((frames + 2, rows, win, width), BF16),
             pltpu.VMEM((frames, blocks, win, 128), BF16),
             pltpu.SemaphoreType.DMA((frames,)),
         ],

time: 55.6 us -> 55.6 us (level)
  no operation moved by 1% of the time
where the time goes in v8:
time: 55.6 us; the launch traced here: 55.2 us
  Pallas kernels  22.6 us (41%)
  starting transfers between devices  20.4 us (37%)
  waiting for transfers between devices  10.9 us (20%)
  local copies, waits for them, and re-layouts  1.12 us (2%)
    ppermute x1, starting transfers between devices, local(): far = lax.ppermute(edge((rows - 1) * odd), 'rows', swaps(blocks, 1))  7.03 us
    all_to_all x1, waiting for transfers between devices, local(): lax.all_to_all(partial.reshape(groups * blocks, WIN, 128), ('tm', 'rows')...  6.93 us
    all_to_all x1, starting transfers between devices, local(): lax.all_to_all(feature_windows(features[0], groups), 'tm', 0, 0, tiled=True)  6.89 us
    all_to_all x1, starting transfers between devices, local(): lax.all_to_all(partial.reshape(groups * blocks, WIN, 128), ('tm', 'rows')...  6.39 us
    pallas_call x1, Pallas kernels, folded_weights(): pl.pallas_call(folded_kernel, in_specs=[ON_CHIP, IN_HBM], out_specs=[ON_C...  5.57 us
    pallas_call x1, Pallas kernels, section(): pl.pallas_call(functools.partial(section_kernel, cols, depth), in_specs=[...  4.78 us
    pallas_call x1, Pallas kernels, inner_rows(): pl.pallas_call(functools.partial(inner_kernel, cols), in_specs=[SCALAR] +...  4.53 us
    all_to_all x1, waiting for transfers between devices, local(): lax.all_to_all(feature_windows(features[0], groups), 'tm', 0, 0, tiled=True)  3.98 us
  transfers between devices with their start and end apart: 4, of which 2 were waited for; matrix products, arithmetic and copies ran while one was open for 0% of the time, Pallas kernels for 23%

profile of v8, /device:TPU:1, one launch (start us, length us, event | category | flops | bytes accessed | tf_op | source)
XLA Modules:
  0.0 55.2 jit_solution(3443996772820015261)
XLA Ops:
  0.0 1.7 %feature_windows.1 = bf16[8,4,16,384]{3,2,1,0:T(8,128)(2,1)} custom-call(bf16[4,104,384]{2,1,0:T(8,128)(2,1)} %bitcast.27), custom_call_target="tpu_custom_call" | custom-call | tf_op jit(solution)/shard_map/feature_windows/pallas_call | solution.py:365
  1.8 6.9 %all-to-all-start = ((bf16[8,4,16,384]{3,2,1,0:T(8,128)(2,1)}), bf16[8,4,16,384]{3,2,1,0:T(8,128)(2,1)S(1)}, u32[]{:S(2)}, u32[]{:S(2)}) async-start(bf16[8,4,16,384]{3,2,1,0:T(8,128)(2,1)} %feature_windows.1), calls=%async_computation | async-start | bytes 786432 | tf_op jit(solution)/shard_map/all_to_all | solution.py:500
  8.6 0.1 pad_add_fusion.position.place_in_mesh
  8.7 2.7 %cache_windows.1 = (bf16[2,4,16,384]{3,2,1,0:T(8,128)(2,1)S(1)}, bf16[2,4,16,384]{3,2,1,0:T(8,128)(2,1)S(1)}, bf16[3,3,384,384]{3,2,1,0:T(8,128)(2,1)S(1)}) custom-call(s32[2]{0:T(128)S(1)} %pad_add_fusion.position.place_in_mesh, bf16[2,4,104,384]{3,2,1,0:T(8,128)(2,1)} %conv_cache.1, bf16[2,4,104,384]{3,2,1,0:T(8,128)(2,1)} %head_cache.1, ...), custom_call_target="tpu_custom_call" | custom-call | tf_op jit(solution)/shard_map/cache_windows/pallas_call | solution.py:384
  11.5 4.0 %all-to-all-done.main = bf16[8,4,16,384]{3,2,1,0:T(8,128)(2,1)S(1)} async-done(((bf16[8,4,16,384]{3,2,1,0:T(8,128)(2,1)}), bf16[8,4,16,384]{3,2,1,0:T(8,128)(2,1)S(1)}, u32[]{:S(2)}, u32[]{:S(2)}) %all-to-all-start) | async-done | bytes 393248 | tf_op jit(solution)/shard_map/all_to_all | solution.py:500
  15.5 7.0 %collective-permute-start.1 = (bf16[10,16,384]{2,1,0:T(8,128)(2,1)S(1)}, bf16[10,16,384]{2,1,0:T(8,128)(2,1)S(1)}, u32[]{:S(2)}, u32[]{:S(2)}) collective-permute-start(bf16[10,16,384]{2,1,0:T(8,128)(2,1)S(1)} %pad_maximum_fusion.1), channel_id=1, source_target_pairs={{1,2},{3,4},{5,6},{7,8},{9,10},{11,12},{13,14},{2,1},{4,3},{6,5},{... | collective-permute-start | bytes 368648 | tf_op jit(solution)/shard_map/ppermute | solution.py:509
  22.6 0.1 collective-permute-start
  22.7 4.5 %inner_rows.1 = (bf16[6,3,384,384]{3,2,1,0:T(8,128)(2,1)S(1)}, bf16[640,384]{1,0:T(8,128)(2,1)S(1)}, bf16[10,4,16,384]{3,2,1,0:T(8,128)(2,1)S(1)}, bf16[8,2,16,384]{3,2,1,0:T(8,128)(2,1)S(1)}) custom-call(s32[2]{0:T(128)S(1)} %pad_add_fusion.position.place_in_mesh, bf16[8,4,16,384]{3,2,1,0:T(8,128)(2,1)S(1)} %all-to-all-done.main, ...), custom_call_target="tpu_custom_call" | custom-call | tf_op jit(solution)/shard_map/inner_rows/pallas_call | solution.py:402
  27.2 0.0 collective-permute-done.1.far
  27.2 0.0 collective-permute-done.near
  27.2 4.8 %section.1 = bf16[8,16,16,128]{3,2,1,0:T(8,128)(2,1)} custom-call(s32[2]{0:T(128)S(1)} %pad_add_fusion.position.place_in_mesh, bf16[8,4,16,384]{3,2,1,0:T(8,128)(2,1)S(1)} %all-to-all-done.main, bf16[10,16,384]{2,1,0:T(8,128)(2,1)S(1)} %collective-permute-done.near, bf16[10,16,384]{2,1,0:T(8,128)(2,1)S(1)} %collective-permute-done.1.far, ...), custom_call_target="tpu_custom_call" | custom-call | tf_op jit(solution)/shard_map/section/pallas_call | solution.py:424
  32.0 6.4 %all-to-all-start.1 = ((bf16[128,16,128]{2,1,0:T(8,128)(2,1)}), bf16[128,16,128]{2,1,0:T(8,128)(2,1)S(1)}, u32[]{:S(2)}, u32[]{:S(2)}) async-start(bf16[128,16,128]{2,1,0:T(8,128)(2,1)} %bitcast.25), calls=%async_computation.1 | async-start | bytes 1048576 | tf_op jit(solution)/shard_map/all_to_all | solution.py:515
  38.4 0.0 copy-start
  38.4 1.1 %copy-done = bf16[2,2,16,5120]{3,2,1,0:T(8,128)(2,1)S(1)} copy-done((bf16[2,2,16,5120]{3,2,1,0:T(8,128)(2,1)S(1)}, bf16[2,2,16,5120]{3,2,1,0:T(8,128)(2,1)}, u32[]{:S(2)}) %copy-start) | copy-done | bytes 655384
  39.5 5.6 %folded_weights.1 = (bf16[960,256]{1,0:T(8,128)(2,1)S(1)}, bf16[64,256]{1,0:T(8,128)(2,1)S(1)}) custom-call(bf16[2,2,16,5120]{3,2,1,0:T(8,128)(2,1)S(1)} %copy-done, bf16[960,5120]{1,0:T(8,128)(2,1)} %bitcast.24), custom_call_target="tpu_custom_call" | custom-call | tf_op jit(solution)/shard_map/folded_weights/pallas_call | solution.py:442
  45.1 6.9 %all-to-all-done.1 = bf16[128,16,128]{2,1,0:T(8,128)(2,1)S(1)} async-done(((bf16[128,16,128]{2,1,0:T(8,128)(2,1)}), bf16[128,16,128]{2,1,0:T(8,128)(2,1)S(1)}, u32[]{:S(2)}, u32[]{:S(2)}) %all-to-all-start.1) | async-done | bytes 524320 | tf_op jit(solution)/shard_map/all_to_all | solution.py:515
  52.0 3.2 %project.1 = bf16[960,1664]{1,0:T(8,128)(2,1)} custom-call(bf16[8,16,16,128]{3,2,1,0:T(8,128)(2,1)S(1)} %bitcast.21, bf16[960,256]{1,0:T(8,128)(2,1)S(1)} %get-tuple-element.21.folded, bf16[64,256]{1,0:T(8,128)(2,1)S(1)} %get-tuple-element.22.gram), custom_call_target="tpu_custom_call" | custom-call | tf_op jit(solution)/shard_map/project/pallas_call | solution.py:467
  (4 shorter events, 0.1 us)
Async XLA Ops:
  1.8 13.7 %all-to-all-start = ((bf16[8,4,16,384]{3,2,1,0:T(8,128)(2,1)}), bf16[8,4,16,384]{3,2,1,0:T(8,128)(2,1)S(1)}, u32[]{:S(2)}, u32[]{:S(2)}) async-start(bf16[8,4,16,384]{3,2,1,0:T(8,128)(2,1)} %feature_windows.1), calls=%async_computation | async-start | bytes 786432 | tf_op jit(solution)/shard_map/all_to_all | solution.py:500
  15.5 11.7 %collective-permute-start.1 = (bf16[10,16,384]{2,1,0:T(8,128)(2,1)S(1)}, bf16[10,16,384]{2,1,0:T(8,128)(2,1)S(1)}, u32[]{:S(2)}, u32[]{:S(2)}) collective-permute-start(bf16[10,16,384]{2,1,0:T(8,128)(2,1)S(1)} %pad_maximum_fusion.1), channel_id=1, source_target_pairs={{1,2},{3,4},{5,6},{7,8},{9,10},{11,12},{13,14},{2,1},{4,3},{6,5},{... | collective-permute-start | bytes 368648 | tf_op jit(solution)/shard_map/ppermute | solution.py:509
  22.6 4.6 %collective-permute-start = (bf16[10,16,384]{2,1,0:T(8,128)(2,1)S(1)}, bf16[10,16,384]{2,1,0:T(8,128)(2,1)S(1)}, u32[]{:S(2)}, u32[]{:S(2)}) collective-permute-start(bf16[10,16,384]{2,1,0:T(8,128)(2,1)S(1)} %pad_maximum_fusion), channel_id=1, source_target_pairs={{0,1},{2,3},{4,5},{6,7},{8,9},{10,11},{12,13},{14,15},{1,0},{3,2},... | collective-permute-start | bytes 368648 | tf_op jit(solution)/shard_map/ppermute | solution.py:510
  32.0 20.0 %all-to-all-start.1 = ((bf16[128,16,128]{2,1,0:T(8,128)(2,1)}), bf16[128,16,128]{2,1,0:T(8,128)(2,1)S(1)}, u32[]{:S(2)}, u32[]{:S(2)}) async-start(bf16[128,16,128]{2,1,0:T(8,128)(2,1)} %bitcast.25), calls=%async_computation.1 | async-start | bytes 1048576 | tf_op jit(solution)/shard_map/all_to_all | solution.py:515
  38.4 1.1 %copy-start = (bf16[2,2,16,5120]{3,2,1,0:T(8,128)(2,1)S(1)}, bf16[2,2,16,5120]{3,2,1,0:T(8,128)(2,1)}, u32[]{:S(2)}) copy-start(bf16[2,2,16,5120]{3,2,1,0:T(8,128)(2,1)} %patch.1) | copy-start | bytes 1966084
